TPU v7x, 512 devices: a whole 4x8x8 slice. The times are simulated.
512 devices in a mesh: rows: 64 (over y, x, core), vars: 8 (over z).
Axes of the slice: x: 4, y: 8, z: 8, core: 2. Of those that a mesh axis runs over, the one named last changes fastest.
Arguments:
- fields: bfloat16 [64, 262144], P('vars', 'rows'), may hold values from -6 to 6
- stencil: int32 [131072, 4], P('rows'), may hold values from 0 to 1023
- stencil_weight: float32 [131072, 4], P('rows'), may hold values from 0.1 to 1
- owner_map: int32 [8192, 1], P('rows'), may hold values from 0 to 63; in each aligned block of 128 rows (0 to 127, 128 to 255, ...) at most 4 rows name the same one
- embed_weight: bfloat16 [64, 16, 1024], P('vars'), may hold values from -1.5 to 1.5
- embed_bias: bfloat16 [64, 1024], P('vars'), may hold values from -3 to 3
- agg_query: float32 [16, 64], replicated, may hold values from -40 to 40
- out_grad: bfloat16 [16384, 1024], P('rows'), may hold values from -6 to 6
Outputs:
- tokens: bfloat16 [16384, 1024], P('rows', 'vars')
- field_grad: float32 [64, 262144], P('vars', 'rows')
- weight_grad: float32 [64, 16, 1024], P('vars')
- bias_grad: float32 [64, 1024], P('vars')
- query_grad: float32 [16, 64], replicated
Inputs may be any that keep to these rules, and one draw needn't show every extreme that they name: `stencil`: the index of a point within the pixel's own block. `owner_map`: among the 128 patches of one device along rows, no owner is named more than 4 times, a bound that some block reaches.
All inputs are finite; a program needn't handle non-finite values.
Results may differ from a plain program's by a relative error of at most 0.0055.
The roundings to bfloat16 on the way count: a program that leaves them out, or rounds other values in their place, can miss the bound.
Values may be sent and summed in bfloat16 or wider, within the bound.
No kernel may reach another device: no remote copies, remote signals or barrier semaphores. Data moves between devices by JAX's collectives and lax.ppermute only.
A program may use at most 128 MiB of HBM per device.

v0:
```python
import math

import jax
import jax.numpy as jnp
from jax import lax
from jax.sharding import PartitionSpec as P

D = 1024
H = 16
DH = 64
P_SIZE = 16
K = 4
PTS_BLK = 1024
PB = 32


def combined_all(value, axis, join):
    pieces = jax.tree.map(lambda part: lax.all_gather(part, axis), value)
    head = jax.tree.map(lambda part: part[0], pieces)
    tail = jax.tree.map(lambda part: part[1:], pieces)
    so_far, _ = lax.scan(lambda so_far, piece: (join(so_far, piece), None), head, tail)
    return so_far


def interp_matrix(index_rows, weight_rows):
    columns = jnp.arange(PTS_BLK, dtype=jnp.int32)
    summed = jnp.zeros((index_rows.shape[0], PTS_BLK), jnp.float32)
    for entry in range(K):
        summed = summed + jnp.where(
            index_rows[:, entry : entry + 1] == columns[None, :],
            weight_rows[:, entry : entry + 1],
            0.0,
        )
    return summed.astype(jnp.bfloat16)


def local(
    fields, stencil, stencil_weight, owner_map, embed_weight, embed_bias, agg_query, out_grad
):
    high = lax.Precision.HIGHEST
    row_devices = lax.axis_size("rows")
    var_devices = lax.axis_size("vars")
    var_local = fields.shape[0]
    point_count = fields.shape[1]
    blocks = point_count // PTS_BLK
    patch_count = owner_map.shape[0]
    capacity = out_grad.shape[0]
    slot_depth = capacity // row_devices
    block_pixels = PB * P_SIZE
    score_scale = 1.0 / math.sqrt(DH)
    field_blocks = fields.reshape(var_local, blocks, PTS_BLK).transpose(1, 0, 2)
    index_blocks = stencil.reshape(blocks, block_pixels, K)
    weight_blocks = stencil_weight.reshape(blocks, block_pixels, K)

    def forward_block(pieces):
        field_block, index_rows, weight_rows = pieces
        matrix = interp_matrix(index_rows, weight_rows)
        return jnp.dot(field_block, matrix.T, preferred_element_type=jnp.float32).astype(
            jnp.bfloat16
        )

    pixels = lax.map(forward_block, (field_blocks, index_blocks, weight_blocks))
    pixels = (
        pixels.reshape(blocks, var_local, PB, P_SIZE)
        .transpose(0, 2, 1, 3)
        .reshape(patch_count, var_local * P_SIZE)
    )
    routes = owner_map[:, 0]
    onehot = (routes[:, None] == jnp.arange(row_devices, dtype=jnp.int32)[None, :]).astype(
        jnp.int32
    )
    order_rank = jnp.sum(onehot * (jnp.cumsum(onehot, axis=0) - 1), axis=1)
    target = routes * slot_depth + order_rank
    outbox = jnp.zeros((capacity, var_local * P_SIZE), jnp.bfloat16).at[target].set(pixels)
    markers = (
        jnp.zeros((capacity,), jnp.bfloat16).at[target].set(jnp.ones((patch_count,), jnp.bfloat16))
    )
    inbox, filled = (
        lax.all_to_all(
            outbox.reshape(row_devices, slot_depth, var_local * P_SIZE),
            "rows",
            split_axis=0,
            concat_axis=0,
            tiled=True,
        ),
        lax.all_to_all(
            markers.reshape(row_devices, slot_depth),
            "rows",
            split_axis=0,
            concat_axis=0,
            tiled=True,
        ),
    )
    filled = filled.reshape(capacity).astype(jnp.float32)
    row_block = min(256, capacity)
    block_count = capacity // row_block
    pix_split = inbox.reshape(block_count, row_block, var_local, P_SIZE)
    bias_f = embed_bias.astype(jnp.float32)

    def embed_rows(pix_rows):
        projected = jnp.einsum(
            "svp,vpd->svd", pix_rows, embed_weight, preferred_element_type=jnp.float32
        )
        return (projected + bias_f[None]).astype(jnp.bfloat16)

    def head_scores(embedded):
        head_view = embedded.astype(jnp.float32).reshape(row_block, var_local, H, DH)
        return (
            head_view,
            jnp.einsum("svhe,he->shv", head_view, agg_query, precision=high) * score_scale,
        )

    def forward_rows(pix_rows):
        embedded = embed_rows(pix_rows)
        head_view, scores = head_scores(embedded)
        peak = jnp.max(scores, axis=2)
        weights_exp = jnp.exp(scores - peak[:, :, None])
        weighted = jnp.einsum("shv,svhe->she", weights_exp, head_view, precision=high)
        return (embedded, peak, jnp.sum(weights_exp, axis=2), weighted)

    embeds, peaks, totals, weighted_sums = lax.map(forward_rows, pix_split)
    peaks = peaks.reshape(capacity, H)
    totals = totals.reshape(capacity, H)
    weighted_sums = weighted_sums.reshape(capacity, H, DH)
    upstream = out_grad.astype(jnp.float32).reshape(capacity, H, DH) * filled[:, None, None]
    heads_local = H // var_devices
    first_head = lax.axis_index("vars") * heads_local

    def combine(first, second):
        peak_both = jnp.maximum(first[0], second[0])
        left_factor = jnp.exp(first[0] - peak_both)
        right_factor = jnp.exp(second[0] - peak_both)
        return (
            peak_both,
            first[1] * left_factor + second[1] * right_factor,
            first[2] * left_factor[:, :, None] + second[2] * right_factor[:, :, None],
        )

    peak_all, summed, weighted_all = combined_all((peaks, totals, weighted_sums), "vars", combine)
    mixture = weighted_all / summed[:, :, None]
    inner_out = jnp.sum(upstream * mixture, axis=2)
    own_heads = lax.dynamic_slice_in_dim(mixture, first_head, heads_local, 1)
    tokens = (
        (own_heads * filled[:, None, None]).reshape(capacity, heads_local * DH).astype(jnp.bfloat16)
    )

    def backward_rows(running, pieces):
        weight_acc, bias_acc, query_acc = running
        stored_rows, pix_rows, peak_rows, total_rows, inner_rows, grad_rows = pieces
        embedded = embed_rows(stored_rows)
        head_view, scores = head_scores(embedded)
        attention = jnp.exp(scores - peak_rows[:, :, None]) / total_rows[:, :, None]
        grad_attn = jnp.einsum("she,svhe->shv", grad_rows, head_view, precision=high)
        grad_score = attention * (grad_attn - inner_rows[:, :, None])
        grad_embed = (
            jnp.einsum("shv,she->svhe", attention, grad_rows, precision=high)
            + jnp.einsum("shv,he->svhe", grad_score, agg_query, precision=high) * score_scale
        )
        grad_embed = grad_embed.reshape(row_block, var_local, D)
        grad_low = grad_embed.astype(jnp.bfloat16)
        weight_acc = weight_acc + jnp.einsum(
            "svp,svd->vpd", pix_rows, grad_low, preferred_element_type=jnp.float32
        )
        bias_acc = bias_acc + jnp.sum(grad_embed, axis=0)
        query_acc = (
            query_acc
            + jnp.einsum("shv,svhe->he", grad_score, head_view, precision=high) * score_scale
        )
        grad_pixels = jnp.einsum(
            "svd,vpd->svp", grad_low, embed_weight, preferred_element_type=jnp.float32
        ).astype(jnp.bfloat16)
        return ((weight_acc, bias_acc, query_acc), grad_pixels)

    start_sums = (
        jnp.zeros((var_local, P_SIZE, D), jnp.float32),
        jnp.zeros((var_local, D), jnp.float32),
        jnp.zeros((H, DH), jnp.float32),
    )
    scan_inputs = (
        pix_split,
        pix_split,
        peak_all.reshape(block_count, row_block, H),
        summed.reshape(block_count, row_block, H),
        inner_out.reshape(block_count, row_block, H),
        upstream.reshape(block_count, row_block, H, DH),
    )
    sums_final, grad_pixels = lax.scan(backward_rows, start_sums, scan_inputs)
    weight_acc, bias_acc, query_acc = sums_final
    returned = lax.all_to_all(
        grad_pixels.reshape(row_devices, slot_depth, var_local * P_SIZE),
        "rows",
        split_axis=0,
        concat_axis=0,
        tiled=True,
    )
    grad_patches = returned.reshape(capacity, var_local * P_SIZE)[target]
    grad_blocks = (
        grad_patches.reshape(blocks, PB, var_local, P_SIZE)
        .transpose(0, 2, 1, 3)
        .reshape(blocks, var_local, block_pixels)
    )

    def backward_block(pieces):
        grad_block, index_rows, weight_rows = pieces
        matrix = interp_matrix(index_rows, weight_rows)
        return jnp.dot(grad_block, matrix, preferred_element_type=jnp.float32)

    field_grad = (
        lax.map(backward_block, (grad_blocks, index_blocks, weight_blocks))
        .transpose(1, 0, 2)
        .reshape(var_local, point_count)
    )
    weight_grad, bias_grad = lax.psum((weight_acc, bias_acc), "rows")
    query_grad = lax.psum(query_acc, ("rows", "vars"))
    return (tokens, field_grad, weight_grad, bias_grad, query_grad)


def solution(mesh):
    return jax.shard_map(
        local,
        mesh=mesh,
        in_specs=(
            P("vars", "rows"),
            P("rows", None),
            P("rows", None),
            P("rows", None),
            P("vars", None, None),
            P("vars", None),
            P(),
            P("rows", None),
        ),
        out_specs=(
            P("rows", "vars"),
            P("vars", "rows"),
            P("vars", None, None),
            P("vars", None),
            P(),
        ),
        check_vma=False,
    )
```

profile of v0, /device:TPU:1, one launch (start us, length us, event | category | flops | bytes accessed | tf_op | source)
XLA Modules:
  0.0 614.8 jit_solution(1491750393747009394)
XLA Ops:
  9.6 14.3 %while.7 = (s32[]{:T(128)}, bf16[4,8,512]{2,1,0:T(8,128)(2,1)S(1)}, bf16[4,8,1024]{2,1,0:T(8,128)(2,1)}, s32[4,512,4]{1,2,0:T(4,128)}, f32[4,512,4]{1,2,0:T(4,128)}, /*index=5*/s32[]{:T(128)}) while((s32[]{:T(128)}, bf16[4,8,512]{2,1,0:T(8,128)(2,1)S(1)}, bf16[4,8,1024]{2,1,0:T(8,128)(2,1)}, s32[4,512,4]{1,2,0:T(4,128)}, ...), condition=%wide.region_3.4_spmd, body=%wide.region_2.3_spmd.sunk | while | flops 14684162 | bytes 107605 | solution.py:62
  11.1 2.1 fusion.80
  14.7 2.1 fusion.80
  18.2 2.1 fusion.80
  21.8 2.1 fusion.80
  24.6 1.5 scatter_custom_fusion
  26.1 11.6 %all-to-all-start = ((bf16[64,4,128]{2,1,0:T(4,128)(2,1)}), bf16[64,4,128]{2,1,0:T(4,128)(2,1)S(1)}, u32[]{:S(2)}, u32[]{:S(2)}) async-start(bf16[64,4,128]{2,1,0:T(4,128)(2,1)} %bitcast.37), calls=%async_computation | async-start | bytes 131072 | tf_op jit(solution)/shard_map/all_to_all | solution.py:79
  37.8 10.0 %all-to-all-done = bf16[64,4,128]{2,1,0:T(4,128)(2,1)S(1)} async-done(((bf16[64,4,128]{2,1,0:T(4,128)(2,1)}), bf16[64,4,128]{2,1,0:T(4,128)(2,1)S(1)}, u32[]{:S(2)}, u32[]{:S(2)}) %all-to-all-start) | async-done | bytes 65568 | tf_op jit(solution)/shard_map/all_to_all | solution.py:79
  48.5 3.2 fusion.33
  51.7 6.5 %copy.63 = bf16[256,8,1024]{0,2,1:T(8,128)(2,1)} copy(bf16[256,8,1024]{2,0,1:T(8,128)(2,1)} %fusion.33) | data formatting | bytes 8388608 | tf_op jit(solution)/shard_map/while/body/eval_jaxpr/convert_element_type | solution.py:104
  58.2 4.1 fusion.36
  62.4 2.2 multiply_reduce_fusion.1
  64.7 1.3 scatter_custom_fusion.1
  66.8 4.4 all-to-all-start.1
  72.8 7.8 %all-to-all-done.1 = bf16[64,1,4]{2,1,0:T(2,128)(2,1)S(1)} async-done(((bf16[64,1,4]{2,1,0:T(2,128)(2,1)}), bf16[64,1,4]{2,1,0:T(2,128)(2,1)S(1)}, u32[]{:S(2)}, u32[]{:S(2)}) %all-to-all-start.1) | async-done | bytes 544 | tf_op jit(solution)/shard_map/all_to_all | solution.py:86
  81.4 28.5 %all-gather = f32[2048,16]{0,1:T(8,128)S(1)} all-gather(f32[256,16]{0,1:T(8,128)S(1)} %bitcast_reduce_fusion), channel_id=2, replica_groups=mesh['rows'=64,'vars'=8] {'vars'}, dimensions={0}, use_global_device_ids=true | all-gather | bytes 147456 | tf_op jit(solution)/shard_map/all_gather | solution.py:18
  110.6 22.5 %all-gather.1 = f32[2048,16]{0,1:T(8,128)S(1)} all-gather(f32[256,16]{0,1:T(8,128)S(1)} %get-tuple-element.244), channel_id=3, replica_groups=mesh['rows'=64,'vars'=8] {'vars'}, dimensions={0}, use_global_device_ids=true | all-gather | bytes 147456 | tf_op jit(solution)/shard_map/all_gather | solution.py:18
  134.4 27.7 %all-gather.5.cloned.1.call-done = f32[2048,16,64]{0,2,1:T(8,128)} async-done(((f32[256,16,64]{0,2,1:T(8,128)}), f32[2048,16,64]{0,2,1:T(8,128)}) %all-gather.5.cloned.1.call-update) | async-done | bytes 8388624 | tf_op jit(solution)/shard_map/all_gather | solution.py:18
  162.1 1.2 slice-done
  163.3 1.3 copy.64
  164.6 6.7 %slice.101 = f32[1792,16,64]{0,2,1:T(8,128)} slice(f32[2048,16,64]{0,2,1:T(8,128)} %all-gather.5.cloned.1.call-done), slice={[256:2048], [0:16], [0:64]} | slice | bytes 14680064 | tf_op jit(solution)/shard_map/slice | solution.py:20
  171.4 13.2 %copy.97 = f32[1792,16,64]{2,1,0:T(8,128)} copy(f32[1792,16,64]{0,2,1:T(8,128)} %slice.101) | data formatting | bytes 14680064 | tf_op jit(solution)/shard_map/while | solution.py:21
  184.6 35.6 %while.8 = (s32[]{:T(128)}, f32[256,16]{0,1:T(8,128)S(1)}, f32[256,16]{0,1:T(8,128)S(1)}, f32[256,16,64]{2,1,0:T(8,128)S(1)}, f32[7,256,16]{1,0,2:T(8,128)}, /*i...) while((s32[]{:T(128)}, f32[256,16]{0,1:T(8,128)S(1)}, f32[256,16]{0,1:T(8,128)S(1)}, ...), condition=%wide.region_8.9_spmd, body=%wide.region_7.8_spmd.sunk | while | flops 811010 | bytes 3440741 | solution.py:21
  185.8 3.8 fusion.82
  189.6 1.0 constant_dynamic-slice_fusion.3
  190.9 3.8 fusion.82
  196.0 3.8 fusion.82
  199.8 1.0 constant_dynamic-slice_fusion.3
  201.1 3.8 fusion.82
  206.2 3.8 fusion.82
  210.0 1.0 constant_dynamic-slice_fusion.3
  211.3 3.8 fusion.82
  216.3 3.8 fusion.82
  220.8 1.0 copy.68
  221.8 1.3 multiply_reduce_fusion.2
  223.2 3.7 multiply_reduce_fusion
  227.0 2.1 fusion.31
  229.9 2.0 fusion.59
  233.9 10.5 %all-to-all-start.2 = ((bf16[64,4,128]{2,1,0:T(4,128)(2,1)}), bf16[64,4,128]{2,1,0:T(4,128)(2,1)S(1)}, u32[]{:S(2)}, u32[]{:S(2)}) async-start(bf16[64,4,128]{2,1,0:T(4,128)(2,1)} %reshape.110), calls=%async_computation.2 | async-start | bytes 131072 | tf_op jit(solution)/shard_map/all_to_all | solution.py:189
  245.2 5.1 fusion.34
  250.4 98.8 %psum.23 = f32[16,64]{1,0:T(8,128)} all-reduce(f32[16,64]{1,0:T(8,128)S(1)} %broadcast_multiply_fusion), channel_id=1, replica_groups=mesh['rows'=64,'vars'=8] {'rows','vars'}, use_global_device_ids=true, to_apply=%region_16.17 | all-reduce | flops 1024 | bytes 8192 | tf_op jit(solution)/shard_map/psum | solution.py:214
  349.2 242.3 %psum.22 = f32[8,1024]{1,0:T(8,128)} all-reduce(f32[8,1024]{1,0:T(8,128)S(1)} %reduce_sum.47), channel_id=1, replica_groups=mesh['rows'=64,'vars'=8] {'rows'}, use_global_device_ids=true, to_apply=%region_15.16 | all-reduce | flops 8192 | bytes 65536 | tf_op jit(solution)/shard_map/psum | solution.py:213
  593.0 13.0 %while.9 = (s32[]{:T(128)}, f32[4,8,1024]{2,1,0:T(8,128)}, bf16[4,8,512]{2,1,0:T(8,128)(2,1)S(1)}, s32[4,512,4]{1,2,0:T(4,128)}, f32[4,512,4]{1,2,0:T(4,128)}, /*index=5*/s32[]{:T(128)}) while((s32[]{:T(128)}, f32[4,8,1024]{2,1,0:T(8,128)}, bf16[4,8,512]{2,1,0:T(8,128)(2,1)S(1)}, s32[4,512,4]{1,2,0:T(4,128)}, f32[4,512,4]{1,2,0:T(4,128)}, ...), condition=%wide.region_12.13_spmd, body=%wide.region_11.12_spmd.sunk | while | flops 14680066 | bytes 123989 | solution.py:209
  594.5 1.8 fusion.86
  597.7 1.8 fusion.86
  601.0 1.8 fusion.86
  604.2 1.8 fusion.86
  606.1 1.9 copy.165
  (130 shorter events, 32.0 us)
Async XLA Ops:
  7.2 41.3 %copy-start = (bf16[8,16,1024]{2,1,0:T(8,128)(2,1)S(1)}, bf16[8,16,1024]{2,1,0:T(8,128)(2,1)}, u32[]{:S(2)}) copy-start(bf16[8,16,1024]{2,1,0:T(8,128)(2,1)} %param.18) | copy-start | bytes 786436
  9.6 28.1 %copy-start.8 = (bf16[8,1024]{1,0:T(8,128)(2,1)S(1)}, bf16[8,1024]{1,0:T(8,128)(2,1)}, u32[]{:S(2)}) copy-start(bf16[8,1024]{1,0:T(8,128)(2,1)} %param.19) | copy-start | bytes 49156
  26.1 21.7 %all-to-all-start = ((bf16[64,4,128]{2,1,0:T(4,128)(2,1)}), bf16[64,4,128]{2,1,0:T(4,128)(2,1)S(1)}, u32[]{:S(2)}, u32[]{:S(2)}) async-start(bf16[64,4,128]{2,1,0:T(4,128)(2,1)} %bitcast.37), calls=%async_computation | async-start | bytes 131072 | tf_op jit(solution)/shard_map/all_to_all | solution.py:79
  37.7 124.4 %all-gather.5.cloned.1.call-start = ((), (), s32[]{:S(2)}) async-start(), calls=%async_computation.4 | async-start | bytes 9437184 | tf_op jit(solution)/shard_map/all_gather | solution.py:18
  48.5 3.2 copy-start.5
  51.7 6.5 %copy-start.10 = (f32[16,64]{1,0:T(8,128)S(1)}, f32[16,64]{1,0:T(8,128)}, u32[]{:S(2)}) copy-start(f32[16,64]{1,0:T(8,128)} %param.20) | copy-start | bytes 12292
  58.2 4.2 copy-start.1
  62.4 9.4 %copy-start.7 = (bf16[256,1024]{1,0:T(8,128)(2,1)S(1)}, bf16[256,1024]{1,0:T(8,128)(2,1)}, u32[]{:S(2)}) copy-start(bf16[256,1024]{1,0:T(8,128)(2,1)} %param.21) | copy-start | bytes 1572868
  66.8 13.9 %all-to-all-start.1 = ((bf16[64,1,4]{2,1,0:T(2,128)(2,1)}), bf16[64,1,4]{2,1,0:T(2,128)(2,1)S(1)}, u32[]{:S(2)}, u32[]{:S(2)}) async-start(bf16[64,1,4]{2,1,0:T(2,128)(2,1)} %all_to_all.16), calls=%async_computation.1 | async-start | bytes 65536 | tf_op jit(solution)/shard_map/all_to_all | solution.py:86
  109.9 0.7 copy-start.2
  162.1 1.2 slice-start
  171.4 13.2 %slice-start.1 = ((f32[2048,16]{0,1:T(8,128)}), f32[256,16]{0,1:T(8,128)S(1)}, s32[]{:S(2)}) async-start(f32[2048,16]{0,1:T(8,128)} %copy-done.2), calls=%async_computation.6 | async-start | bytes 32768 | tf_op jit(solution)/shard_map/slice | solution.py:19
  220.2 0.6 copy-start.3
  223.1 3.7 copy-start.4
  223.1 3.8 copy-start.11
  229.1 0.8 copy-start.6
  229.9 2.0 copy-start.9
  233.9 357.5 %all-to-all-start.2 = ((bf16[64,4,128]{2,1,0:T(4,128)(2,1)}), bf16[64,4,128]{2,1,0:T(4,128)(2,1)S(1)}, u32[]{:S(2)}, u32[]{:S(2)}) async-start(bf16[64,4,128]{2,1,0:T(4,128)(2,1)} %reshape.110), calls=%async_computation.2 | async-start | bytes 131072 | tf_op jit(solution)/shard_map/all_to_all | solution.py:189
  244.5 361.6 %all-reduce.2.cloned.1.call-start = ((), (), s32[]{:S(2)}) async-start(), calls=%async_computation.3 | async-start | bytes 1048576 | tf_op jit(solution)/shard_map/psum | solution.py:213
Sparse Core Ops, SparseCore 0:
  64.8 97.2 all-gather.4
  249.4 191.2 all-reduce.1
where the time goes:
time: 620 us; the launch traced here: 615 us
  blocking collectives  392 us (63%)
  local copies, waits for them, and re-layouts  64.8 us (10%)
  waiting for transfers between devices  46.2 us (7%)
  other arithmetic  39.6 us (6%)
  matrix products  30.9 us (5%)
  starting transfers between devices  26.7 us (4%)
  between operations  14.4 us (2%)
    psum x1, blocking collectives, local(): weight_grad, bias_grad = lax.psum((weight_acc, bias_acc), 'rows')  242 us
    psum x1, blocking collectives, local(): query_grad = lax.psum(query_acc, ('rows', 'vars'))  98.8 us
    all_gather x2, blocking collectives, combined_all(): pieces = jax.tree.map(lambda part: lax.all_gather(part, axis), value)  51 us
    all_gather x1, waiting for transfers between devices, combined_all(): pieces = jax.tree.map(lambda part: lax.all_gather(part, axis), value)  27.7 us
    add x7, other arithmetic, combine(): first[2] * left_factor[:, :, None] + second[2] * right_factor[:, :, None]  26.8 us
    while x3, local copies, waits for them, and re-layouts, combined_all(): lax.scan(lambda so_far, piece: (join(so_far, piece), None), head, tail)  15.5 us
  transfers between devices with their start and end apart: 5, of which 3 were waited for; matrix products, arithmetic and copies ran while one was open for 4% of the time, Pallas kernels for 0%

commit v1 on v0

v1 whole, which is shorter than its diff:
```python
import math

import jax
import jax.numpy as jnp
from jax import lax
from jax.experimental import pallas as pl
from jax.experimental.pallas import tpu as pltpu
from jax.sharding import Mesh
from jax.sharding import PartitionSpec as P

D = 1024
H = 16
DH = 64
P_SIZE = 16
K = 4
PTS_BLK = 1024
PB = 32
PIX_BLK = PB * P_SIZE
LANES = 128
TILES = D // LANES
CHUNK = 24
INTERPRET = False

f32 = jnp.float32
bf16 = jnp.bfloat16


def iota(shape, axis):
    return lax.broadcasted_iota(jnp.int32, shape, axis)


def dot(first, second):
    return lax.dot_general(first, second, (((1,), (0,)), ((), ())), preferred_element_type=f32)


def dot_t(first, second):
    return lax.dot_general(first, second, (((1,), (1,)), ((), ())), preferred_element_type=f32)


def split(value, parts):
    pieces = []
    for _ in range(parts):
        piece = value.astype(bf16)
        pieces.append(piece)
        value = value - piece.astype(f32)
    return pieces


def kernel_call(body, out_shape, scratch=(), in_specs=None, out_specs=None, aliases=None):
    extra = {}
    if in_specs is not None:
        extra["in_specs"] = in_specs
    if out_specs is not None:
        extra["out_specs"] = out_specs
    return pl.pallas_call(
        body,
        out_shape=out_shape,
        scratch_shapes=list(scratch),
        input_output_aliases=aliases or {},
        interpret=INTERPRET,
        compiler_params=pltpu.CompilerParams(vmem_limit_bytes=50 << 20),
        **extra,
    )


def interp_transposed(index_ref, weight_ref, block):
    where = pl.ds(block * PIX_BLK, PIX_BLK)
    index = [index_ref[k : k + 1, where] for k in range(K)]
    weight = [weight_ref[k : k + 1, where] for k in range(K)]
    points = iota((PTS_BLK, PIX_BLK), 0)
    matrix = jnp.zeros((PTS_BLK, PIX_BLK), f32)
    for k in range(K):
        total = jnp.zeros((1, PIX_BLK), f32)
        for j in range(K):
            total = total + jnp.where(index[j] == index[k], weight[j], 0.0)
        matrix = jnp.where(points == index[k], total, matrix)
    return matrix.astype(bf16)


def spread(rows, cols, test):
    return jnp.where(test(iota((rows, cols), 0), iota((rows, cols), 1)), 1.0, 0.0).astype(bf16)


def pixel_masks(var_local):
    wide = var_local * P_SIZE
    copy_rows = spread(wide, var_local, lambda r, c: r // P_SIZE == c)
    own_pixel = iota((wide, PIX_BLK), 0) % P_SIZE == iota((wide, PIX_BLK), 1) % P_SIZE
    return copy_rows, own_pixel


def head_expand(copies):
    return spread(copies * H, D, lambda r, c: r % H == c // DH)


def forward_kernel(
    index_ref, weight_ref, fields_ref, embed_ref, bias_ref, query_ref, x_ref, e_ref, s_ref, exch_ref, sum_ref
):
    var_local = fields_ref.shape[0]
    blocks = fields_ref.shape[1] // PTS_BLK
    wide = var_local * P_SIZE
    copy_rows, own_pixel = pixel_masks(var_local)
    gather = spread(PB, PIX_BLK, lambda r, c: r == c // P_SIZE)
    for block in range(blocks):
        matrix = interp_transposed(index_ref, weight_ref, block)
        pixels = dot(fields_ref[:, pl.ds(block * PTS_BLK, PTS_BLK)], matrix).astype(bf16)
        widened = jnp.where(own_pixel, dot(copy_rows, pixels), 0.0).astype(bf16)
        x_ref[pl.ds(block * PB, PB), :] = dot_t(gather, widened).astype(bf16)
    x_all = x_ref[...]
    patches = x_all.shape[0]
    var_of = iota((patches, wide), 1) // P_SIZE
    head_rows = iota((3 * H, D), 0) % H == iota((3 * H, D), 1) // DH
    parts = split(query_ref[...], 3)
    query_rows = jnp.concatenate(
        [jnp.broadcast_to(part.astype(f32), (H, D)) for part in parts], axis=0
    )
    query_rows = jnp.where(head_rows, query_rows, 0.0).astype(bf16)
    peak = None
    scores = []
    for v in range(var_local):
        own = jnp.where(var_of == v, x_all, jnp.zeros_like(x_all))
        embedded = (dot(own, embed_ref[...]) + bias_ref[v : v + 1, :].astype(f32)).astype(bf16)
        e_ref[v] = embedded
        three = dot_t(embedded, query_rows)
        score = (three[:, :H] + three[:, H : 2 * H] + three[:, 2 * H :]) * (1.0 / math.sqrt(DH))
        s_ref[v] = score
        scores.append(score)
        peak = score if peak is None else jnp.maximum(peak, score)
    expand = head_expand(2)
    total = None
    for v in range(var_local):
        weights = jnp.exp(scores[v] - peak)
        total = weights if total is None else total + weights
        both = jnp.concatenate(split(weights, 2), axis=1)
        term = dot(both, expand) * e_ref[v].astype(f32)
        if v == 0:
            sum_ref[...] = term
        else:
            sum_ref[...] += term
    groups = exch_ref.shape[0]
    width = D // groups
    for g in range(groups):
        exch_ref[g] = sum_ref[:, g * width : (g + 1) * width]


def target_of(column_ref, row_ref, depth, as_row):
    column = column_ref[...]
    row = row_ref[...]
    count = column.shape[0]
    same = column == row
    first, second = iota((count, count), 0), iota((count, count), 1)
    if as_row:
        rank = jnp.sum(jnp.where(same & (first < second), 1.0, 0.0), axis=0, keepdims=True)
        return row * depth + rank.astype(jnp.int32)
    rank = jnp.sum(jnp.where(same & (second < first), 1.0, 0.0), axis=1, keepdims=True)
    return column * depth + rank.astype(jnp.int32)


def stats_kernel(depth, column_ref, row_ref, inbox_ref, e_ref, s_ref, up_ref, ga_ref, stats_ref):
    patches = column_ref.shape[0]
    slots = inbox_ref.shape[0]
    target = target_of(column_ref, row_ref, depth, False)
    pick = jnp.where(iota((patches, slots), 1) == target, 1.0, 0.0).astype(bf16)
    upstream = dot(pick, inbox_ref[...])
    up_ref[...] = upstream.astype(bf16)
    reduce_heads = spread(D, H, lambda r, c: r // DH == c)
    var_local = e_ref.shape[0]
    peak = s_ref[0]
    for v in range(1, var_local):
        peak = jnp.maximum(peak, s_ref[v])
    total = jnp.zeros_like(peak)
    inner = jnp.zeros_like(peak)
    for v in range(var_local):
        high, low = split(upstream * e_ref[v].astype(f32), 2)
        grad_attn = dot(high, reduce_heads) + dot(low, reduce_heads)
        ga_ref[v] = grad_attn
        weights = jnp.exp(s_ref[v] - peak)
        total = total + weights
        inner = inner + weights * grad_attn
    packed = jnp.concatenate([peak, total, inner, jnp.zeros((patches, LANES - 3 * H), f32)], axis=1)
    if patches < LANES:
        packed = jnp.concatenate([packed, jnp.zeros((LANES - patches, LANES), f32)], axis=0)
    stats_ref[...] = packed.T[: 3 * H, :]


def combine_stats(stats_ref, patches):
    groups = stats_ref.shape[0]
    peaks, totals, inners = [], [], []
    for g in range(groups):
        rows = jnp.concatenate([stats_ref[g], jnp.zeros((LANES - 3 * H, LANES), f32)], axis=0).T
        rows = rows[:patches]
        peaks.append(rows[:, :H])
        totals.append(rows[:, H : 2 * H])
        inners.append(rows[:, 2 * H : 3 * H])
    peak = peaks[0]
    for other in peaks[1:]:
        peak = jnp.maximum(peak, other)
    factors = [jnp.exp(one - peak) for one in peaks]
    total = sum(f * t for f, t in zip(factors, totals))
    inner = sum(f * t for f, t in zip(factors, inners)) / total
    return peak, total, inner, factors


def tokens_kernel(depth, slots, place_ref, column_ref, row_ref, stats_ref, sums_ref, out_ref):
    patches = column_ref.shape[0]
    groups, _, width = sums_ref.shape
    _, total, _, factors = combine_stats(stats_ref, patches)
    heads = width // DH
    first = place_ref[0] * heads
    pick = jnp.where(
        iota((3 * H, width), 0) % H == first + iota((3 * H, width), 1) // DH, 1.0, 0.0
    ).astype(bf16)
    mixture = jnp.zeros((patches, width), f32)
    for g in range(groups):
        scale = jnp.concatenate(split(factors[g] / total, 3), axis=1)
        mixture = mixture + dot(scale, pick) * sums_ref[g]
    target = target_of(column_ref, row_ref, depth, True)
    place = jnp.where(iota((slots, patches), 0) == target, 1.0, 0.0).astype(bf16)
    out_ref[...] = dot(place, mixture.astype(bf16)).astype(bf16)


def backward_kernel(
    stats_ref, s_ref, ga_ref, up_ref, e_ref, x_ref, embed_ref, query_ref, wide_ref, gx_ref
):
    var_local, patches = e_ref.shape[0], e_ref.shape[1]
    wide = var_local * P_SIZE
    peak, total, inner, _ = combine_stats(stats_ref, patches)
    inverse = 1.0 / total
    expand = head_expand(2)
    query = query_ref[...]
    q_parts = split(query, 3)
    rows = [q_parts[0], q_parts[1], q_parts[2], q_parts[0], q_parts[1], q_parts[2]]
    query_rows = jnp.concatenate([jnp.broadcast_to(r.astype(f32), (H, D)) for r in rows], axis=0)
    on_head = iota((6 * H, D), 0) % H == iota((6 * H, D), 1) // DH
    query_rows = jnp.where(on_head, query_rows, 0.0).astype(bf16)
    upstream = up_ref[...].astype(f32)
    x_t = x_ref[...].astype(f32).T.astype(bf16)
    embed_t = embed_ref[...].astype(f32).T.astype(bf16)
    lane_var = iota((patches, wide), 1) // P_SIZE
    grad_x = jnp.zeros((patches, wide), f32)
    query_sum = jnp.zeros((2 * H, D), f32)
    for v in range(var_local):
        attention = jnp.exp(s_ref[v] - peak) * inverse
        grad_score = attention * (ga_ref[v] - inner) * (1.0 / math.sqrt(DH))
        attn = jnp.concatenate(split(attention, 2), axis=1)
        high, low = split(grad_score, 2)
        scored = jnp.concatenate([high, high, high, low, low, low], axis=1)
        grad = dot(attn, expand) * upstream + dot(scored, query_rows)
        low_grad = grad.astype(bf16)
        bias_row = jnp.sum(grad, axis=0, keepdims=True)
        weight_rows = dot(x_t[v * P_SIZE : (v + 1) * P_SIZE, :], low_grad)
        for t in range(TILES):
            cut = slice(t * LANES, (t + 1) * LANES)
            wide_ref[v * TILES + t, :P_SIZE, :] = weight_rows[:, cut]
            wide_ref[v * TILES + t, P_SIZE : P_SIZE + 1, :] = bias_row[:, cut]
        grad_x = jnp.where(lane_var == v, dot(low_grad, embed_t), grad_x)
        pair = jnp.concatenate([high.astype(f32), low.astype(f32)], axis=1)
        pair = jnp.concatenate([pair, jnp.zeros((patches, LANES - 2 * H), f32)], axis=1)
        query_sum = query_sum + dot(pair.T[: 2 * H, :].astype(bf16), e_ref[v])
    gx_ref[...] = grad_x.astype(bf16)
    diagonal = iota((2 * H, D), 0) % H == iota((2 * H, D), 1) // DH
    query_row = jnp.sum(jnp.where(diagonal, query_sum, 0.0), axis=0, keepdims=True)
    chunks = wide_ref.shape[0]
    share = D // chunks
    for j in range(chunks):
        t, at = (j * share) // LANES, (j * share) % LANES
        row = query_row[:, t * LANES : (t + 1) * LANES]
        wide_ref[j, P_SIZE + 1 : P_SIZE + 2, :] = row
        wide_ref[j, P_SIZE + 2 :, :] = jnp.zeros((CHUNK - P_SIZE - 2, LANES), f32)


def field_kernel(index_ref, weight_ref, gx_ref, out_ref):
    wide = gx_ref.shape[1]
    var_local = wide // P_SIZE
    blocks = gx_ref.shape[0] // PB
    gx_t = gx_ref[...].astype(f32).T.astype(bf16)
    fold = spread(var_local, wide, lambda r, c: c // P_SIZE == r)
    own_pixel = iota((wide, PIX_BLK), 0) % P_SIZE == iota((wide, PIX_BLK), 1) % P_SIZE
    copy = spread(PB, PIX_BLK, lambda r, c: r == c // P_SIZE)
    for block in range(blocks):
        wide_grad = dot(gx_t[:, block * PB : (block + 1) * PB], copy)
        wide_grad = jnp.where(own_pixel, wide_grad, 0.0).astype(bf16)
        grad = dot(fold, wide_grad).astype(bf16)
        matrix = interp_transposed(index_ref, weight_ref, block)
        out_ref[:, pl.ds(block * PTS_BLK, PTS_BLK)] = dot_t(grad, matrix)


def local(
    fields, stencil, stencil_weight, owner_map, embed_weight, embed_bias, agg_query, out_grad
):
    rows = ("r", "c")
    ring = lax.axis_size("r")
    groups = lax.axis_size("z")
    row_devices = ring * 2
    var_local = fields.shape[0]
    patches = owner_map.shape[0]
    capacity = out_grad.shape[0]
    depth = capacity // row_devices
    width = D // groups
    wide = var_local * P_SIZE
    shape = jax.ShapeDtypeStruct

    inbox = lax.all_to_all(
        out_grad.reshape(row_devices, depth, D), rows, split_axis=0, concat_axis=0, tiled=True
    ).reshape(capacity, D)

    index_t = stencil.T
    weight_t = stencil_weight.T
    embed_flat = embed_weight.reshape(wide, D)
    query = agg_query.reshape(1, D)
    row_map = owner_map.reshape(1, patches)
    x_all, embedded, scores, sums = kernel_call(
        forward_kernel,
        (
            shape((patches, wide), bf16),
            shape((var_local, patches, D), bf16),
            shape((var_local, patches, H), f32),
            shape((groups, patches, width), f32),
        ),
        scratch=[pltpu.VMEM((patches, D), f32)],
    )(index_t, weight_t, fields, embed_flat, embed_bias, query)

    upstream, grad_attn, stats = kernel_call(
        lambda *refs: stats_kernel(depth, *refs),
        (
            shape((patches, D), bf16),
            shape((var_local, patches, H), f32),
            shape((3 * H, LANES), f32),
        ),
    )(owner_map, row_map, inbox, embedded, scores)

    all_stats = lax.all_to_all(
        jnp.broadcast_to(stats[None], (groups, 3 * H, LANES)), "z", 0, 0, tiled=True
    )
    all_sums = lax.all_to_all(sums, "z", 0, 0, tiled=True)

    place = lax.axis_index("z").astype(jnp.int32).reshape(1)
    outbox = kernel_call(
        lambda *refs: tokens_kernel(depth, capacity, *refs),
        shape((capacity, width), bf16),
        in_specs=[pl.BlockSpec(memory_space=pltpu.SMEM)] + [pl.BlockSpec(memory_space=pltpu.VMEM)] * 4,
    )(place, owner_map, row_map, all_stats, all_sums)
    tokens = lax.all_to_all(
        outbox.reshape(row_devices, depth, width), rows, 0, 0, tiled=True
    ).reshape(capacity, width)

    chunks = row_devices if row_devices == var_local * TILES else var_local * TILES
    partial, grad_x = kernel_call(
        backward_kernel,
        (
            shape((chunks, CHUNK, LANES), f32),
            shape((patches, wide), bf16),
        ),
    )(all_stats, scores, grad_attn, upstream, embedded, x_all, embed_flat, query)

    field_grad = kernel_call(field_kernel, shape((var_local, blocks_of(fields)), f32))(
        index_t, weight_t, grad_x
    )

    halves = lax.all_to_all(
        partial.reshape(2, chunks // 2, CHUNK, LANES), "c", 0, 0, tiled=True
    )
    mine = lax.all_to_all(halves[0] + halves[1], "r", 0, 0, tiled=True)
    own = jnp.sum(mine.reshape(ring, chunks // (2 * ring), CHUNK, LANES), axis=0)
    spread_out = jnp.broadcast_to(own[None], (ring,) + own.shape).reshape(mine.shape)
    half = lax.all_to_all(spread_out, "r", 0, 0, tiled=True)
    other = lax.ppermute(half, "c", [(0, 1), (1, 0)])
    core = lax.axis_index("c")
    whole = jnp.where(
        core == 0, jnp.stack([half, other]), jnp.stack([other, half])
    ).reshape(var_local, TILES, CHUNK, LANES)
    weight_grad = whole[:, :, :P_SIZE, :].transpose(0, 2, 1, 3).reshape(var_local, P_SIZE, D)
    bias_grad = whole[:, :, P_SIZE, :].reshape(var_local, D)
    share = D // chunks
    per_tile = LANES // share
    query_rows = whole.reshape(TILES, per_tile, CHUNK, LANES)[:, :, P_SIZE + 1, :]
    query_sum = query_rows[:, 0, :]
    query_all = lax.all_to_all(
        jnp.broadcast_to(query_sum[None], (groups, TILES, LANES)), "z", 0, 0, tiled=True
    )
    query_grad = jnp.sum(query_all, axis=0).reshape(H, DH)
    return (tokens, field_grad, weight_grad, bias_grad, query_grad)


def blocks_of(fields):
    return fields.shape[1]


def solution(mesh):
    rows, groups = mesh.shape["rows"], mesh.shape["vars"]
    inner = Mesh(mesh.devices.reshape(rows // 2, 2, groups), ("r", "c", "z"))
    by_rows = ("r", "c")
    return jax.shard_map(
        local,
        mesh=inner,
        in_specs=(
            P("z", by_rows),
            P(by_rows, None),
            P(by_rows, None),
            P(by_rows, None),
            P("z", None, None),
            P("z", None),
            P(),
            P(by_rows, None),
        ),
        out_specs=(
            P(by_rows, "z"),
            P("z", by_rows),
            P("z", None, None),
            P("z", None),
            P(),
        ),
        check_vma=False,
    )
```

time: 620 us -> 154 us (0.25)
  blocking collectives: 392 us -> 61 us
  local copies, waits for them, and re-layouts: 64.8 us -> 7.62 us
  other arithmetic: 39.6 us -> 0.14 us
  matrix products: 30.9 us -> 0 us
  Pallas kernels: 0 us -> 20.1 us
  waiting for transfers between devices: 46.2 us -> 29.4 us
  between operations: 14.4 us -> 0.85 us
  starting transfers between devices: 26.7 us -> 34.5 us
    psum x2 -> x0, blocking collectives: 341 us -> none  [the longest x1 242 us: local(): weight_grad, bias_grad = lax.psum((weight_acc, bias_acc), 'rows')]
    all_to_all x0 -> x4, blocking collectives: none -> 61 us  [the longest x1 19.3 us: local(): lax.all_to_all(jnp.broadcast_to(stats[None], (groups, 3 * H, LANES)), 'z'...]
    all_gather x2 -> x0, blocking collectives: 51 us -> none  [combined_all(): pieces = jax.tree.map(lambda part: lax.all_gather(part, axis), value)]
    dot_general x13 -> x0, matrix products: 30.9 us -> none  [the longest x4 8.54 us: forward_block(): jnp.dot(field_block, matrix.T, preferred_element_type=jnp.float32)]
    all_gather x1 -> x0, waiting for transfers between devices: 27.7 us -> none  [combined_all(): pieces = jax.tree.map(lambda part: lax.all_gather(part, axis), value)]
    add x14 -> x1, other arithmetic: 27 us -> 0.04 us  [local(): mine = lax.all_to_all(halves[0] + halves[1], 'r', 0, 0, tiled=True)]
    pallas_call x0 -> x5, Pallas kernels: none -> 20.1 us  [the longest x1 6.87 us: local(): kernel_call(forward_kernel, (shape((patches, wide), bf16), shape((var_loc...]
    while x3 -> x0, local copies, waits for them, and re-layouts: 15.5 us -> none  [combined_all(): lax.scan(lambda so_far, piece: (join(so_far, piece), None), head, tail)]
  transfers between devices with their start and end apart: 5 -> 5, of which waited for: 3 -> 4; matrix products, arithmetic and copies ran while one was open for 4% -> 1% of each run, Pallas kernels for 0% -> 8%
where the time goes in v1:
time: 154 us
  blocking collectives  61 us (40%)
  starting transfers between devices  34.5 us (22%)
  waiting for transfers between devices  29.4 us (19%)
  Pallas kernels  20.1 us (13%)
  local copies, waits for them, and re-layouts  7.62 us (5%)
    all_to_all x1, blocking collectives, local(): lax.all_to_all(jnp.broadcast_to(stats[None], (groups, 3 * H, LANES)), 'z'...  19.3 us
    all_to_all x1, blocking collectives, local(): mine = lax.all_to_all(halves[0] + halves[1], 'r', 0, 0, tiled=True)  18.2 us
    all_to_all x1, blocking collectives, local(): half = lax.all_to_all(spread_out, 'r', 0, 0, tiled=True)  17.6 us
    all_to_all x1, starting transfers between devices, local(): lax.all_to_all(out_grad.reshape(row_devices, depth, D), rows, split_axis=...  11.8 us
    all_to_all x1, starting transfers between devices, local(): lax.all_to_all(outbox.reshape(row_devices, depth, width), rows, 0, 0, til...  10.4 us
    all_to_all x1, waiting for transfers between devices, local(): lax.all_to_all(out_grad.reshape(row_devices, depth, D), rows, split_axis=...  9.89 us
    all_to_all x1, waiting for transfers between devices, local(): all_sums = lax.all_to_all(sums, 'z', 0, 0, tiled=True)  8.66 us
    pallas_call x1, Pallas kernels, local(): kernel_call(forward_kernel, (shape((patches, wide), bf16), shape((var_loc...  6.87 us
  transfers between devices with their start and end apart: 5, of which 4 were waited for; matrix products, arithmetic and copies ran while one was open for 1% of the time, Pallas kernels for 8%

profile of v1, /device:TPU:1, one launch (start us, length us, event | category | flops | bytes accessed | tf_op | source)
XLA Modules:
  0.0 153.7 jit_solution(4567230950022095085)
XLA Ops:
  0.6 0.0 copy-start.8
  0.6 0.0 copy-start.9
  0.7 0.0 copy-start.2
  0.7 0.0 copy-start.3
  0.7 0.0 copy-start.4
  0.7 0.0 copy-start.1
  0.7 0.0 copy-start.7
  0.7 2.1 %reshape.62 = bf16[64,4,1024]{2,1,0:T(4,128)(2,1)} reshape(bf16[256,1024]{1,0:T(8,128)(2,1)} %param.15) | data formatting | bytes 1048576 | tf_op jit(solution)/shard_map/reshape | solution.py:303
  2.8 11.8 %all-to-all-start = ((bf16[64,4,1024]{2,1,0:T(4,128)(2,1)}), bf16[64,4,1024]{2,1,0:T(4,128)(2,1)}, u32[]{:S(2)}, u32[]{:S(2)}) async-start(bf16[64,4,1024]{2,1,0:T(4,128)(2,1)} %reshape.62), calls=%async_computation | async-start | bytes 1048576 | tf_op jit(solution)/shard_map/all_to_all | solution.py:302
  14.6 0.0 copy-done.8
  14.6 0.1 copy.22.refs_0_.refs_1_
  14.7 0.0 copy-done.9
  14.7 0.1 reshape.65.query_ref
  14.8 0.0 copy-done.2
  14.8 0.0 copy-done.3
  14.8 0.0 copy-done.4
  14.8 0.0 copy-done.1
  14.8 0.0 copy-done.7
  14.8 6.9 %shard_map.119 = (bf16[128,128]{1,0:T(8,128)(2,1)S(1)}, bf16[8,128,1024]{2,1,0:T(8,128)(2,1)S(1)}, f32[8,128,16]{2,1,0:T(8,128)S(1)}, f32[8,128,128]{2,1,0:T(8,128)}) custom-call(s32[4,2048]{1,0:T(4,128)S(1)} %bitcast.28, f32[4,2048]{1,0:T(4,128)S(1)} %bitcast.30, bf16[8,4096]{1,0:T(8,128)(2,1)S(1)} %copy-done.4, bf16[128,1024]{1,0:T(8,128)(2,1)S(1)} %bitcast.25, ...), custom_call_target="tpu_custom_call" | custom-call | tf_op jit(solution)/shard_map/pallas_call | solution.py:311
  21.7 0.6 copy-done.5
  22.3 9.9 %all-to-all-done = bf16[64,4,1024]{2,1,0:T(4,128)(2,1)} async-done(((bf16[64,4,1024]{2,1,0:T(4,128)(2,1)}), bf16[64,4,1024]{2,1,0:T(4,128)(2,1)}, u32[]{:S(2)}, u32[]{:S(2)}) %all-to-all-start) | async-done | bytes 524320 | tf_op jit(solution)/shard_map/all_to_all | solution.py:302
  32.2 1.2 reshape.63.refs_2_
  33.4 0.0 copy-start.6
  33.4 1.8 %shard_map.120 = (bf16[128,1024]{1,0:T(8,128)(2,1)S(1)}, f32[8,128,16]{2,1,0:T(8,128)S(1)}, f32[48,128]{1,0:T(8,128)S(1)}) custom-call(s32[128,1]{1,0:T(8,128)S(1)} %copy.22.refs_0_.refs_1_, s32[1,128]{1,0:T(1,128)S(1)} %bitcast.32, bf16[256,1024]{1,0:T(8,128)(2,1)S(1)} %reshape.63.refs_2_, bf16[8,128,1024]{2,1,0:T(8,128)(2,1)S(1)} %get-tuple-element.14.refs_3_.e_ref, ...), custom_call_target="tpu_custom_call" | custom-call | tf_op jit(solution)/shard_map/pallas_call | solution.py:322
  35.2 0.0 copy-done
  35.2 19.3 %all_to_all.40.refs_3_.stats_ref = f32[8,48,128]{2,1,0:T(8,128)S(1)} all-to-all(f32[8,48,128]{2,1,0:T(8,128)S(1)} %broadcast_in_dim.6), channel_id=1, replica_groups=mesh['r'=32,'c'=2,'z'=8] {'z'}, dimensions={0} | all-to-all | bytes 393216 | tf_op jit(solution)/shard_map/all_to_all | solution.py:331
  54.5 0.0 copy-done.6
  54.5 5.5 %shard_map.122 = (f32[64,24,128]{2,1,0:T(8,128)S(1)}, bf16[128,128]{1,0:T(8,128)(2,1)S(1)}) custom-call(f32[8,48,128]{2,1,0:T(8,128)S(1)} %all_to_all.40.refs_3_.stats_ref, f32[8,128,16]{2,1,0:T(8,128)S(1)} %get-tuple-element.15.refs_4_.s_ref, f32[8,128,16]{2,1,0:T(8,128)S(1)} %get-tuple-element.18.ga_ref, bf16[128,1024]{1,0:T(8,128)(2,1)S(1)} %get-tuple-element.19.up_ref, ...), custom_call_target="tpu_custom_call" | custom-call | tf_op jit(solution)/shard_map/pallas_call | solution.py:347
  60.0 6.0 %all_to_all.41 = f32[2,32,24,128]{3,2,1,0:T(8,128)S(1)} all-to-all(f32[2,32,24,128]{3,2,1,0:T(8,128)S(1)} %bitcast.27), channel_id=1, replica_groups=mesh['r'=32,'c'=2,'z'=8] {'c'}, dimensions={0} | all-to-all | bytes 1572864 | tf_op jit(solution)/shard_map/all_to_all | solution.py:359
  66.0 18.2 %all_to_all.42 = f32[32,24,128]{2,1,0:T(8,128)S(1)} all-to-all(f32[32,24,128]{2,1,0:T(8,128)S(1)} %fusion), channel_id=1, replica_groups=mesh['r'=32,'c'=2,'z'=8] {'r'}, dimensions={0} | all-to-all | bytes 786432 | tf_op jit(solution)/shard_map/all_to_all | solution.py:362
  84.2 17.6 %all_to_all.43 = f32[32,24,128]{2,1,0:T(8,128)S(1)} all-to-all(f32[32,24,128]{2,1,0:T(8,128)S(1)} %reshape.69), channel_id=1, replica_groups=mesh['r'=32,'c'=2,'z'=8] {'r'}, dimensions={0} | all-to-all | bytes 786432 | tf_op jit(solution)/shard_map/all_to_all | solution.py:365
  101.9 3.5 %all-to-all-start.2 = ((f32[8,128,128]{2,1,0:T(8,128)}), f32[8,128,128]{2,1,0:T(8,128)S(1)}, u32[]{:S(2)}, u32[]{:S(2)}) async-start(f32[8,128,128]{2,1,0:T(8,128)} %get-tuple-element.17), calls=%async_computation.2 | async-start | bytes 1048576 | tf_op jit(solution)/shard_map/all_to_all | solution.py:334
  105.4 5.4 %collective-permute-start = (f32[32,24,128]{2,1,0:T(8,128)S(1)}, f32[32,24,128]{2,1,0:T(8,128)S(1)}, u32[]{:S(2)}, u32[]{:S(2)}) collective-permute-start(f32[32,24,128]{2,1,0:T(8,128)S(1)} %all_to_all.43), channel_id=1, source_target_pairs={{0,8},{8,0},{1,9},{9,1},{2,10},{10,2},{3,11},{11,3},{4,12},{12,4},... | collective-permute-start | bytes 1179656 | tf_op jit(solution)/shard_map/ppermute | solution.py:366
  110.8 8.7 %all-to-all-done.2.refs_4_ = f32[8,128,128]{2,1,0:T(8,128)S(1)} async-done(((f32[8,128,128]{2,1,0:T(8,128)}), f32[8,128,128]{2,1,0:T(8,128)S(1)}, u32[]{:S(2)}, u32[]{:S(2)}) %all-to-all-start.2) | async-done | bytes 524320 | tf_op jit(solution)/shard_map/all_to_all | solution.py:334
  119.5 1.5 shard_map.121
  120.9 10.4 %all-to-all-start.3 = ((bf16[64,4,128]{2,1,0:T(4,128)(2,1)}), bf16[64,4,128]{2,1,0:T(4,128)(2,1)S(1)}, u32[]{:S(2)}, u32[]{:S(2)}) async-start(bf16[64,4,128]{2,1,0:T(4,128)(2,1)} %bitcast.5), calls=%async_computation.3 | async-start | bytes 131072 | tf_op jit(solution)/shard_map/all_to_all | solution.py:342
  131.4 4.5 %shard_map.123 = f32[8,4096]{1,0:T(8,128)} custom-call(s32[4,2048]{1,0:T(4,128)S(1)} %bitcast.29, f32[4,2048]{1,0:T(4,128)S(1)} %bitcast.31, bf16[128,128]{1,0:T(8,128)(2,1)S(1)} %get-tuple-element.21.gx_ref), custom_call_target="tpu_custom_call" | custom-call | tf_op jit(solution)/shard_map/pallas_call | solution.py:355
  135.9 5.6 %all-to-all-done.3 = bf16[64,4,128]{2,1,0:T(4,128)(2,1)S(1)} async-done(((bf16[64,4,128]{2,1,0:T(4,128)(2,1)}), bf16[64,4,128]{2,1,0:T(4,128)(2,1)S(1)}, u32[]{:S(2)}, u32[]{:S(2)}) %all-to-all-start.3) | async-done | bytes 65568 | tf_op jit(solution)/shard_map/all_to_all | solution.py:342
  141.5 0.0 collective-permute-done
  141.5 0.1 maximum_select_fusion
  141.5 0.1 fusion.1
  141.7 0.6 broadcast_in_dim.8
  142.3 3.3 %all-to-all-start.7 = ((f32[8,8,128]{2,1,0:T(8,128)}), f32[8,8,128]{2,1,0:T(8,128)S(1)}, u32[]{:S(2)}, u32[]{:S(2)}) async-start(f32[8,8,128]{2,1,0:T(8,128)} %broadcast_in_dim.8), calls=%async_computation.7 | async-start | bytes 65536 | tf_op jit(solution)/shard_map/all_to_all | solution.py:377
  145.6 0.8 copy_bitcast_fusion
  146.5 0.6 copy.28
  147.1 5.3 %all-to-all-done.7 = f32[8,8,128]{2,1,0:T(8,128)S(1)} async-done(((f32[8,8,128]{2,1,0:T(8,128)}), f32[8,8,128]{2,1,0:T(8,128)S(1)}, u32[]{:S(2)}, u32[]{:S(2)}) %all-to-all-start.7) | async-done | bytes 32800 | tf_op jit(solution)/shard_map/all_to_all | solution.py:377
  152.4 0.7 reshape.71
  153.1 0.6 copy.30
  (8 shorter events, 0.1 us)
Async XLA Ops:
  0.6 14.0 %copy-start.8 = (s32[128,1]{0,1:T(1,128)S(1)}, s32[128,1]{0,1:T(1,128)}, u32[]{:S(2)}) copy-start(s32[128,1]{0,1:T(1,128)} %param.11) | copy-start | bytes 1540
  0.6 14.1 %copy-start.9 = (f32[16,64]{1,0:T(8,128)S(1)}, f32[16,64]{1,0:T(8,128)}, u32[]{:S(2)}) copy-start(f32[16,64]{1,0:T(8,128)} %param.14) | copy-start | bytes 12292
  0.7 14.1 %copy-start.2 = (s32[2048,4]{0,1:T(4,128)S(1)}, s32[2048,4]{0,1:T(4,128)}, u32[]{:S(2)}) copy-start(s32[2048,4]{0,1:T(4,128)} %param.9) | copy-start | bytes 98308
  0.7 14.1 %copy-start.3 = (f32[2048,4]{0,1:T(4,128)S(1)}, f32[2048,4]{0,1:T(4,128)}, u32[]{:S(2)}) copy-start(f32[2048,4]{0,1:T(4,128)} %param.10) | copy-start | bytes 98308
  0.7 14.1 %copy-start.4 = (bf16[8,4096]{1,0:T(8,128)(2,1)S(1)}, bf16[8,4096]{1,0:T(8,128)(2,1)}, u32[]{:S(2)}) copy-start(bf16[8,4096]{1,0:T(8,128)(2,1)} %fields_ref.1) | copy-start | bytes 196612
  0.7 14.1 %copy-start.1 = (bf16[8,16,1024]{2,1,0:T(8,128)(2,1)S(1)}, bf16[8,16,1024]{2,1,0:T(8,128)(2,1)}, u32[]{:S(2)}) copy-start(bf16[8,16,1024]{2,1,0:T(8,128)(2,1)} %param.12) | copy-start | bytes 786436
  0.7 14.1 %copy-start.7 = (bf16[8,1024]{1,0:T(8,128)(2,1)S(1)}, bf16[8,1024]{1,0:T(8,128)(2,1)}, u32[]{:S(2)}) copy-start(bf16[8,1024]{1,0:T(8,128)(2,1)} %bias_ref.1) | copy-start | bytes 49156
  2.8 29.4 %all-to-all-start = ((bf16[64,4,1024]{2,1,0:T(4,128)(2,1)}), bf16[64,4,1024]{2,1,0:T(4,128)(2,1)}, u32[]{:S(2)}, u32[]{:S(2)}) async-start(bf16[64,4,1024]{2,1,0:T(4,128)(2,1)} %reshape.62), calls=%async_computation | async-start | bytes 1048576 | tf_op jit(solution)/shard_map/all_to_all | solution.py:302
  21.7 0.6 copy-start.5
  22.3 12.9 %copy-start = (bf16[8,128,1024]{2,1,0:T(8,128)(2,1)}, bf16[8,128,1024]{2,1,0:T(8,128)(2,1)S(1)}, u32[]{:S(2)}) copy-start(bf16[8,128,1024]{2,1,0:T(8,128)(2,1)S(1)} %get-tuple-element.14.refs_3_.e_ref) | copy-start | bytes 6291460
  33.4 21.1 %copy-start.6 = (bf16[128,128]{1,0:T(8,128)(2,1)S(1)}, bf16[128,128]{1,0:T(8,128)(2,1)}, u32[]{:S(2)}) copy-start(bf16[128,128]{1,0:T(8,128)(2,1)} %copy-done.5) | copy-start | bytes 98308
  101.9 17.6 %all-to-all-start.2 = ((f32[8,128,128]{2,1,0:T(8,128)}), f32[8,128,128]{2,1,0:T(8,128)S(1)}, u32[]{:S(2)}, u32[]{:S(2)}) async-start(f32[8,128,128]{2,1,0:T(8,128)} %get-tuple-element.17), calls=%async_computation.2 | async-start | bytes 1048576 | tf_op jit(solution)/shard_map/all_to_all | solution.py:334
  105.4 36.1 %collective-permute-start = (f32[32,24,128]{2,1,0:T(8,128)S(1)}, f32[32,24,128]{2,1,0:T(8,128)S(1)}, u32[]{:S(2)}, u32[]{:S(2)}) collective-permute-start(f32[32,24,128]{2,1,0:T(8,128)S(1)} %all_to_all.43), channel_id=1, source_target_pairs={{0,8},{8,0},{1,9},{9,1},{2,10},{10,2},{3,11},{11,3},{4,12},{12,4},... | collective-permute-start | bytes 1179656 | tf_op jit(solution)/shard_map/ppermute | solution.py:366
  120.9 20.5 %all-to-all-start.3 = ((bf16[64,4,128]{2,1,0:T(4,128)(2,1)}), bf16[64,4,128]{2,1,0:T(4,128)(2,1)S(1)}, u32[]{:S(2)}, u32[]{:S(2)}) async-start(bf16[64,4,128]{2,1,0:T(4,128)(2,1)} %bitcast.5), calls=%async_computation.3 | async-start | bytes 131072 | tf_op jit(solution)/shard_map/all_to_all | solution.py:342
  142.3 10.1 %all-to-all-start.7 = ((f32[8,8,128]{2,1,0:T(8,128)}), f32[8,8,128]{2,1,0:T(8,128)S(1)}, u32[]{:S(2)}, u32[]{:S(2)}) async-start(f32[8,8,128]{2,1,0:T(8,128)} %broadcast_in_dim.8), calls=%async_computation.7 | async-start | bytes 65536 | tf_op jit(solution)/shard_map/all_to_all | solution.py:377

commit v2 on v1

--- a/solution.py
+++ b/solution.py
@@ -139,7 +139,7 @@
     groups = exch_ref.shape[0]
     width = D // groups
     for g in range(groups):
-        exch_ref[g] = sum_ref[:, g * width : (g + 1) * width]
+        exch_ref[g, :patches, :] = sum_ref[:, g * width : (g + 1) * width]
 
 
 def target_of(column_ref, row_ref, depth, as_row):
@@ -155,7 +155,9 @@
     return column * depth + rank.astype(jnp.int32)
 
 
-def stats_kernel(depth, column_ref, row_ref, inbox_ref, e_ref, s_ref, up_ref, ga_ref, stats_ref):
+def stats_kernel(
+    depth, column_ref, row_ref, inbox_ref, e_ref, s_ref, old_ref, up_ref, ga_ref, exch_ref, stats_ref, sems
+):
     patches = column_ref.shape[0]
     slots = inbox_ref.shape[0]
     target = target_of(column_ref, row_ref, depth, False)
@@ -180,13 +182,22 @@
     if patches < LANES:
         packed = jnp.concatenate([packed, jnp.zeros((LANES - patches, LANES), f32)], axis=0)
     stats_ref[...] = packed.T[: 3 * H, :]
-
-
-def combine_stats(stats_ref, patches):
-    groups = stats_ref.shape[0]
+    copies = [
+        pltpu.make_async_copy(stats_ref, exch_ref.at[g, pl.ds(patches, 3 * H)], sems.at[g])
+        for g in range(exch_ref.shape[0])
+    ]
+    for copy in copies:
+        copy.start()
+    for copy in copies:
+        copy.wait()
+
+
+def combine_stats(exch_ref, patches):
+    groups = exch_ref.shape[0]
     peaks, totals, inners = [], [], []
     for g in range(groups):
-        rows = jnp.concatenate([stats_ref[g], jnp.zeros((LANES - 3 * H, LANES), f32)], axis=0).T
+        stats = exch_ref[g, patches : patches + 3 * H, :]
+        rows = jnp.concatenate([stats, jnp.zeros((LANES - 3 * H, LANES), f32)], axis=0).T
         rows = rows[:patches]
         peaks.append(rows[:, :H])
         totals.append(rows[:, H : 2 * H])
@@ -200,10 +211,10 @@
     return peak, total, inner, factors
 
 
-def tokens_kernel(depth, slots, place_ref, column_ref, row_ref, stats_ref, sums_ref, out_ref):
+def tokens_kernel(depth, slots, place_ref, column_ref, row_ref, exch_ref, out_ref):
     patches = column_ref.shape[0]
-    groups, _, width = sums_ref.shape
-    _, total, _, factors = combine_stats(stats_ref, patches)
+    groups, _, width = exch_ref.shape
+    _, total, _, factors = combine_stats(exch_ref, patches)
     heads = width // DH
     first = place_ref[0] * heads
     pick = jnp.where(
@@ -212,18 +223,18 @@
     mixture = jnp.zeros((patches, width), f32)
     for g in range(groups):
         scale = jnp.concatenate(split(factors[g] / total, 3), axis=1)
-        mixture = mixture + dot(scale, pick) * sums_ref[g]
+        mixture = mixture + dot(scale, pick) * exch_ref[g, :patches, :]
     target = target_of(column_ref, row_ref, depth, True)
     place = jnp.where(iota((slots, patches), 0) == target, 1.0, 0.0).astype(bf16)
-    out_ref[...] = dot(place, mixture.astype(bf16)).astype(bf16)
+    out_ref[...] = dot(place, mixture.astype(bf16))
 
 
 def backward_kernel(
-    stats_ref, s_ref, ga_ref, up_ref, e_ref, x_ref, embed_ref, query_ref, wide_ref, gx_ref
+    exch_ref, s_ref, ga_ref, up_ref, e_ref, x_ref, embed_ref, query_ref, wide_ref, gx_ref
 ):
     var_local, patches = e_ref.shape[0], e_ref.shape[1]
     wide = var_local * P_SIZE
-    peak, total, inner, _ = combine_stats(stats_ref, patches)
+    peak, total, inner, _ = combine_stats(exch_ref, patches)
     inverse = 1.0 / total
     expand = head_expand(2)
     query = query_ref[...]
@@ -259,13 +270,10 @@
     gx_ref[...] = grad_x.astype(bf16)
     diagonal = iota((2 * H, D), 0) % H == iota((2 * H, D), 1) // DH
     query_row = jnp.sum(jnp.where(diagonal, query_sum, 0.0), axis=0, keepdims=True)
-    chunks = wide_ref.shape[0]
-    share = D // chunks
-    for j in range(chunks):
-        t, at = (j * share) // LANES, (j * share) % LANES
-        row = query_row[:, t * LANES : (t + 1) * LANES]
-        wide_ref[j, P_SIZE + 1 : P_SIZE + 2, :] = row
-        wide_ref[j, P_SIZE + 2 :, :] = jnp.zeros((CHUNK - P_SIZE - 2, LANES), f32)
+    half = wide_ref.shape[0] // 2
+    for t in range(TILES):
+        at = (t // (TILES // 2)) * half + t % (TILES // 2)
+        wide_ref[at, P_SIZE + 1 : P_SIZE + 2, :] = query_row[:, t * LANES : (t + 1) * LANES]
 
 
 def field_kernel(index_ref, weight_ref, gx_ref, out_ref):
@@ -314,70 +322,82 @@
             shape((patches, wide), bf16),
             shape((var_local, patches, D), bf16),
             shape((var_local, patches, H), f32),
-            shape((groups, patches, width), f32),
+            shape((groups, patches + 3 * H, width), f32),
         ),
         scratch=[pltpu.VMEM((patches, D), f32)],
     )(index_t, weight_t, fields, embed_flat, embed_bias, query)
 
-    upstream, grad_attn, stats = kernel_call(
+    vmem = pl.BlockSpec(memory_space=pltpu.VMEM)
+    anywhere = pl.BlockSpec(memory_space=pl.ANY)
+    upstream, grad_attn, exchange = kernel_call(
         lambda *refs: stats_kernel(depth, *refs),
         (
             shape((patches, D), bf16),
             shape((var_local, patches, H), f32),
-            shape((3 * H, LANES), f32),
+            shape(sums.shape, f32),
         ),
-    )(owner_map, row_map, inbox, embedded, scores)
-
-    all_stats = lax.all_to_all(
-        jnp.broadcast_to(stats[None], (groups, 3 * H, LANES)), "z", 0, 0, tiled=True
-    )
-    all_sums = lax.all_to_all(sums, "z", 0, 0, tiled=True)
-
-    place = lax.axis_index("z").astype(jnp.int32).reshape(1)
-    outbox = kernel_call(
-        lambda *refs: tokens_kernel(depth, capacity, *refs),
-        shape((capacity, width), bf16),
-        in_specs=[pl.BlockSpec(memory_space=pltpu.SMEM)] + [pl.BlockSpec(memory_space=pltpu.VMEM)] * 4,
-    )(place, owner_map, row_map, all_stats, all_sums)
-    tokens = lax.all_to_all(
-        outbox.reshape(row_devices, depth, width), rows, 0, 0, tiled=True
-    ).reshape(capacity, width)
-
-    chunks = row_devices if row_devices == var_local * TILES else var_local * TILES
+        scratch=[pltpu.VMEM((3 * H, LANES), f32), pltpu.SemaphoreType.DMA((groups,))],
+        in_specs=[vmem] * 5 + [anywhere],
+        out_specs=(vmem, vmem, anywhere),
+        aliases={5: 2},
+    )(owner_map, row_map, inbox, embedded, scores, sums)
+    exchange = lax.all_to_all(exchange, "z", 0, 0, tiled=True)
+
+    chunks = var_local * TILES
     partial, grad_x = kernel_call(
         backward_kernel,
         (
             shape((chunks, CHUNK, LANES), f32),
             shape((patches, wide), bf16),
         ),
-    )(all_stats, scores, grad_attn, upstream, embedded, x_all, embed_flat, query)
+    )(exchange, scores, grad_attn, upstream, embedded, x_all, embed_flat, query)
+
+    place = lax.axis_index("z").astype(jnp.int32).reshape(1)
+    outbox = kernel_call(
+        lambda *refs: tokens_kernel(depth, capacity, *refs),
+        shape((capacity, width), f32),
+        in_specs=[pl.BlockSpec(memory_space=pltpu.SMEM)] + [vmem] * 3,
+    )(place, owner_map, row_map, exchange)
 
     field_grad = kernel_call(field_kernel, shape((var_local, blocks_of(fields)), f32))(
         index_t, weight_t, grad_x
     )
 
+    core = lax.axis_index("c")
+    share = chunks // (2 * ring)
+    both = 2 * depth
     halves = lax.all_to_all(
         partial.reshape(2, chunks // 2, CHUNK, LANES), "c", 0, 0, tiled=True
     )
-    mine = lax.all_to_all(halves[0] + halves[1], "r", 0, 0, tiled=True)
-    own = jnp.sum(mine.reshape(ring, chunks // (2 * ring), CHUNK, LANES), axis=0)
-    spread_out = jnp.broadcast_to(own[None], (ring,) + own.shape).reshape(mine.shape)
-    half = lax.all_to_all(spread_out, "r", 0, 0, tiled=True)
-    other = lax.ppermute(half, "c", [(0, 1), (1, 0)])
-    core = lax.axis_index("c")
-    whole = jnp.where(
-        core == 0, jnp.stack([half, other]), jnp.stack([other, half])
-    ).reshape(var_local, TILES, CHUNK, LANES)
+    halves = halves[0] + halves[1]
+    going = jnp.concatenate(
+        [halves.reshape(ring, share * CHUNK, LANES), outbox.reshape(ring, both, width)], axis=1
+    )
+    coming = lax.all_to_all(going, "r", 0, 0, tiled=True)
+    query_half = lax.psum(halves[: TILES // 2, P_SIZE + 1, :], "z")
+    own = jnp.sum(coming[:, : share * CHUNK], axis=0).reshape(share, CHUNK, LANES)
+    spare = jnp.zeros((share, CHUNK - P_SIZE - 1, LANES), f32)
+    spare = spare.at[0, : TILES // 2].set(query_half)
+    own = jnp.concatenate([own[:, : P_SIZE + 1], spare], axis=1)
+    half = lax.all_to_all(
+        jnp.broadcast_to(own[None], (ring,) + own.shape), "r", 0, 0, tiled=True
+    )
+
+    arrived = coming[:, share * CHUNK :].astype(bf16).reshape(ring, 2, depth, width)
+    swap = [(0, 1), (1, 0)]
+    crossed = lax.ppermute(jnp.where(core == 0, arrived[:, 1], arrived[:, 0]), "c", swap)
+    kept = jnp.where(core == 0, arrived[:, 0], arrived[:, 1])
+    tokens = jnp.where(
+        core == 0, jnp.stack([kept, crossed], axis=1), jnp.stack([crossed, kept], axis=1)
+    ).reshape(capacity, width)
+
+    other = lax.ppermute(half, "c", swap)
+    whole = jnp.where(core == 0, jnp.stack([half, other]), jnp.stack([other, half]))
+    query_rows = whole[:, :, 0, P_SIZE + 1 : P_SIZE + 1 + TILES // 2, :]
+    query_grad = jnp.sum(query_rows, axis=1).reshape(H, DH)
+    whole = whole.reshape(var_local, TILES, CHUNK, LANES)
     weight_grad = whole[:, :, :P_SIZE, :].transpose(0, 2, 1, 3).reshape(var_local, P_SIZE, D)
     bias_grad = whole[:, :, P_SIZE, :].reshape(var_local, D)
-    share = D // chunks
-    per_tile = LANES // share
-    query_rows = whole.reshape(TILES, per_tile, CHUNK, LANES)[:, :, P_SIZE + 1, :]
-    query_sum = query_rows[:, 0, :]
-    query_all = lax.all_to_all(
-        jnp.broadcast_to(query_sum[None], (groups, TILES, LANES)), "z", 0, 0, tiled=True
-    )
-    query_grad = jnp.sum(query_all, axis=0).reshape(H, DH)
     return (tokens, field_grad, weight_grad, bias_grad, query_grad)
 
 

time: 154 us -> 132 us (0.86)
  blocking collectives: 61 us -> 16.6 us
  waiting for transfers between devices: 29.4 us -> 43.9 us
  starting transfers between devices: 34.5 us -> 40 us
  Pallas kernels: 20.1 us -> 21.9 us
  other arithmetic: 0.14 us -> 1.78 us
    all_to_all x3 -> x0, blocking collectives: 55 us -> none  [the longest x1 19.3 us: local(): lax.all_to_all(jnp.broadcast_to(stats[None], (groups, 3 * H, LANES)), 'z'...]
    all_to_all x3, waiting for transfers between devices: 19.6 us -> 33.6 us  [the longest x1 22.2 us: local(): exchange = lax.all_to_all(exchange, 'z', 0, 0, tiled=True)]
    psum x0 -> x1, blocking collectives: none -> 12.1 us  [local(): query_half = lax.psum(halves[:TILES // 2, P_SIZE + 1, :], 'z')]
    ppermute x1 -> x2, starting transfers between devices: 5.44 us -> 8.89 us  [the longest x1 6.97 us: local(): other = lax.ppermute(half, 'c', swap)]
    pallas_call x1, Pallas kernels: 1.8 us -> 4.14 us  [local(): kernel_call(lambda *refs: stats_kernel(depth, *refs), (shape((patches, D)...]
    all_to_all x3, starting transfers between devices: 17.3 us -> 19.5 us  [the longest x1 10 us: local(): exchange = lax.all_to_all(exchange, 'z', 0, 0, tiled=True)]
  transfers between devices with their start and end apart: 5 -> 6, of which waited for: 4 -> 5; matrix products, arithmetic and copies ran while one was open for 1% -> 1% of each run, Pallas kernels for 8% -> 9%
where the time goes in v2:
time: 132 us
  waiting for transfers between devices  43.9 us (33%)
  starting transfers between devices  40 us (30%)
  Pallas kernels  21.9 us (17%)
  blocking collectives  16.6 us (13%)
  local copies, waits for them, and re-layouts  6.77 us (5%)
  other arithmetic  1.78 us (1%)
    all_to_all x1, waiting for transfers between devices, local(): exchange = lax.all_to_all(exchange, 'z', 0, 0, tiled=True)  22.2 us
    psum x1, blocking collectives, local(): query_half = lax.psum(halves[:TILES // 2, P_SIZE + 1, :], 'z')  12.1 us
    all_to_all x1, starting transfers between devices, local(): lax.all_to_all(out_grad.reshape(row_devices, depth, D), rows, split_axis=...  11.6 us
    all_to_all x1, starting transfers between devices, local(): exchange = lax.all_to_all(exchange, 'z', 0, 0, tiled=True)  10 us
    all_to_all x1, waiting for transfers between devices, local(): lax.all_to_all(out_grad.reshape(row_devices, depth, D), rows, split_axis=...  9.14 us
    ppermute x1, starting transfers between devices, local(): other = lax.ppermute(half, 'c', swap)  6.97 us
    pallas_call x1, Pallas kernels, local(): kernel_call(forward_kernel, (shape((patches, wide), bf16), shape((var_loc...  6.96 us
    all_to_all x1, waiting for transfers between devices, local(): lax.all_to_all(jnp.broadcast_to(own[None], (ring,) + own.shape), 'r', 0,...  6.93 us
  transfers between devices with their start and end apart: 6, of which 5 were waited for; matrix products, arithmetic and copies ran while one was open for 1% of the time, Pallas kernels for 9%

profile of v2, /device:TPU:1, one launch (start us, length us, event | category | flops | bytes accessed | tf_op | source)
XLA Modules:
  0.0 131.7 jit_solution(18041184744195444137)
XLA Ops:
  0.6 0.0 copy-start.7
  0.6 0.0 copy-start.6
  0.7 0.0 copy-start.2
  0.7 0.0 copy-start.3
  0.7 0.0 copy-start.1
  0.7 0.0 copy-start.4
  0.7 0.0 copy-start.5
  0.7 2.1 %reshape.169 = bf16[64,4,1024]{2,1,0:T(4,128)(2,1)} reshape(bf16[256,1024]{1,0:T(8,128)(2,1)} %param.17) | data formatting | bytes 1048576 | tf_op jit(solution)/shard_map/reshape | solution.py:311
  2.8 11.6 %all-to-all-start = ((bf16[64,4,1024]{2,1,0:T(4,128)(2,1)}), bf16[64,4,1024]{2,1,0:T(4,128)(2,1)S(1)}, u32[]{:S(2)}, u32[]{:S(2)}) async-start(bf16[64,4,1024]{2,1,0:T(4,128)(2,1)} %reshape.169), calls=%async_computation | async-start | bytes 1048576 | tf_op jit(solution)/shard_map/all_to_all | solution.py:310
  14.4 0.0 copy-done.7
  14.4 0.1 reshape.172.query_ref
  14.5 0.0 copy-done.6
  14.5 0.1 copy.37.refs_0_.refs_1_
  14.6 0.0 copy-done.2
  14.6 0.0 copy-done.3
  14.6 0.0 copy-done.1
  14.6 0.0 copy-done.4
  14.6 0.0 copy-done.5
  14.6 7.0 %shard_map.119 = (bf16[128,128]{1,0:T(8,128)(2,1)S(1)}, bf16[8,128,1024]{2,1,0:T(8,128)(2,1)S(1)}, f32[8,128,16]{2,1,0:T(8,128)S(1)}, f32[8,176,128]{2,1,0:T(8,128)}) custom-call(s32[4,2048]{1,0:T(4,128)S(1)} %bitcast.49, f32[4,2048]{1,0:T(4,128)S(1)} %bitcast.51, bf16[8,4096]{1,0:T(8,128)(2,1)S(1)} %copy-done.4, bf16[128,1024]{1,0:T(8,128)(2,1)S(1)} %bitcast.45, ...), custom_call_target="tpu_custom_call" | custom-call | tf_op jit(solution)/shard_map/pallas_call | solution.py:319
  21.6 0.0 copy-start
  21.6 1.3 %copy-done = bf16[8,128,1024]{2,1,0:T(8,128)(2,1)} copy-done((bf16[8,128,1024]{2,1,0:T(8,128)(2,1)}, bf16[8,128,1024]{2,1,0:T(8,128)(2,1)S(1)}, u32[]{:S(2)}) %copy-start) | copy-done | bytes 2097176
  22.9 9.1 %all-to-all-done = bf16[64,4,1024]{2,1,0:T(4,128)(2,1)S(1)} async-done(((bf16[64,4,1024]{2,1,0:T(4,128)(2,1)}), bf16[64,4,1024]{2,1,0:T(4,128)(2,1)S(1)}, u32[]{:S(2)}, u32[]{:S(2)}) %all-to-all-start) | async-done | bytes 524320 | tf_op jit(solution)/shard_map/all_to_all | solution.py:310
  32.1 0.1 reshape.170.refs_2_
  32.2 4.1 %shard_map.120 = (bf16[128,1024]{1,0:T(8,128)(2,1)S(1)}, f32[8,128,16]{2,1,0:T(8,128)S(1)}, f32[8,176,128]{2,1,0:T(8,128)}) custom-call(s32[128,1]{1,0:T(8,128)S(1)} %copy.37.refs_0_.refs_1_, s32[1,128]{1,0:T(1,128)S(1)} %bitcast.53, bf16[256,1024]{1,0:T(8,128)(2,1)S(1)} %reshape.170.refs_2_, ...), custom_call_target="tpu_custom_call", output_to_operand_aliasing={{2}: (5, {})} | custom-call | tf_op jit(solution)/shard_map/pallas_call | solution.py:332
  36.4 10.0 %all-to-all-start.1 = ((f32[8,176,128]{2,1,0:T(8,128)}), f32[8,176,128]{2,1,0:T(8,128)S(1)}, u32[]{:S(2)}, u32[]{:S(2)}) async-start(f32[8,176,128]{2,1,0:T(8,128)} %get-tuple-element.29), calls=%async_computation.1 | async-start | bytes 1441792 | tf_op jit(solution)/shard_map/all_to_all | solution.py:344
  46.4 22.2 %all-to-all-done.1.exch_ref.refs_3_ = f32[8,176,128]{2,1,0:T(8,128)S(1)} async-done(((f32[8,176,128]{2,1,0:T(8,128)}), f32[8,176,128]{2,1,0:T(8,128)S(1)}, u32[]{:S(2)}, u32[]{:S(2)}) %all-to-all-start.1) | async-done | bytes 720928 | tf_op jit(solution)/shard_map/all_to_all | solution.py:344
  68.6 5.5 %shard_map.121 = (f32[64,24,128]{2,1,0:T(8,128)S(1)}, bf16[128,128]{1,0:T(8,128)(2,1)S(1)}) custom-call(f32[8,176,128]{2,1,0:T(8,128)S(1)} %all-to-all-done.1.exch_ref.refs_3_, f32[8,128,16]{2,1,0:T(8,128)S(1)} %get-tuple-element.27.refs_4_.s_ref, f32[8,128,16]{2,1,0:T(8,128)S(1)} %get-tuple-element.30.ga_ref, ...), custom_call_target="tpu_custom_call" | custom-call | tf_op jit(solution)/shard_map/pallas_call | solution.py:347
  74.0 4.5 %all_to_all.25 = f32[2,32,24,128]{3,2,1,0:T(8,128)S(1)} all-to-all(f32[2,32,24,128]{3,2,1,0:T(8,128)S(1)} %bitcast.47), channel_id=1, replica_groups=mesh['r'=32,'c'=2,'z'=8] {'c'}, dimensions={0} | all-to-all | bytes 1572864 | tf_op jit(solution)/shard_map/all_to_all | solution.py:369
  78.6 0.8 shard_map.122
  79.4 0.9 pad_maximum_fusion
  80.3 4.5 %all-to-all-start.3 = ((f32[32,32,128]{2,1,0:T(8,128)}), f32[32,32,128]{2,1,0:T(8,128)S(1)}, u32[]{:S(2)}, u32[]{:S(2)}) async-start(f32[32,32,128]{2,1,0:T(8,128)} %pad_maximum_fusion), calls=%async_computation.3 | async-start | bytes 1048576 | tf_op jit(solution)/shard_map/all_to_all | solution.py:376
  84.8 12.1 %psum.7 = f32[1,4,128]{2,1,0:T(4,128)S(1)} all-reduce(f32[1,4,128]{2,1,0:T(4,128)S(1)} %bitcast.67), channel_id=1, replica_groups=mesh['r'=32,'c'=2,'z'=8] {'z'}, use_global_device_ids=true, to_apply=%region_1.0 | all-reduce | flops 512 | bytes 4096 | tf_op jit(solution)/shard_map/psum | solution.py:377
  96.9 4.5 %all-to-all-done.3 = f32[32,32,128]{2,1,0:T(8,128)S(1)} async-done(((f32[32,32,128]{2,1,0:T(8,128)}), f32[32,32,128]{2,1,0:T(8,128)S(1)}, u32[]{:S(2)}, u32[]{:S(2)}) %all-to-all-start.3) | async-done | bytes 524320 | tf_op jit(solution)/shard_map/all_to_all | solution.py:376
  101.4 0.8 broadcast_in_dim.10
  102.2 4.9 %all-to-all-start.4 = ((f32[32,1,24,128]{3,2,1,0:T(8,128)}), f32[32,1,24,128]{3,2,1,0:T(8,128)S(1)}, u32[]{:S(2)}, u32[]{:S(2)}) async-start(f32[32,1,24,128]{3,2,1,0:T(8,128)} %broadcast_in_dim.10), calls=%async_computation.4 | async-start | bytes 786432 | tf_op jit(solution)/shard_map/all_to_all | solution.py:382
  107.1 4.5 %shard_map.123 = f32[8,4096]{1,0:T(8,128)} custom-call(s32[4,2048]{1,0:T(4,128)S(1)} %bitcast.50, f32[4,2048]{1,0:T(4,128)S(1)} %bitcast.52, bf16[128,128]{1,0:T(8,128)(2,1)S(1)} %get-tuple-element.34.gx_ref), custom_call_target="tpu_custom_call" | custom-call | tf_op jit(solution)/shard_map/pallas_call | solution.py:362
  111.7 6.9 %all-to-all-done.4 = f32[32,1,24,128]{3,2,1,0:T(8,128)S(1)} async-done(((f32[32,1,24,128]{3,2,1,0:T(8,128)}), f32[32,1,24,128]{3,2,1,0:T(8,128)S(1)}, u32[]{:S(2)}, u32[]{:S(2)}) %all-to-all-start.4) | async-done | bytes 393248 | tf_op jit(solution)/shard_map/all_to_all | solution.py:382
  118.6 7.0 %collective-permute-start.1 = (f32[32,1,24,128]{3,2,0,1:T(8,128)S(1)}, f32[32,1,24,128]{3,2,0,1:T(8,128)S(1)}, u32[]{:S(2)}, u32[]{:S(2)}) collective-permute-start(f32[32,1,24,128]{3,2,0,1:T(8,128)S(1)} %bitcast.57), channel_id=1, source_target_pairs={{0,8},{8,0},{1,9},{9,1},{2,10},{10,2},{3,11},{11,3},{4,12},{12,4},... | collective-permute-start | bytes 1179656 | tf_op jit(solution)/shard_map/ppermute | solution.py:394
  125.6 1.9 %collective-permute-start = (bf16[32,4,128]{2,1,0:T(4,128)(2,1)S(1)}, bf16[32,4,128]{2,1,0:T(4,128)(2,1)S(1)}, u32[]{:S(2)}, u32[]{:S(2)}) collective-permute-start(bf16[32,4,128]{2,1,0:T(4,128)(2,1)S(1)} %fusion.1), channel_id=1, source_target_pairs={{0,8},{8,0},{1,9},{9,1},{2,10},{10,2},{3,11},{11,3},{4,12},{12,4},... | collective-permute-start | bytes 98312 | tf_op jit(solution)/shard_map/ppermute | solution.py:388
  127.6 1.1 collective-permute-done
  128.7 0.7 maximum_select_fusion.1
  129.4 0.0 collective-permute-done.1
  129.4 0.1 maximum_select_fusion
  129.5 0.9 copy_bitcast_fusion
  130.3 0.1 slice_reduce_fusion.2
  130.4 0.6 copy.52
  131.1 0.7 reshape.180
  (8 shorter events, 0.2 us)
Async XLA Ops:
  0.6 13.8 %copy-start.7 = (f32[16,64]{1,0:T(8,128)S(1)}, f32[16,64]{1,0:T(8,128)}, u32[]{:S(2)}) copy-start(f32[16,64]{1,0:T(8,128)} %param.16) | copy-start | bytes 12292
  0.6 13.8 %copy-start.6 = (s32[128,1]{0,1:T(1,128)S(1)}, s32[128,1]{0,1:T(1,128)}, u32[]{:S(2)}) copy-start(s32[128,1]{0,1:T(1,128)} %param.13) | copy-start | bytes 1540
  0.7 13.9 %copy-start.2 = (s32[2048,4]{0,1:T(4,128)S(1)}, s32[2048,4]{0,1:T(4,128)}, u32[]{:S(2)}) copy-start(s32[2048,4]{0,1:T(4,128)} %param.11) | copy-start | bytes 98308
  0.7 13.9 %copy-start.3 = (f32[2048,4]{0,1:T(4,128)S(1)}, f32[2048,4]{0,1:T(4,128)}, u32[]{:S(2)}) copy-start(f32[2048,4]{0,1:T(4,128)} %param.12) | copy-start | bytes 98308
  0.7 13.9 %copy-start.1 = (bf16[8,16,1024]{2,1,0:T(8,128)(2,1)S(1)}, bf16[8,16,1024]{2,1,0:T(8,128)(2,1)}, u32[]{:S(2)}) copy-start(bf16[8,16,1024]{2,1,0:T(8,128)(2,1)} %param.14) | copy-start | bytes 786436
  0.7 13.9 %copy-start.4 = (bf16[8,4096]{1,0:T(8,128)(2,1)S(1)}, bf16[8,4096]{1,0:T(8,128)(2,1)}, u32[]{:S(2)}) copy-start(bf16[8,4096]{1,0:T(8,128)(2,1)} %fields_ref.1) | copy-start | bytes 196612
  0.7 13.9 %copy-start.5 = (bf16[8,1024]{1,0:T(8,128)(2,1)S(1)}, bf16[8,1024]{1,0:T(8,128)(2,1)}, u32[]{:S(2)}) copy-start(bf16[8,1024]{1,0:T(8,128)(2,1)} %bias_ref.1) | copy-start | bytes 49156
  2.8 29.3 %all-to-all-start = ((bf16[64,4,1024]{2,1,0:T(4,128)(2,1)}), bf16[64,4,1024]{2,1,0:T(4,128)(2,1)S(1)}, u32[]{:S(2)}, u32[]{:S(2)}) async-start(bf16[64,4,1024]{2,1,0:T(4,128)(2,1)} %reshape.169), calls=%async_computation | async-start | bytes 1048576 | tf_op jit(solution)/shard_map/all_to_all | solution.py:310
  21.6 1.3 %copy-start = (bf16[8,128,1024]{2,1,0:T(8,128)(2,1)}, bf16[8,128,1024]{2,1,0:T(8,128)(2,1)S(1)}, u32[]{:S(2)}) copy-start(bf16[8,128,1024]{2,1,0:T(8,128)(2,1)S(1)} %get-tuple-element.26.refs_3_.e_ref) | copy-start | bytes 6291460
  36.4 32.2 %all-to-all-start.1 = ((f32[8,176,128]{2,1,0:T(8,128)}), f32[8,176,128]{2,1,0:T(8,128)S(1)}, u32[]{:S(2)}, u32[]{:S(2)}) async-start(f32[8,176,128]{2,1,0:T(8,128)} %get-tuple-element.29), calls=%async_computation.1 | async-start | bytes 1441792 | tf_op jit(solution)/shard_map/all_to_all | solution.py:344
  80.3 21.1 %all-to-all-start.3 = ((f32[32,32,128]{2,1,0:T(8,128)}), f32[32,32,128]{2,1,0:T(8,128)S(1)}, u32[]{:S(2)}, u32[]{:S(2)}) async-start(f32[32,32,128]{2,1,0:T(8,128)} %pad_maximum_fusion), calls=%async_computation.3 | async-start | bytes 1048576 | tf_op jit(solution)/shard_map/all_to_all | solution.py:376
  102.2 16.4 %all-to-all-start.4 = ((f32[32,1,24,128]{3,2,1,0:T(8,128)}), f32[32,1,24,128]{3,2,1,0:T(8,128)S(1)}, u32[]{:S(2)}, u32[]{:S(2)}) async-start(f32[32,1,24,128]{3,2,1,0:T(8,128)} %broadcast_in_dim.10), calls=%async_computation.4 | async-start | bytes 786432 | tf_op jit(solution)/shard_map/all_to_all | solution.py:382
  118.6 10.8 %collective-permute-start.1 = (f32[32,1,24,128]{3,2,0,1:T(8,128)S(1)}, f32[32,1,24,128]{3,2,0,1:T(8,128)S(1)}, u32[]{:S(2)}, u32[]{:S(2)}) collective-permute-start(f32[32,1,24,128]{3,2,0,1:T(8,128)S(1)} %bitcast.57), channel_id=1, source_target_pairs={{0,8},{8,0},{1,9},{9,1},{2,10},{10,2},{3,11},{11,3},{4,12},{12,4},... | collective-permute-start | bytes 1179656 | tf_op jit(solution)/shard_map/ppermute | solution.py:394
  125.6 3.1 %collective-permute-start = (bf16[32,4,128]{2,1,0:T(4,128)(2,1)S(1)}, bf16[32,4,128]{2,1,0:T(4,128)(2,1)S(1)}, u32[]{:S(2)}, u32[]{:S(2)}) collective-permute-start(bf16[32,4,128]{2,1,0:T(4,128)(2,1)S(1)} %fusion.1), channel_id=1, source_target_pairs={{0,8},{8,0},{1,9},{9,1},{2,10},{10,2},{3,11},{11,3},{4,12},{12,4},... | collective-permute-start | bytes 98312 | tf_op jit(solution)/shard_map/ppermute | solution.py:388

commit v3 on v2

--- a/solution.py
+++ b/solution.py
@@ -46,7 +46,7 @@
     return pieces
 
 
-def kernel_call(body, out_shape, scratch=(), in_specs=None, out_specs=None, aliases=None):
+def kernel_call(body, out_shape, mib, scratch=(), in_specs=None, out_specs=None, aliases=None):
     extra = {}
     if in_specs is not None:
         extra["in_specs"] = in_specs
@@ -58,7 +58,7 @@
         scratch_shapes=list(scratch),
         input_output_aliases=aliases or {},
         interpret=INTERPRET,
-        compiler_params=pltpu.CompilerParams(vmem_limit_bytes=50 << 20),
+        compiler_params=pltpu.CompilerParams(vmem_limit_bytes=mib << 20),
         **extra,
     )
 
@@ -211,9 +211,10 @@
     return peak, total, inner, factors
 
 
-def tokens_kernel(depth, slots, place_ref, column_ref, row_ref, exch_ref, out_ref):
+def merge_kernel(depth, slots, place_ref, column_ref, row_ref, exch_ref, halves_ref, going_ref, query_ref):
     patches = column_ref.shape[0]
     groups, _, width = exch_ref.shape
+    ring, rows = halves_ref.shape[1], halves_ref.shape[2]
     _, total, _, factors = combine_stats(exch_ref, patches)
     heads = width // DH
     first = place_ref[0] * heads
@@ -226,7 +227,48 @@
         mixture = mixture + dot(scale, pick) * exch_ref[g, :patches, :]
     target = target_of(column_ref, row_ref, depth, True)
     place = jnp.where(iota((slots, patches), 0) == target, 1.0, 0.0).astype(bf16)
-    out_ref[...] = dot(place, mixture.astype(bf16))
+    tokens = dot(place, mixture.astype(bf16))
+    going_ref[:, rows:, :] = tokens.reshape(ring, slots // ring, width)
+    going_ref[:, :rows, :] = halves_ref[0] + halves_ref[1]
+    share = rows // CHUNK
+    for t in range(TILES // 2):
+        at = (t % share) * CHUNK + P_SIZE + 1
+        query_ref[t : t + 1, :] = going_ref[t // share, at : at + 1, :]
+
+
+def own_kernel(coming_ref, query_ref, out_ref):
+    ring, rows = out_ref.shape[0], out_ref.shape[1]
+    own = coming_ref[0, :rows, :]
+    for r in range(1, ring):
+        own = own + coming_ref[r, :rows, :]
+    spare = jnp.concatenate(
+        [query_ref[...], jnp.zeros((CHUNK - P_SIZE - 1 - TILES // 2, LANES), f32)], axis=0
+    )
+    rest = [own[CHUNK:]] if rows > CHUNK else []
+    own = jnp.concatenate([own[: P_SIZE + 1], spare] + rest, axis=0)
+    for r in range(ring):
+        out_ref[r] = own
+
+
+def final_kernel(core_ref, half_ref, other_ref, weight_ref, bias_ref, query_ref):
+    ring, rows = half_ref.shape[0], half_ref.shape[1]
+    share = rows // CHUNK
+    low = core_ref[0] == 0
+    for c in range(2):
+        query = jnp.zeros((TILES // 2, LANES), f32)
+        for r in range(ring):
+            half, other = half_ref[r], other_ref[r]
+            block = jnp.where(low, half, other) if c == 0 else jnp.where(low, other, half)
+            for k in range(share):
+                v, t = divmod((c * ring + r) * share + k, TILES)
+                cut = slice(t * LANES, (t + 1) * LANES)
+                weight_ref[v * P_SIZE : (v + 1) * P_SIZE, cut] = block[k * CHUNK : k * CHUNK + P_SIZE]
+                bias_ref[v : v + 1, cut] = block[k * CHUNK + P_SIZE : k * CHUNK + P_SIZE + 1]
+            query = query + block[P_SIZE + 1 : P_SIZE + 1 + TILES // 2]
+        for t in range(TILES // 2):
+            at = (c * (TILES // 2) + t) * 2
+            query_ref[at : at + 1, :] = query[t : t + 1, :DH]
+            query_ref[at + 1 : at + 2, :] = query[t : t + 1, DH:]
 
 
 def backward_kernel(
@@ -295,7 +337,7 @@
 def local(
     fields, stencil, stencil_weight, owner_map, embed_weight, embed_bias, agg_query, out_grad
 ):
-    rows = ("r", "c")
+    by_rows = ("r", "c")
     ring = lax.axis_size("r")
     groups = lax.axis_size("z")
     row_devices = ring * 2
@@ -308,7 +350,7 @@
     shape = jax.ShapeDtypeStruct
 
     inbox = lax.all_to_all(
-        out_grad.reshape(row_devices, depth, D), rows, split_axis=0, concat_axis=0, tiled=True
+        out_grad.reshape(row_devices, depth, D), by_rows, split_axis=0, concat_axis=0, tiled=True
     ).reshape(capacity, D)
 
     index_t = stencil.T
@@ -324,6 +366,7 @@
             shape((var_local, patches, H), f32),
             shape((groups, patches + 3 * H, width), f32),
         ),
+        mib=20,
         scratch=[pltpu.VMEM((patches, D), f32)],
     )(index_t, weight_t, fields, embed_flat, embed_bias, query)
 
@@ -336,6 +379,7 @@
             shape((var_local, patches, H), f32),
             shape(sums.shape, f32),
         ),
+        mib=12,
         scratch=[pltpu.VMEM((3 * H, LANES), f32), pltpu.SemaphoreType.DMA((groups,))],
         in_specs=[vmem] * 5 + [anywhere],
         out_specs=(vmem, vmem, anywhere),
@@ -350,40 +394,31 @@
             shape((chunks, CHUNK, LANES), f32),
             shape((patches, wide), bf16),
         ),
+        mib=16,
     )(exchange, scores, grad_attn, upstream, embedded, x_all, embed_flat, query)
 
-    place = lax.axis_index("z").astype(jnp.int32).reshape(1)
-    outbox = kernel_call(
-        lambda *refs: tokens_kernel(depth, capacity, *refs),
-        shape((capacity, width), f32),
-        in_specs=[pl.BlockSpec(memory_space=pltpu.SMEM)] + [vmem] * 3,
-    )(place, owner_map, row_map, exchange)
-
-    field_grad = kernel_call(field_kernel, shape((var_local, blocks_of(fields)), f32))(
+    field_grad = kernel_call(field_kernel, shape((var_local, fields.shape[1]), f32), mib=16)(
         index_t, weight_t, grad_x
     )
 
-    core = lax.axis_index("c")
-    share = chunks // (2 * ring)
+    core = lax.axis_index("c").astype(jnp.int32)
+    place = lax.axis_index("z").astype(jnp.int32)
+    smem = pl.BlockSpec(memory_space=pltpu.SMEM)
+    rows = chunks // (2 * ring) * CHUNK
     both = 2 * depth
-    halves = lax.all_to_all(
-        partial.reshape(2, chunks // 2, CHUNK, LANES), "c", 0, 0, tiled=True
-    )
-    halves = halves[0] + halves[1]
-    going = jnp.concatenate(
-        [halves.reshape(ring, share * CHUNK, LANES), outbox.reshape(ring, both, width)], axis=1
-    )
+    halves = lax.all_to_all(partial.reshape(2, ring, rows, LANES), "c", 0, 0, tiled=True)
+    going, query_half = kernel_call(
+        lambda *refs: merge_kernel(depth, capacity, *refs),
+        (shape((ring, rows + both, LANES), f32), shape((TILES // 2, LANES), f32)),
+        mib=8,
+        in_specs=[smem] + [vmem] * 4,
+    )(place.reshape(1), owner_map, row_map, exchange, halves)
     coming = lax.all_to_all(going, "r", 0, 0, tiled=True)
-    query_half = lax.psum(halves[: TILES // 2, P_SIZE + 1, :], "z")
-    own = jnp.sum(coming[:, : share * CHUNK], axis=0).reshape(share, CHUNK, LANES)
-    spare = jnp.zeros((share, CHUNK - P_SIZE - 1, LANES), f32)
-    spare = spare.at[0, : TILES // 2].set(query_half)
-    own = jnp.concatenate([own[:, : P_SIZE + 1], spare], axis=1)
-    half = lax.all_to_all(
-        jnp.broadcast_to(own[None], (ring,) + own.shape), "r", 0, 0, tiled=True
-    )
-
-    arrived = coming[:, share * CHUNK :].astype(bf16).reshape(ring, 2, depth, width)
+    query_half = lax.psum(query_half, "z")
+    own = kernel_call(own_kernel, shape((ring, rows, LANES), f32), mib=8)(coming, query_half)
+    half = lax.all_to_all(own, "r", 0, 0, tiled=True)
+
+    arrived = coming[:, rows:].astype(bf16).reshape(ring, 2, depth, width)
     swap = [(0, 1), (1, 0)]
     crossed = lax.ppermute(jnp.where(core == 0, arrived[:, 1], arrived[:, 0]), "c", swap)
     kept = jnp.where(core == 0, arrived[:, 0], arrived[:, 1])
@@ -391,18 +426,16 @@
         core == 0, jnp.stack([kept, crossed], axis=1), jnp.stack([crossed, kept], axis=1)
     ).reshape(capacity, width)
 
+    half, tokens = lax.optimization_barrier((half, tokens))
     other = lax.ppermute(half, "c", swap)
-    whole = jnp.where(core == 0, jnp.stack([half, other]), jnp.stack([other, half]))
-    query_rows = whole[:, :, 0, P_SIZE + 1 : P_SIZE + 1 + TILES // 2, :]
-    query_grad = jnp.sum(query_rows, axis=1).reshape(H, DH)
-    whole = whole.reshape(var_local, TILES, CHUNK, LANES)
-    weight_grad = whole[:, :, :P_SIZE, :].transpose(0, 2, 1, 3).reshape(var_local, P_SIZE, D)
-    bias_grad = whole[:, :, P_SIZE, :].reshape(var_local, D)
+    weight_grad, bias_grad, query_grad = kernel_call(
+        final_kernel,
+        (shape((wide, D), f32), shape((var_local, D), f32), shape((H, DH), f32)),
+        mib=8,
+        in_specs=[smem, vmem, vmem],
+    )(core.reshape(1), half, other)
+    weight_grad = weight_grad.reshape(var_local, P_SIZE, D)
     return (tokens, field_grad, weight_grad, bias_grad, query_grad)
-
-
-def blocks_of(fields):
-    return fields.shape[1]
 
 
 def solution(mesh):

time: 132 us -> 134 us (1.015)
  starting transfers between devices: 40 us -> 43.7 us
  local copies, waits for them, and re-layouts: 6.77 us -> 8.56 us
  waiting for transfers between devices: 43.9 us -> 42.2 us
  other arithmetic: 1.78 us -> 0.09 us
    ppermute x1, starting transfers between devices: 1.92 us -> 5.52 us  [local(): lax.ppermute(jnp.where(core == 0, arrived[:, 1], arrived[:, 0]), 'c', swap)]
    pallas_call x2 -> x4, Pallas kernels: 5.33 us -> 7.8 us  [the longest x1 4.51 us: local(): kernel_call(field_kernel, shape((var_local, fields.shape[1]), f32), mib=16)]
    unnamed x18 -> x25, local copies, waits for them, and re-layouts: 2.1 us -> 4.57 us
    pallas_call x1, Pallas kernels: 4.14 us -> 2.56 us  [local(): kernel_call(lambda *refs: stats_kernel(depth, *refs), (shape((patches, D)...]
    pallas_call x1, Pallas kernels: 5.46 us -> 3.87 us  [local(): kernel_call(backward_kernel, (shape((chunks, CHUNK, LANES), f32), shape((...]
where the time goes in v3:
time: 134 us; the launch traced here: 133 us
  starting transfers between devices  43.7 us (33%)
  waiting for transfers between devices  42.2 us (31%)
  Pallas kernels  21.2 us (16%)
  blocking collectives  16.6 us (12%)
  local copies, waits for them, and re-layouts  8.56 us (6%)
    all_to_all x1, waiting for transfers between devices, local(): exchange = lax.all_to_all(exchange, 'z', 0, 0, tiled=True)  22.2 us
    psum x1, blocking collectives, local(): query_half = lax.psum(query_half, 'z')  12.1 us
    all_to_all x1, starting transfers between devices, local(): lax.all_to_all(out_grad.reshape(row_devices, depth, D), by_rows, split_ax...  11.8 us
    all_to_all x1, waiting for transfers between devices, local(): lax.all_to_all(out_grad.reshape(row_devices, depth, D), by_rows, split_ax...  10.4 us
    all_to_all x1, starting transfers between devices, local(): exchange = lax.all_to_all(exchange, 'z', 0, 0, tiled=True)  10 us
    ppermute x1, starting transfers between devices, local(): other = lax.ppermute(half, 'c', swap)  6.96 us
    pallas_call x1, Pallas kernels, local(): kernel_call(forward_kernel, (shape((patches, wide), bf16), shape((var_loc...  6.93 us
    ppermute x1, starting transfers between devices, local(): lax.ppermute(jnp.where(core == 0, arrived[:, 1], arrived[:, 0]), 'c', swap)  5.52 us
  transfers between devices with their start and end apart: 6, of which 5 were waited for; matrix products, arithmetic and copies ran while one was open for 1% of the time, Pallas kernels for 9%

profile of v3, /device:TPU:1, one launch (start us, length us, event | category | flops | bytes accessed | tf_op | source)
XLA Modules:
  0.0 133.2 jit_solution(6679626791664230471)
XLA Ops:
  0.6 0.0 copy-start.11
  0.6 0.0 copy-start.10
  0.7 0.0 copy-start.6
  0.7 0.0 copy-start.7
  0.7 0.0 copy-start
  0.7 0.0 copy-start.9
  0.7 0.0 copy-start.8
  0.7 2.1 %reshape.49 = bf16[64,4,1024]{2,1,0:T(4,128)(2,1)} reshape(bf16[256,1024]{1,0:T(8,128)(2,1)} %param.15) | data formatting | bytes 1048576 | tf_op jit(solution)/shard_map/reshape | solution.py:353
  2.8 11.8 %all-to-all-start = ((bf16[64,4,1024]{2,1,0:T(4,128)(2,1)}), bf16[64,4,1024]{2,1,0:T(4,128)(2,1)}, u32[]{:S(2)}, u32[]{:S(2)}) async-start(bf16[64,4,1024]{2,1,0:T(4,128)(2,1)} %reshape.49), calls=%async_computation | async-start | bytes 1048576 | tf_op jit(solution)/shard_map/all_to_all | solution.py:352
  14.6 0.0 copy-done.11
  14.6 0.1 reshape.52.query_ref
  14.7 0.0 copy-done.10
  14.7 0.1 copy.15.refs_0_.refs_1_
  14.8 0.0 copy-done.6
  14.8 0.0 copy-done.7
  14.8 0.0 copy-done
  14.8 0.0 copy-done.9
  14.8 0.0 copy-done.8
  14.8 6.9 %shard_map.119 = (bf16[128,128]{1,0:T(8,128)(2,1)S(1)}, bf16[8,128,1024]{2,1,0:T(8,128)(2,1)S(1)}, f32[8,128,16]{2,1,0:T(8,128)S(1)}, f32[8,176,128]{2,1,0:T(8,128)}) custom-call(s32[4,2048]{1,0:T(4,128)S(1)} %bitcast.26, f32[4,2048]{1,0:T(4,128)S(1)} %bitcast.28, bf16[8,4096]{1,0:T(8,128)(2,1)S(1)} %copy-done.8, bf16[128,1024]{1,0:T(8,128)(2,1)S(1)} %bitcast.23, ...), custom_call_target="tpu_custom_call" | custom-call | tf_op jit(solution)/shard_map/pallas_call | solution.py:361
  21.8 10.4 %all-to-all-done = bf16[64,4,1024]{2,1,0:T(4,128)(2,1)} async-done(((bf16[64,4,1024]{2,1,0:T(4,128)(2,1)}), bf16[64,4,1024]{2,1,0:T(4,128)(2,1)}, u32[]{:S(2)}, u32[]{:S(2)}) %all-to-all-start) | async-done | bytes 524320 | tf_op jit(solution)/shard_map/all_to_all | solution.py:352
  32.2 1.2 reshape.50.refs_2_
  33.4 2.6 %shard_map.120 = (bf16[128,1024]{1,0:T(8,128)(2,1)S(1)}, f32[8,128,16]{2,1,0:T(8,128)S(1)}, f32[8,176,128]{2,1,0:T(8,128)}) custom-call(s32[128,1]{1,0:T(8,128)S(1)} %copy.15.refs_0_.refs_1_, s32[1,128]{1,0:T(1,128)S(1)} %bitcast.30, bf16[256,1024]{1,0:T(8,128)(2,1)S(1)} %reshape.50.refs_2_, ...), custom_call_target="tpu_custom_call", output_to_operand_aliasing={{2}: (5, {})} | custom-call | tf_op jit(solution)/shard_map/pallas_call | solution.py:375
  35.9 0.0 copy-start.2
  35.9 0.8 copy-done.2
  36.7 0.0 copy-start.4
  36.7 0.7 copy-done.4
  37.4 10.0 %all-to-all-start.1 = ((f32[8,176,128]{2,1,0:T(8,128)}), f32[8,176,128]{2,1,0:T(8,128)S(1)}, u32[]{:S(2)}, u32[]{:S(2)}) async-start(f32[8,176,128]{2,1,0:T(8,128)} %get-tuple-element.24), calls=%async_computation.1 | async-start | bytes 1441792 | tf_op jit(solution)/shard_map/all_to_all | solution.py:388
  47.5 22.2 %all-to-all-done.1.exch_ref.refs_3_ = f32[8,176,128]{2,1,0:T(8,128)S(1)} async-done(((f32[8,176,128]{2,1,0:T(8,128)}), f32[8,176,128]{2,1,0:T(8,128)S(1)}, u32[]{:S(2)}, u32[]{:S(2)}) %all-to-all-start.1) | async-done | bytes 720928 | tf_op jit(solution)/shard_map/all_to_all | solution.py:388
  69.6 0.9 copy-done.1
  70.6 1.0 copy-done.3
  71.6 0.9 copy-done.5
  72.6 3.9 %shard_map.121 = (f32[64,24,128]{2,1,0:T(8,128)S(1)}, bf16[128,128]{1,0:T(8,128)(2,1)S(1)}) custom-call(f32[8,176,128]{2,1,0:T(8,128)S(1)} %all-to-all-done.1.exch_ref.refs_3_, f32[8,128,16]{2,1,0:T(8,128)S(1)} %get-tuple-element.22.refs_4_.s_ref, f32[8,128,16]{2,1,0:T(8,128)S(1)} %copy-done.3, bf16[128,1024]{1,0:T(8,128)(2,1)S(1)} %copy-done.5, ...), custom_call_target="tpu_custom_call" | custom-call | tf_op jit(solution)/shard_map/pallas_call | solution.py:391
  76.5 4.5 %all_to_all.25.refs_4_ = f32[2,32,24,128]{3,2,1,0:T(8,128)S(1)} all-to-all(f32[2,32,24,128]{3,2,1,0:T(8,128)S(1)} %bitcast.25), channel_id=1, replica_groups=mesh['r'=32,'c'=2,'z'=8] {'c'}, dimensions={0} | all-to-all | bytes 1572864 | tf_op jit(solution)/shard_map/all_to_all | solution.py:409
  80.9 1.6 %shard_map.122 = (f32[32,32,128]{2,1,0:T(8,128)}, f32[4,128]{1,0:T(4,128)S(1)}) custom-call(s32[1]{0:T(128)} %bitcast.refs_0_, s32[128,1]{1,0:T(8,128)S(1)} %copy.15.refs_0_.refs_1_, s32[1,128]{1,0:T(1,128)S(1)} %bitcast.31, f32[8,176,128]{2,1,0:T(8,128)S(1)} %all-to-all-done.1.exch_ref.refs_3_, f32[2,32,24,128]{3,2,1,0:T(8,128)S(1)} %all_to_all.25.refs_4_), custom_call_target="tpu_custom_call" | custom-call | tf_op jit(solution)/shard_map/pallas_call | solution.py:410
  82.6 4.5 %all-to-all-start.3 = ((f32[32,32,128]{2,1,0:T(8,128)}), f32[32,32,128]{2,1,0:T(8,128)S(1)}, u32[]{:S(2)}, u32[]{:S(2)}) async-start(f32[32,32,128]{2,1,0:T(8,128)} %get-tuple-element.29), calls=%async_computation.3 | async-start | bytes 1048576 | tf_op jit(solution)/shard_map/all_to_all | solution.py:416
  87.1 12.1 %psum.7.query_ref = f32[4,128]{1,0:T(4,128)S(1)} all-reduce(f32[4,128]{1,0:T(4,128)S(1)} %get-tuple-element.30), channel_id=1, replica_groups=mesh['r'=32,'c'=2,'z'=8] {'z'}, use_global_device_ids=true, to_apply=%region_0.0 | all-reduce | flops 512 | bytes 4096 | tf_op jit(solution)/shard_map/psum | solution.py:417
  99.2 4.5 %all-to-all-done.3.coming_ref = f32[32,32,128]{2,1,0:T(8,128)S(1)} async-done(((f32[32,32,128]{2,1,0:T(8,128)}), f32[32,32,128]{2,1,0:T(8,128)S(1)}, u32[]{:S(2)}, u32[]{:S(2)}) %all-to-all-start.3) | async-done | bytes 524320 | tf_op jit(solution)/shard_map/all_to_all | solution.py:416
  103.7 0.8 shard_map.123
  104.5 4.9 %all-to-all-start.4 = ((f32[32,24,128]{2,1,0:T(8,128)}), f32[32,24,128]{2,1,0:T(8,128)S(1)}, u32[]{:S(2)}, u32[]{:S(2)}) async-start(f32[32,24,128]{2,1,0:T(8,128)} %shard_map.123), calls=%async_computation.4 | async-start | bytes 786432 | tf_op jit(solution)/shard_map/all_to_all | solution.py:419
  109.5 5.5 %collective-permute-start = (bf16[32,4,128]{2,1,0:T(4,128)(2,1)S(1)}, bf16[32,4,128]{2,1,0:T(4,128)(2,1)S(1)}, u32[]{:S(2)}, u32[]{:S(2)}) collective-permute-start(bf16[32,4,128]{2,1,0:T(4,128)(2,1)S(1)} %fusion), channel_id=1, source_target_pairs={{0,8},{8,0},{1,9},{9,1},{2,10},{10,2},{3,11},{11,3},{4,12},{12,4},... | collective-permute-start | bytes 98312 | tf_op jit(solution)/shard_map/ppermute | solution.py:423
  115.0 0.8 collective-permute-done
  115.8 0.1 maximum_select_fusion
  115.9 0.7 copy.20
  116.6 4.3 %all-to-all-done.4.half_ref = f32[32,24,128]{2,1,0:T(8,128)S(1)} async-done(((f32[32,24,128]{2,1,0:T(8,128)}), f32[32,24,128]{2,1,0:T(8,128)S(1)}, u32[]{:S(2)}, u32[]{:S(2)}) %all-to-all-start.4) | async-done | bytes 393248 | tf_op jit(solution)/shard_map/all_to_all | solution.py:419
  120.9 7.0 %collective-permute-start.1 = (f32[32,24,128]{2,1,0:T(8,128)S(1)}, f32[32,24,128]{2,1,0:T(8,128)S(1)}, u32[]{:S(2)}, u32[]{:S(2)}) collective-permute-start(f32[32,24,128]{2,1,0:T(8,128)S(1)} %all-to-all-done.4.half_ref), channel_id=1, source_target_pairs={{0,8},{8,0},{1,9},{9,1},{2,10},{10,2},{3,11},{11,3},{4,12},{12,4},... | collective-permute-start | bytes 1179656 | tf_op jit(solution)/shard_map/ppermute | solution.py:430
  127.9 4.5 %shard_map.124 = f32[8,4096]{1,0:T(8,128)} custom-call(s32[4,2048]{1,0:T(4,128)S(1)} %bitcast.27, f32[4,2048]{1,0:T(4,128)S(1)} %bitcast.29, bf16[128,128]{1,0:T(8,128)(2,1)S(1)} %get-tuple-element.32.gx_ref), custom_call_target="tpu_custom_call" | custom-call | tf_op jit(solution)/shard_map/pallas_call | solution.py:400
  132.4 0.0 collective-permute-done.1.other_ref
  132.4 0.9 shard_map.125
  (6 shorter events, 0.1 us)
Async XLA Ops:
  0.6 14.0 %copy-start.11 = (f32[16,64]{1,0:T(8,128)S(1)}, f32[16,64]{1,0:T(8,128)}, u32[]{:S(2)}) copy-start(f32[16,64]{1,0:T(8,128)} %param.14) | copy-start | bytes 12292
  0.6 14.0 %copy-start.10 = (s32[128,1]{0,1:T(1,128)S(1)}, s32[128,1]{0,1:T(1,128)}, u32[]{:S(2)}) copy-start(s32[128,1]{0,1:T(1,128)} %param.11) | copy-start | bytes 1540
  0.7 14.1 %copy-start.6 = (s32[2048,4]{0,1:T(4,128)S(1)}, s32[2048,4]{0,1:T(4,128)}, u32[]{:S(2)}) copy-start(s32[2048,4]{0,1:T(4,128)} %param.9) | copy-start | bytes 98308
  0.7 14.1 %copy-start.7 = (f32[2048,4]{0,1:T(4,128)S(1)}, f32[2048,4]{0,1:T(4,128)}, u32[]{:S(2)}) copy-start(f32[2048,4]{0,1:T(4,128)} %param.10) | copy-start | bytes 98308
  0.7 14.1 %copy-start = (bf16[8,16,1024]{2,1,0:T(8,128)(2,1)S(1)}, bf16[8,16,1024]{2,1,0:T(8,128)(2,1)}, u32[]{:S(2)}) copy-start(bf16[8,16,1024]{2,1,0:T(8,128)(2,1)} %param.12) | copy-start | bytes 786436
  0.7 14.1 %copy-start.9 = (bf16[8,1024]{1,0:T(8,128)(2,1)S(1)}, bf16[8,1024]{1,0:T(8,128)(2,1)}, u32[]{:S(2)}) copy-start(bf16[8,1024]{1,0:T(8,128)(2,1)} %bias_ref.1) | copy-start | bytes 49156
  0.7 14.1 %copy-start.8 = (bf16[8,4096]{1,0:T(8,128)(2,1)S(1)}, bf16[8,4096]{1,0:T(8,128)(2,1)}, u32[]{:S(2)}) copy-start(bf16[8,4096]{1,0:T(8,128)(2,1)} %fields_ref.1) | copy-start | bytes 196612
  2.8 29.4 %all-to-all-start = ((bf16[64,4,1024]{2,1,0:T(4,128)(2,1)}), bf16[64,4,1024]{2,1,0:T(4,128)(2,1)}, u32[]{:S(2)}, u32[]{:S(2)}) async-start(bf16[64,4,1024]{2,1,0:T(4,128)(2,1)} %reshape.49), calls=%async_computation | async-start | bytes 1048576 | tf_op jit(solution)/shard_map/all_to_all | solution.py:352
  35.9 0.8 copy-start.2
  36.7 0.7 copy-start.4
  37.4 32.2 %all-to-all-start.1 = ((f32[8,176,128]{2,1,0:T(8,128)}), f32[8,176,128]{2,1,0:T(8,128)S(1)}, u32[]{:S(2)}, u32[]{:S(2)}) async-start(f32[8,176,128]{2,1,0:T(8,128)} %get-tuple-element.24), calls=%async_computation.1 | async-start | bytes 1441792 | tf_op jit(solution)/shard_map/all_to_all | solution.py:388
  69.6 1.0 copy-start.1
  70.6 1.0 copy-start.3
  71.6 0.9 copy-start.5
  82.6 21.1 %all-to-all-start.3 = ((f32[32,32,128]{2,1,0:T(8,128)}), f32[32,32,128]{2,1,0:T(8,128)S(1)}, u32[]{:S(2)}, u32[]{:S(2)}) async-start(f32[32,32,128]{2,1,0:T(8,128)} %get-tuple-element.29), calls=%async_computation.3 | async-start | bytes 1048576 | tf_op jit(solution)/shard_map/all_to_all | solution.py:416
  104.5 16.4 %all-to-all-start.4 = ((f32[32,24,128]{2,1,0:T(8,128)}), f32[32,24,128]{2,1,0:T(8,128)S(1)}, u32[]{:S(2)}, u32[]{:S(2)}) async-start(f32[32,24,128]{2,1,0:T(8,128)} %shard_map.123), calls=%async_computation.4 | async-start | bytes 786432 | tf_op jit(solution)/shard_map/all_to_all | solution.py:419
  109.5 6.4 %collective-permute-start = (bf16[32,4,128]{2,1,0:T(4,128)(2,1)S(1)}, bf16[32,4,128]{2,1,0:T(4,128)(2,1)S(1)}, u32[]{:S(2)}, u32[]{:S(2)}) collective-permute-start(bf16[32,4,128]{2,1,0:T(4,128)(2,1)S(1)} %fusion), channel_id=1, source_target_pairs={{0,8},{8,0},{1,9},{9,1},{2,10},{10,2},{3,11},{11,3},{4,12},{12,4},... | collective-permute-start | bytes 98312 | tf_op jit(solution)/shard_map/ppermute | solution.py:423
  120.9 11.5 %collective-permute-start.1 = (f32[32,24,128]{2,1,0:T(8,128)S(1)}, f32[32,24,128]{2,1,0:T(8,128)S(1)}, u32[]{:S(2)}, u32[]{:S(2)}) collective-permute-start(f32[32,24,128]{2,1,0:T(8,128)S(1)} %all-to-all-done.4.half_ref), channel_id=1, source_target_pairs={{0,8},{8,0},{1,9},{9,1},{2,10},{10,2},{3,11},{11,3},{4,12},{12,4},... | collective-permute-start | bytes 1179656 | tf_op jit(solution)/shard_map/ppermute | solution.py:430

commit v4 on v3

--- a/solution.py
+++ b/solution.py
@@ -44,6 +44,18 @@
         pieces.append(piece)
         value = value - piece.astype(f32)
     return pieces
+
+
+def over_vars(value, join):
+    shift = value.shape[1] // 2
+    while shift >= H:
+        value = join(value, pltpu.roll(value, shift, axis=1))
+        shift //= 2
+    return value
+
+
+def group(value, v):
+    return value[:, v * H : (v + 1) * H]
 
 
 def kernel_call(body, out_shape, mib, scratch=(), in_specs=None, out_specs=None, aliases=None):
@@ -114,23 +126,19 @@
         [jnp.broadcast_to(part.astype(f32), (H, D)) for part in parts], axis=0
     )
     query_rows = jnp.where(head_rows, query_rows, 0.0).astype(bf16)
-    peak = None
     scores = []
     for v in range(var_local):
         own = jnp.where(var_of == v, x_all, jnp.zeros_like(x_all))
         embedded = (dot(own, embed_ref[...]) + bias_ref[v : v + 1, :].astype(f32)).astype(bf16)
         e_ref[v] = embedded
         three = dot_t(embedded, query_rows)
-        score = (three[:, :H] + three[:, H : 2 * H] + three[:, 2 * H :]) * (1.0 / math.sqrt(DH))
-        s_ref[v] = score
-        scores.append(score)
-        peak = score if peak is None else jnp.maximum(peak, score)
+        scores.append(three[:, :H] + three[:, H : 2 * H] + three[:, 2 * H :])
+    scores = jnp.concatenate(scores, axis=1) * (1.0 / math.sqrt(DH))
+    s_ref[...] = scores
+    weights = split(jnp.exp(scores - over_vars(scores, jnp.maximum)), 2)
     expand = head_expand(2)
-    total = None
     for v in range(var_local):
-        weights = jnp.exp(scores[v] - peak)
-        total = weights if total is None else total + weights
-        both = jnp.concatenate(split(weights, 2), axis=1)
+        both = jnp.concatenate([group(part, v) for part in weights], axis=1)
         term = dot(both, expand) * e_ref[v].astype(f32)
         if v == 0:
             sum_ref[...] = term
@@ -155,30 +163,49 @@
     return column * depth + rank.astype(jnp.int32)
 
 
+def outbox_kernel(grad_ref, out_ref):
+    out_ref[...] = grad_ref[...].reshape(out_ref.shape)
+
+
 def stats_kernel(
-    depth, column_ref, row_ref, inbox_ref, e_ref, s_ref, old_ref, up_ref, ga_ref, exch_ref, stats_ref, sems
+    depth,
+    column_ref,
+    row_ref,
+    inbox_ref,
+    e_ref,
+    s_ref,
+    x_ref,
+    old_ref,
+    up_ref,
+    both_ref,
+    xt_ref,
+    exch_ref,
+    stats_ref,
+    sems,
 ):
     patches = column_ref.shape[0]
-    slots = inbox_ref.shape[0]
+    slots = inbox_ref.shape[0] * inbox_ref.shape[1]
     target = target_of(column_ref, row_ref, depth, False)
     pick = jnp.where(iota((patches, slots), 1) == target, 1.0, 0.0).astype(bf16)
-    upstream = dot(pick, inbox_ref[...])
+    upstream = dot(pick, inbox_ref[...].reshape(slots, D))
     up_ref[...] = upstream.astype(bf16)
     reduce_heads = spread(D, H, lambda r, c: r // DH == c)
     var_local = e_ref.shape[0]
-    peak = s_ref[0]
-    for v in range(1, var_local):
-        peak = jnp.maximum(peak, s_ref[v])
-    total = jnp.zeros_like(peak)
-    inner = jnp.zeros_like(peak)
+    grad_attn = []
     for v in range(var_local):
         high, low = split(upstream * e_ref[v].astype(f32), 2)
-        grad_attn = dot(high, reduce_heads) + dot(low, reduce_heads)
-        ga_ref[v] = grad_attn
-        weights = jnp.exp(s_ref[v] - peak)
-        total = total + weights
-        inner = inner + weights * grad_attn
-    packed = jnp.concatenate([peak, total, inner, jnp.zeros((patches, LANES - 3 * H), f32)], axis=1)
+        grad_attn.append(dot(high, reduce_heads) + dot(low, reduce_heads))
+    grad_attn = jnp.concatenate(grad_attn, axis=1)
+    scores = s_ref[...]
+    both_ref[0] = scores
+    both_ref[1] = grad_attn
+    xt_ref[...] = x_ref[...].astype(f32).T.astype(bf16)
+    peak = over_vars(scores, jnp.maximum)
+    weights = jnp.exp(scores - peak)
+    total = over_vars(weights, jnp.add)
+    inner = over_vars(weights * grad_attn, jnp.add)
+    packed = [group(peak, 0), group(total, 0), group(inner, 0)]
+    packed = jnp.concatenate(packed + [jnp.zeros((patches, LANES - 3 * H), f32)], axis=1)
     if patches < LANES:
         packed = jnp.concatenate([packed, jnp.zeros((LANES - patches, LANES), f32)], axis=0)
     stats_ref[...] = packed.T[: 3 * H, :]
@@ -272,12 +299,19 @@
 
 
 def backward_kernel(
-    exch_ref, s_ref, ga_ref, up_ref, e_ref, x_ref, embed_ref, query_ref, wide_ref, gx_ref
+    exch_ref, both_ref, up_ref, e_ref, xt_ref, embed_ref, query_ref, wide_ref, gx_ref
 ):
     var_local, patches = e_ref.shape[0], e_ref.shape[1]
     wide = var_local * P_SIZE
     peak, total, inner, _ = combine_stats(exch_ref, patches)
-    inverse = 1.0 / total
+    peak, inner, inverse = (
+        jnp.concatenate([one] * var_local, axis=1) for one in (peak, inner, 1.0 / total)
+    )
+    attention = jnp.exp(both_ref[0] - peak) * inverse
+    grad_score = attention * (both_ref[1] - inner) * (1.0 / math.sqrt(DH))
+    attention = split(attention, 2)
+    high, low = split(grad_score, 2)
+    turned = [part.astype(f32).T.astype(bf16) for part in (high, low)]
     expand = head_expand(2)
     query = query_ref[...]
     q_parts = split(query, 3)
@@ -286,17 +320,15 @@
     on_head = iota((6 * H, D), 0) % H == iota((6 * H, D), 1) // DH
     query_rows = jnp.where(on_head, query_rows, 0.0).astype(bf16)
     upstream = up_ref[...].astype(f32)
-    x_t = x_ref[...].astype(f32).T.astype(bf16)
+    x_t = xt_ref[...]
     embed_t = embed_ref[...].astype(f32).T.astype(bf16)
     lane_var = iota((patches, wide), 1) // P_SIZE
     grad_x = jnp.zeros((patches, wide), f32)
     query_sum = jnp.zeros((2 * H, D), f32)
     for v in range(var_local):
-        attention = jnp.exp(s_ref[v] - peak) * inverse
-        grad_score = attention * (ga_ref[v] - inner) * (1.0 / math.sqrt(DH))
-        attn = jnp.concatenate(split(attention, 2), axis=1)
-        high, low = split(grad_score, 2)
-        scored = jnp.concatenate([high, high, high, low, low, low], axis=1)
+        attn = jnp.concatenate([group(part, v) for part in attention], axis=1)
+        first, second = group(high, v), group(low, v)
+        scored = jnp.concatenate([first, first, first, second, second, second], axis=1)
         grad = dot(attn, expand) * upstream + dot(scored, query_rows)
         low_grad = grad.astype(bf16)
         bias_row = jnp.sum(grad, axis=0, keepdims=True)
@@ -306,9 +338,8 @@
             wide_ref[v * TILES + t, :P_SIZE, :] = weight_rows[:, cut]
             wide_ref[v * TILES + t, P_SIZE : P_SIZE + 1, :] = bias_row[:, cut]
         grad_x = jnp.where(lane_var == v, dot(low_grad, embed_t), grad_x)
-        pair = jnp.concatenate([high.astype(f32), low.astype(f32)], axis=1)
-        pair = jnp.concatenate([pair, jnp.zeros((patches, LANES - 2 * H), f32)], axis=1)
-        query_sum = query_sum + dot(pair.T[: 2 * H, :].astype(bf16), e_ref[v])
+        pair = jnp.concatenate([part[v * H : (v + 1) * H] for part in turned], axis=0)
+        query_sum = query_sum + dot(pair, e_ref[v])
     gx_ref[...] = grad_x.astype(bf16)
     diagonal = iota((2 * H, D), 0) % H == iota((2 * H, D), 1) // DH
     query_row = jnp.sum(jnp.where(diagonal, query_sum, 0.0), axis=0, keepdims=True)
@@ -350,8 +381,12 @@
     shape = jax.ShapeDtypeStruct
 
     inbox = lax.all_to_all(
-        out_grad.reshape(row_devices, depth, D), by_rows, split_axis=0, concat_axis=0, tiled=True
-    ).reshape(capacity, D)
+        kernel_call(outbox_kernel, shape((row_devices, depth, D), bf16), mib=8)(out_grad),
+        by_rows,
+        split_axis=0,
+        concat_axis=0,
+        tiled=True,
+    )
 
     index_t = stencil.T
     weight_t = stencil_weight.T
@@ -363,7 +398,7 @@
         (
             shape((patches, wide), bf16),
             shape((var_local, patches, D), bf16),
-            shape((var_local, patches, H), f32),
+            shape((patches, var_local * H), f32),
             shape((groups, patches + 3 * H, width), f32),
         ),
         mib=20,
@@ -372,19 +407,20 @@
 
     vmem = pl.BlockSpec(memory_space=pltpu.VMEM)
     anywhere = pl.BlockSpec(memory_space=pl.ANY)
-    upstream, grad_attn, exchange = kernel_call(
+    upstream, both, x_turned, exchange = kernel_call(
         lambda *refs: stats_kernel(depth, *refs),
         (
             shape((patches, D), bf16),
-            shape((var_local, patches, H), f32),
+            shape((2, patches, var_local * H), f32),
+            shape((wide, patches), bf16),
             shape(sums.shape, f32),
         ),
         mib=12,
         scratch=[pltpu.VMEM((3 * H, LANES), f32), pltpu.SemaphoreType.DMA((groups,))],
-        in_specs=[vmem] * 5 + [anywhere],
-        out_specs=(vmem, vmem, anywhere),
-        aliases={5: 2},
-    )(owner_map, row_map, inbox, embedded, scores, sums)
+        in_specs=[vmem] * 6 + [anywhere],
+        out_specs=(vmem, vmem, vmem, anywhere),
+        aliases={6: 3},
+    )(owner_map, row_map, inbox, embedded, scores, x_all, sums)
     exchange = lax.all_to_all(exchange, "z", 0, 0, tiled=True)
 
     chunks = var_local * TILES
@@ -395,7 +431,7 @@
             shape((patches, wide), bf16),
         ),
         mib=16,
-    )(exchange, scores, grad_attn, upstream, embedded, x_all, embed_flat, query)
+    )(exchange, both, upstream, embedded, x_turned, embed_flat, query)
 
     field_grad = kernel_call(field_kernel, shape((var_local, fields.shape[1]), f32), mib=16)(
         index_t, weight_t, grad_x
@@ -405,11 +441,11 @@
     place = lax.axis_index("z").astype(jnp.int32)
     smem = pl.BlockSpec(memory_space=pltpu.SMEM)
     rows = chunks // (2 * ring) * CHUNK
-    both = 2 * depth
+    pair = 2 * depth
     halves = lax.all_to_all(partial.reshape(2, ring, rows, LANES), "c", 0, 0, tiled=True)
     going, query_half = kernel_call(
         lambda *refs: merge_kernel(depth, capacity, *refs),
-        (shape((ring, rows + both, LANES), f32), shape((TILES // 2, LANES), f32)),
+        (shape((ring, rows + pair, LANES), f32), shape((TILES // 2, LANES), f32)),
         mib=8,
         in_specs=[smem] + [vmem] * 4,
     )(place.reshape(1), owner_map, row_map, exchange, halves)
@@ -426,7 +462,7 @@
         core == 0, jnp.stack([kept, crossed], axis=1), jnp.stack([crossed, kept], axis=1)
     ).reshape(capacity, width)
 
-    half, tokens = lax.optimization_barrier((half, tokens))
+    half, tokens, field_grad = lax.optimization_barrier((half, tokens, field_grad))
     other = lax.ppermute(half, "c", swap)
     weight_grad, bias_grad, query_grad = kernel_call(
         final_kernel,

time: 134 us -> 127 us (0.948)
  local copies, waits for them, and re-layouts: 8.56 us -> 3.52 us
  waiting for transfers between devices: 42.2 us -> 39 us
  Pallas kernels: 21.2 us -> 22.8 us
    all_to_all x1, waiting for transfers between devices: 4.33 us -> 0.01 us  [local(): half = lax.all_to_all(own, 'r', 0, 0, tiled=True)]
    reshape x2 -> x0, local copies, waits for them, and re-layouts: 3.24 us -> none  [the longest x1 2.08 us: local(): out_grad.reshape(row_devices, depth, D)]
    unnamed x25 -> x21, local copies, waits for them, and re-layouts: 4.57 us -> 2.77 us
where the time goes in v4:
time: 127 us; the launch traced here: 126 us
  starting transfers between devices  43.4 us (34%)
  waiting for transfers between devices  39 us (31%)
  Pallas kernels  22.8 us (18%)
  blocking collectives  16.6 us (13%)
  local copies, waits for them, and re-layouts  3.52 us (3%)
    all_to_all x1, waiting for transfers between devices, local(): exchange = lax.all_to_all(exchange, 'z', 0, 0, tiled=True)  22.2 us
    psum x1, blocking collectives, local(): query_half = lax.psum(query_half, 'z')  12.1 us
    all_to_all x1, starting transfers between devices, local(): lax.all_to_all(kernel_call(outbox_kernel, shape((row_devices, depth, D),...  11.6 us
    all_to_all x1, waiting for transfers between devices, local(): lax.all_to_all(kernel_call(outbox_kernel, shape((row_devices, depth, D),...  10.2 us
    all_to_all x1, starting transfers between devices, local(): exchange = lax.all_to_all(exchange, 'z', 0, 0, tiled=True)  10 us
    pallas_call x1, Pallas kernels, local(): kernel_call(forward_kernel, (shape((patches, wide), bf16), shape((var_loc...  7.19 us
    ppermute x1, starting transfers between devices, local(): other = lax.ppermute(half, 'c', swap)  6.79 us
    ppermute x1, starting transfers between devices, local(): lax.ppermute(jnp.where(core == 0, arrived[:, 1], arrived[:, 0]), 'c', swap)  5.52 us
  transfers between devices with their start and end apart: 6, of which 5 were waited for; matrix products, arithmetic and copies ran while one was open for 1% of the time, Pallas kernels for 9%

profile of v4, /device:TPU:1, one launch (start us, length us, event | category | flops | bytes accessed | tf_op | source)
XLA Modules:
  0.0 126.3 jit_solution(16984338255381981189)
XLA Ops:
  0.6 0.0 copy-start
  0.6 0.0 copy-start.1
  0.7 1.1 copy-done.1
  1.7 0.0 copy-start.9
  1.7 0.0 copy-start.8
  1.7 0.0 copy-start.2
  1.7 0.0 copy-start.3
  1.7 0.0 copy-start.6
  1.8 0.0 copy-start.7
  1.8 0.8 shard_map.119
  2.6 11.6 %all-to-all-start = ((bf16[64,4,1024]{2,1,0:T(4,128)(2,1)}), bf16[64,4,1024]{2,1,0:T(4,128)(2,1)S(1)}, u32[]{:S(2)}, u32[]{:S(2)}) async-start(bf16[64,4,1024]{2,1,0:T(4,128)(2,1)} %shard_map.119), calls=%async_computation | async-start | bytes 1048576 | tf_op jit(solution)/shard_map/all_to_all | solution.py:383
  14.2 0.0 copy-done.9
  14.2 0.1 reshape.44.query_ref
  14.3 0.0 copy-done.8
  14.3 0.1 copy.15.refs_0_.refs_1_
  14.4 0.0 copy-done
  14.4 0.0 copy-done.2
  14.4 0.0 copy-done.3
  14.5 0.0 copy-done.6
  14.5 0.0 copy-done.7
  14.5 7.2 %shard_map.120 = (bf16[128,128]{1,0:T(8,128)(2,1)S(1)}, bf16[8,128,1024]{2,1,0:T(8,128)(2,1)S(1)}, f32[128,128]{1,0:T(8,128)S(1)}, f32[8,176,128]{2,1,0:T(8,128)}) custom-call(s32[4,2048]{1,0:T(4,128)S(1)} %bitcast.26, f32[4,2048]{1,0:T(4,128)S(1)} %bitcast.28, bf16[8,4096]{1,0:T(8,128)(2,1)S(1)} %copy-done.6, bf16[128,1024]{1,0:T(8,128)(2,1)S(1)} %bitcast.23, ...), custom_call_target="tpu_custom_call" | custom-call | tf_op jit(solution)/shard_map/pallas_call | solution.py:396
  21.7 10.2 %all-to-all-done.refs_2_ = bf16[64,4,1024]{2,1,0:T(4,128)(2,1)S(1)} async-done(((bf16[64,4,1024]{2,1,0:T(4,128)(2,1)}), bf16[64,4,1024]{2,1,0:T(4,128)(2,1)S(1)}, u32[]{:S(2)}, u32[]{:S(2)}) %all-to-all-start) | async-done | bytes 524320 | tf_op jit(solution)/shard_map/all_to_all | solution.py:383
  31.9 2.8 %shard_map.121 = (bf16[128,1024]{1,0:T(8,128)(2,1)S(1)}, f32[2,128,128]{2,1,0:T(8,128)S(1)}, bf16[128,128]{1,0:T(8,128)(2,1)S(1)}, f32[8,176,128]{2,1,0:T(8,128)}) custom-call(s32[128,1]{1,0:T(8,128)S(1)} %copy.15.refs_0_.refs_1_, s32[1,128]{1,0:T(1,128)S(1)} %bitcast.30, ...), custom_call_target="tpu_custom_call", output_to_operand_aliasing={{3}: (6, {})} | custom-call | tf_op jit(solution)/shard_map/pallas_call | solution.py:410
  34.7 0.0 copy-start.4
  34.7 0.6 copy-done.4
  35.4 10.0 %all-to-all-start.1 = ((f32[8,176,128]{2,1,0:T(8,128)}), f32[8,176,128]{2,1,0:T(8,128)S(1)}, u32[]{:S(2)}, u32[]{:S(2)}) async-start(f32[8,176,128]{2,1,0:T(8,128)} %get-tuple-element.27), calls=%async_computation.1 | async-start | bytes 1441792 | tf_op jit(solution)/shard_map/all_to_all | solution.py:424
  45.4 22.2 %all-to-all-done.1.exch_ref.refs_3_ = f32[8,176,128]{2,1,0:T(8,128)S(1)} async-done(((f32[8,176,128]{2,1,0:T(8,128)}), f32[8,176,128]{2,1,0:T(8,128)S(1)}, u32[]{:S(2)}, u32[]{:S(2)}) %all-to-all-start.1) | async-done | bytes 720928 | tf_op jit(solution)/shard_map/all_to_all | solution.py:424
  67.6 0.0 copy-start.5
  67.6 0.9 copy-done.5
  68.5 4.2 %shard_map.122 = (f32[64,24,128]{2,1,0:T(8,128)S(1)}, bf16[128,128]{1,0:T(8,128)(2,1)S(1)}) custom-call(f32[8,176,128]{2,1,0:T(8,128)S(1)} %all-to-all-done.1.exch_ref.refs_3_, f32[2,128,128]{2,1,0:T(8,128)S(1)} %copy-done.5, bf16[128,1024]{1,0:T(8,128)(2,1)S(1)} %get-tuple-element.29.up_ref, bf16[8,128,1024]{2,1,0:T(8,128)(2,1)S(1)} %get-tuple-element.23.refs_3_.e_ref, ...), custom_call_target="tpu_custom_call" | custom-call | tf_op jit(solution)/shard_map/pallas_call | solution.py:427
  72.7 4.5 %all_to_all.25.refs_4_ = f32[2,32,24,128]{3,2,1,0:T(8,128)S(1)} all-to-all(f32[2,32,24,128]{3,2,1,0:T(8,128)S(1)} %bitcast.25), channel_id=1, replica_groups=mesh['r'=32,'c'=2,'z'=8] {'c'}, dimensions={0} | all-to-all | bytes 1572864 | tf_op jit(solution)/shard_map/all_to_all | solution.py:445
  77.2 1.6 %shard_map.123 = (f32[32,32,128]{2,1,0:T(8,128)}, f32[4,128]{1,0:T(4,128)S(1)}) custom-call(s32[1]{0:T(128)} %bitcast.refs_0_, s32[128,1]{1,0:T(8,128)S(1)} %copy.15.refs_0_.refs_1_, s32[1,128]{1,0:T(1,128)S(1)} %bitcast.31, f32[8,176,128]{2,1,0:T(8,128)S(1)} %all-to-all-done.1.exch_ref.refs_3_, f32[2,32,24,128]{3,2,1,0:T(8,128)S(1)} %all_to_all.25.refs_4_), custom_call_target="tpu_custom_call" | custom-call | tf_op jit(solution)/shard_map/pallas_call | solution.py:446
  78.8 4.5 %all-to-all-start.3 = ((f32[32,32,128]{2,1,0:T(8,128)}), f32[32,32,128]{2,1,0:T(8,128)S(1)}, u32[]{:S(2)}, u32[]{:S(2)}) async-start(f32[32,32,128]{2,1,0:T(8,128)} %get-tuple-element.32), calls=%async_computation.3 | async-start | bytes 1048576 | tf_op jit(solution)/shard_map/all_to_all | solution.py:452
  83.3 12.1 %psum.7.query_ref = f32[4,128]{1,0:T(4,128)S(1)} all-reduce(f32[4,128]{1,0:T(4,128)S(1)} %get-tuple-element.33), channel_id=1, replica_groups=mesh['r'=32,'c'=2,'z'=8] {'z'}, use_global_device_ids=true, to_apply=%region_0.0 | all-reduce | flops 512 | bytes 4096 | tf_op jit(solution)/shard_map/psum | solution.py:453
  95.4 4.5 %all-to-all-done.3.coming_ref = f32[32,32,128]{2,1,0:T(8,128)S(1)} async-done(((f32[32,32,128]{2,1,0:T(8,128)}), f32[32,32,128]{2,1,0:T(8,128)S(1)}, u32[]{:S(2)}, u32[]{:S(2)}) %all-to-all-start.3) | async-done | bytes 524320 | tf_op jit(solution)/shard_map/all_to_all | solution.py:452
  99.9 0.8 shard_map.124
  100.7 4.9 %all-to-all-start.4 = ((f32[32,24,128]{2,1,0:T(8,128)}), f32[32,24,128]{2,1,0:T(8,128)S(1)}, u32[]{:S(2)}, u32[]{:S(2)}) async-start(f32[32,24,128]{2,1,0:T(8,128)} %shard_map.124), calls=%async_computation.4 | async-start | bytes 786432 | tf_op jit(solution)/shard_map/all_to_all | solution.py:455
  105.7 4.5 %shard_map.125 = f32[8,4096]{1,0:T(8,128)} custom-call(s32[4,2048]{1,0:T(4,128)S(1)} %bitcast.27, f32[4,2048]{1,0:T(4,128)S(1)} %bitcast.29, bf16[128,128]{1,0:T(8,128)(2,1)S(1)} %get-tuple-element.34.gx_ref), custom_call_target="tpu_custom_call" | custom-call | tf_op jit(solution)/shard_map/pallas_call | solution.py:436
  110.2 5.5 %collective-permute-start = (bf16[32,4,128]{2,1,0:T(4,128)(2,1)S(1)}, bf16[32,4,128]{2,1,0:T(4,128)(2,1)S(1)}, u32[]{:S(2)}, u32[]{:S(2)}) collective-permute-start(bf16[32,4,128]{2,1,0:T(4,128)(2,1)S(1)} %fusion), channel_id=1, source_target_pairs={{0,8},{8,0},{1,9},{9,1},{2,10},{10,2},{3,11},{11,3},{4,12},{12,4},... | collective-permute-start | bytes 98312 | tf_op jit(solution)/shard_map/ppermute | solution.py:459
  115.8 0.8 collective-permute-done
  116.6 0.1 maximum_select_fusion
  116.6 0.7 copy.20
  117.3 0.0 all-to-all-done.4.half_ref
  117.3 6.8 %collective-permute-start.1 = (f32[32,24,128]{2,1,0:T(8,128)S(1)}, f32[32,24,128]{2,1,0:T(8,128)S(1)}, u32[]{:S(2)}, u32[]{:S(2)}) collective-permute-start(f32[32,24,128]{2,1,0:T(8,128)S(1)} %all-to-all-done.4.half_ref), channel_id=1, source_target_pairs={{0,8},{8,0},{1,9},{9,1},{2,10},{10,2},{3,11},{11,3},{4,12},{12,4},... | collective-permute-start | bytes 1179656 | tf_op jit(solution)/shard_map/ppermute | solution.py:466
  124.1 1.3 %collective-permute-done.1.other_ref = f32[32,24,128]{2,1,0:T(8,128)S(1)} collective-permute-done((f32[32,24,128]{2,1,0:T(8,128)S(1)}, f32[32,24,128]{2,1,0:T(8,128)S(1)}, u32[]{:S(2)}, u32[]{:S(2)}) %collective-permute-start.1) | collective-permute-done | bytes 393248 | tf_op jit(solution)/shard_map/ppermute | solution.py:466
  125.4 0.9 shard_map.126
  (3 shorter events, 0.1 us)
Async XLA Ops:
  0.6 13.8 %copy-start = (bf16[8,16,1024]{2,1,0:T(8,128)(2,1)S(1)}, bf16[8,16,1024]{2,1,0:T(8,128)(2,1)}, u32[]{:S(2)}) copy-start(bf16[8,16,1024]{2,1,0:T(8,128)(2,1)} %param.12) | copy-start | bytes 786436
  0.6 1.1 copy-start.1
  1.7 12.5 %copy-start.9 = (f32[16,64]{1,0:T(8,128)S(1)}, f32[16,64]{1,0:T(8,128)}, u32[]{:S(2)}) copy-start(f32[16,64]{1,0:T(8,128)} %param.14) | copy-start | bytes 12292
  1.7 12.6 %copy-start.8 = (s32[128,1]{0,1:T(1,128)S(1)}, s32[128,1]{0,1:T(1,128)}, u32[]{:S(2)}) copy-start(s32[128,1]{0,1:T(1,128)} %param.11) | copy-start | bytes 1540
  1.7 12.7 %copy-start.2 = (s32[2048,4]{0,1:T(4,128)S(1)}, s32[2048,4]{0,1:T(4,128)}, u32[]{:S(2)}) copy-start(s32[2048,4]{0,1:T(4,128)} %param.9) | copy-start | bytes 98308
  1.7 12.7 %copy-start.3 = (f32[2048,4]{0,1:T(4,128)S(1)}, f32[2048,4]{0,1:T(4,128)}, u32[]{:S(2)}) copy-start(f32[2048,4]{0,1:T(4,128)} %param.10) | copy-start | bytes 98308
  1.7 12.7 %copy-start.6 = (bf16[8,4096]{1,0:T(8,128)(2,1)S(1)}, bf16[8,4096]{1,0:T(8,128)(2,1)}, u32[]{:S(2)}) copy-start(bf16[8,4096]{1,0:T(8,128)(2,1)} %fields_ref.1) | copy-start | bytes 196612
  1.8 12.7 %copy-start.7 = (bf16[8,1024]{1,0:T(8,128)(2,1)S(1)}, bf16[8,1024]{1,0:T(8,128)(2,1)}, u32[]{:S(2)}) copy-start(bf16[8,1024]{1,0:T(8,128)(2,1)} %bias_ref.1) | copy-start | bytes 49156
  2.6 29.3 %all-to-all-start = ((bf16[64,4,1024]{2,1,0:T(4,128)(2,1)}), bf16[64,4,1024]{2,1,0:T(4,128)(2,1)S(1)}, u32[]{:S(2)}, u32[]{:S(2)}) async-start(bf16[64,4,1024]{2,1,0:T(4,128)(2,1)} %shard_map.119), calls=%async_computation | async-start | bytes 1048576 | tf_op jit(solution)/shard_map/all_to_all | solution.py:383
  34.7 0.7 copy-start.4
  35.4 32.2 %all-to-all-start.1 = ((f32[8,176,128]{2,1,0:T(8,128)}), f32[8,176,128]{2,1,0:T(8,128)S(1)}, u32[]{:S(2)}, u32[]{:S(2)}) async-start(f32[8,176,128]{2,1,0:T(8,128)} %get-tuple-element.27), calls=%async_computation.1 | async-start | bytes 1441792 | tf_op jit(solution)/shard_map/all_to_all | solution.py:424
  67.6 0.9 copy-start.5
  78.8 21.1 %all-to-all-start.3 = ((f32[32,32,128]{2,1,0:T(8,128)}), f32[32,32,128]{2,1,0:T(8,128)S(1)}, u32[]{:S(2)}, u32[]{:S(2)}) async-start(f32[32,32,128]{2,1,0:T(8,128)} %get-tuple-element.32), calls=%async_computation.3 | async-start | bytes 1048576 | tf_op jit(solution)/shard_map/all_to_all | solution.py:452
  100.7 16.6 %all-to-all-start.4 = ((f32[32,24,128]{2,1,0:T(8,128)}), f32[32,24,128]{2,1,0:T(8,128)S(1)}, u32[]{:S(2)}, u32[]{:S(2)}) async-start(f32[32,24,128]{2,1,0:T(8,128)} %shard_map.124), calls=%async_computation.4 | async-start | bytes 786432 | tf_op jit(solution)/shard_map/all_to_all | solution.py:455
  110.2 6.4 %collective-permute-start = (bf16[32,4,128]{2,1,0:T(4,128)(2,1)S(1)}, bf16[32,4,128]{2,1,0:T(4,128)(2,1)S(1)}, u32[]{:S(2)}, u32[]{:S(2)}) collective-permute-start(bf16[32,4,128]{2,1,0:T(4,128)(2,1)S(1)} %fusion), channel_id=1, source_target_pairs={{0,8},{8,0},{1,9},{9,1},{2,10},{10,2},{3,11},{11,3},{4,12},{12,4},... | collective-permute-start | bytes 98312 | tf_op jit(solution)/shard_map/ppermute | solution.py:459
  117.3 8.1 %collective-permute-start.1 = (f32[32,24,128]{2,1,0:T(8,128)S(1)}, f32[32,24,128]{2,1,0:T(8,128)S(1)}, u32[]{:S(2)}, u32[]{:S(2)}) collective-permute-start(f32[32,24,128]{2,1,0:T(8,128)S(1)} %all-to-all-done.4.half_ref), channel_id=1, source_target_pairs={{0,8},{8,0},{1,9},{9,1},{2,10},{10,2},{3,11},{11,3},{4,12},{12,4},... | collective-permute-start | bytes 1179656 | tf_op jit(solution)/shard_map/ppermute | solution.py:466

commit v5 on v4

--- a/solution.py
+++ b/solution.py
@@ -105,7 +105,7 @@
 
 
 def forward_kernel(
-    index_ref, weight_ref, fields_ref, embed_ref, bias_ref, query_ref, x_ref, e_ref, s_ref, exch_ref, sum_ref
+    index_ref, weight_ref, fields_ref, embed_ref, bias_ref, query_ref, x_ref, e_ref, s_ref, exch_ref, matrix_ref, sum_ref
 ):
     var_local = fields_ref.shape[0]
     blocks = fields_ref.shape[1] // PTS_BLK
@@ -114,6 +114,7 @@
     gather = spread(PB, PIX_BLK, lambda r, c: r == c // P_SIZE)
     for block in range(blocks):
         matrix = interp_transposed(index_ref, weight_ref, block)
+        matrix_ref[block] = matrix
         pixels = dot(fields_ref[:, pl.ds(block * PTS_BLK, PTS_BLK)], matrix).astype(bf16)
         widened = jnp.where(own_pixel, dot(copy_rows, pixels), 0.0).astype(bf16)
         x_ref[pl.ds(block * PB, PB), :] = dot_t(gather, widened).astype(bf16)
@@ -135,7 +136,8 @@
         scores.append(three[:, :H] + three[:, H : 2 * H] + three[:, 2 * H :])
     scores = jnp.concatenate(scores, axis=1) * (1.0 / math.sqrt(DH))
     s_ref[...] = scores
-    weights = split(jnp.exp(scores - over_vars(scores, jnp.maximum)), 2)
+    weights = jnp.exp(scores - over_vars(scores, jnp.maximum))
+    weights = split(weights / over_vars(weights, jnp.add), 2)
     expand = head_expand(2)
     for v in range(var_local):
         both = jnp.concatenate([group(part, v) for part in weights], axis=1)
@@ -203,14 +205,14 @@
     peak = over_vars(scores, jnp.maximum)
     weights = jnp.exp(scores - peak)
     total = over_vars(weights, jnp.add)
-    inner = over_vars(weights * grad_attn, jnp.add)
-    packed = [group(peak, 0), group(total, 0), group(inner, 0)]
-    packed = jnp.concatenate(packed + [jnp.zeros((patches, LANES - 3 * H), f32)], axis=1)
+    inner = over_vars(weights * grad_attn, jnp.add) / total
+    packed = [group(peak + jnp.log(total), 0), group(inner, 0)]
+    packed = jnp.concatenate(packed + [jnp.zeros((patches, LANES - 2 * H), f32)], axis=1)
     if patches < LANES:
         packed = jnp.concatenate([packed, jnp.zeros((LANES - patches, LANES), f32)], axis=0)
-    stats_ref[...] = packed.T[: 3 * H, :]
+    stats_ref[...] = packed.T[: 2 * H, :]
     copies = [
-        pltpu.make_async_copy(stats_ref, exch_ref.at[g, pl.ds(patches, 3 * H)], sems.at[g])
+        pltpu.make_async_copy(stats_ref, exch_ref.at[g, pl.ds(patches, 2 * H)], sems.at[g])
         for g in range(exch_ref.shape[0])
     ]
     for copy in copies:
@@ -221,28 +223,27 @@
 
 def combine_stats(exch_ref, patches):
     groups = exch_ref.shape[0]
-    peaks, totals, inners = [], [], []
+    logs, inners = [], []
     for g in range(groups):
-        stats = exch_ref[g, patches : patches + 3 * H, :]
-        rows = jnp.concatenate([stats, jnp.zeros((LANES - 3 * H, LANES), f32)], axis=0).T
+        stats = exch_ref[g, patches : patches + 2 * H, :]
+        rows = jnp.concatenate([stats, jnp.zeros((LANES - 2 * H, LANES), f32)], axis=0).T
         rows = rows[:patches]
-        peaks.append(rows[:, :H])
-        totals.append(rows[:, H : 2 * H])
-        inners.append(rows[:, 2 * H : 3 * H])
-    peak = peaks[0]
-    for other in peaks[1:]:
+        logs.append(rows[:, :H])
+        inners.append(rows[:, H : 2 * H])
+    peak = logs[0]
+    for other in logs[1:]:
         peak = jnp.maximum(peak, other)
-    factors = [jnp.exp(one - peak) for one in peaks]
-    total = sum(f * t for f, t in zip(factors, totals))
-    inner = sum(f * t for f, t in zip(factors, inners)) / total
-    return peak, total, inner, factors
-
-
-def merge_kernel(depth, slots, place_ref, column_ref, row_ref, exch_ref, halves_ref, going_ref, query_ref):
+    factors = [jnp.exp(one - peak) for one in logs]
+    total = sum(factors)
+    shares = [factor / total for factor in factors]
+    inner = sum(f * t for f, t in zip(shares, inners))
+    return peak, total, inner, shares
+
+
+def tokens_kernel(depth, slots, place_ref, column_ref, row_ref, exch_ref, out_ref):
     patches = column_ref.shape[0]
     groups, _, width = exch_ref.shape
-    ring, rows = halves_ref.shape[1], halves_ref.shape[2]
-    _, total, _, factors = combine_stats(exch_ref, patches)
+    _, _, _, shares = combine_stats(exch_ref, patches)
     heads = width // DH
     first = place_ref[0] * heads
     pick = jnp.where(
@@ -250,13 +251,17 @@
     ).astype(bf16)
     mixture = jnp.zeros((patches, width), f32)
     for g in range(groups):
-        scale = jnp.concatenate(split(factors[g] / total, 3), axis=1)
+        scale = jnp.concatenate(split(shares[g], 3), axis=1)
         mixture = mixture + dot(scale, pick) * exch_ref[g, :patches, :]
     target = target_of(column_ref, row_ref, depth, True)
     place = jnp.where(iota((slots, patches), 0) == target, 1.0, 0.0).astype(bf16)
-    tokens = dot(place, mixture.astype(bf16))
-    going_ref[:, rows:, :] = tokens.reshape(ring, slots // ring, width)
-    going_ref[:, :rows, :] = halves_ref[0] + halves_ref[1]
+    out_ref[...] = dot(place, mixture.astype(bf16))
+
+
+def merge_kernel(kept_ref, crossed_ref, tokens_ref, going_ref, query_ref):
+    ring, rows = kept_ref.shape[0], kept_ref.shape[1]
+    going_ref[:, rows:, :] = tokens_ref[...].reshape(ring, tokens_ref.shape[0] // ring, LANES)
+    going_ref[:, :rows, :] = kept_ref[...] + crossed_ref[...]
     share = rows // CHUNK
     for t in range(TILES // 2):
         at = (t % share) * CHUNK + P_SIZE + 1
@@ -299,10 +304,10 @@
 
 
 def backward_kernel(
-    exch_ref, both_ref, up_ref, e_ref, xt_ref, embed_ref, query_ref, wide_ref, gx_ref
+    core_ref, exch_ref, both_ref, up_ref, xt_ref, embed_ref, bias_ref, query_ref, kept_ref, send_ref, gx_ref, wide_ref
 ):
-    var_local, patches = e_ref.shape[0], e_ref.shape[1]
-    wide = var_local * P_SIZE
+    wide, patches = xt_ref.shape
+    var_local = wide // P_SIZE
     peak, total, inner, _ = combine_stats(exch_ref, patches)
     peak, inner, inverse = (
         jnp.concatenate([one] * var_local, axis=1) for one in (peak, inner, 1.0 / total)
@@ -321,6 +326,7 @@
     query_rows = jnp.where(on_head, query_rows, 0.0).astype(bf16)
     upstream = up_ref[...].astype(f32)
     x_t = xt_ref[...]
+    x_all = x_t.astype(f32).T.astype(bf16)
     embed_t = embed_ref[...].astype(f32).T.astype(bf16)
     lane_var = iota((patches, wide), 1) // P_SIZE
     grad_x = jnp.zeros((patches, wide), f32)
@@ -339,7 +345,9 @@
             wide_ref[v * TILES + t, P_SIZE : P_SIZE + 1, :] = bias_row[:, cut]
         grad_x = jnp.where(lane_var == v, dot(low_grad, embed_t), grad_x)
         pair = jnp.concatenate([part[v * H : (v + 1) * H] for part in turned], axis=0)
-        query_sum = query_sum + dot(pair, e_ref[v])
+        own = jnp.where(lane_var == v, x_all, jnp.zeros_like(x_all))
+        embedded = (dot(own, embed_ref[...]) + bias_ref[v : v + 1, :].astype(f32)).astype(bf16)
+        query_sum = query_sum + dot(pair, embedded)
     gx_ref[...] = grad_x.astype(bf16)
     diagonal = iota((2 * H, D), 0) % H == iota((2 * H, D), 1) // DH
     query_row = jnp.sum(jnp.where(diagonal, query_sum, 0.0), axis=0, keepdims=True)
@@ -347,9 +355,12 @@
     for t in range(TILES):
         at = (t // (TILES // 2)) * half + t % (TILES // 2)
         wide_ref[at, P_SIZE + 1 : P_SIZE + 2, :] = query_row[:, t * LANES : (t + 1) * LANES]
-
-
-def field_kernel(index_ref, weight_ref, gx_ref, out_ref):
+    core = core_ref[0]
+    kept_ref[...] = wide_ref[pl.ds(core * half, half)].reshape(kept_ref.shape)
+    send_ref[...] = wide_ref[pl.ds((1 - core) * half, half)].reshape(send_ref.shape)
+
+
+def field_kernel(matrix_ref, gx_ref, out_ref):
     wide = gx_ref.shape[1]
     var_local = wide // P_SIZE
     blocks = gx_ref.shape[0] // PB
@@ -361,8 +372,7 @@
         wide_grad = dot(gx_t[:, block * PB : (block + 1) * PB], copy)
         wide_grad = jnp.where(own_pixel, wide_grad, 0.0).astype(bf16)
         grad = dot(fold, wide_grad).astype(bf16)
-        matrix = interp_transposed(index_ref, weight_ref, block)
-        out_ref[:, pl.ds(block * PTS_BLK, PTS_BLK)] = dot_t(grad, matrix)
+        out_ref[:, pl.ds(block * PTS_BLK, PTS_BLK)] = dot_t(grad, matrix_ref[block])
 
 
 def local(
@@ -393,13 +403,14 @@
     embed_flat = embed_weight.reshape(wide, D)
     query = agg_query.reshape(1, D)
     row_map = owner_map.reshape(1, patches)
-    x_all, embedded, scores, sums = kernel_call(
+    x_all, embedded, scores, sums, matrix = kernel_call(
         forward_kernel,
         (
             shape((patches, wide), bf16),
             shape((var_local, patches, D), bf16),
             shape((patches, var_local * H), f32),
-            shape((groups, patches + 3 * H, width), f32),
+            shape((groups, patches + 2 * H, width), f32),
+            shape((fields.shape[1] // PTS_BLK, PTS_BLK, PIX_BLK), bf16),
         ),
         mib=20,
         scratch=[pltpu.VMEM((patches, D), f32)],
@@ -416,46 +427,55 @@
             shape(sums.shape, f32),
         ),
         mib=12,
-        scratch=[pltpu.VMEM((3 * H, LANES), f32), pltpu.SemaphoreType.DMA((groups,))],
+        scratch=[pltpu.VMEM((2 * H, LANES), f32), pltpu.SemaphoreType.DMA((groups,))],
         in_specs=[vmem] * 6 + [anywhere],
         out_specs=(vmem, vmem, vmem, anywhere),
         aliases={6: 3},
     )(owner_map, row_map, inbox, embedded, scores, x_all, sums)
     exchange = lax.all_to_all(exchange, "z", 0, 0, tiled=True)
 
+    core = lax.axis_index("c").astype(jnp.int32)
+    place = lax.axis_index("z").astype(jnp.int32)
+    smem = pl.BlockSpec(memory_space=pltpu.SMEM)
+    swap = [(0, 1), (1, 0)]
     chunks = var_local * TILES
-    partial, grad_x = kernel_call(
+    rows = chunks // (2 * ring) * CHUNK
+    pair = 2 * depth
+    kept, sent, grad_x = kernel_call(
         backward_kernel,
         (
-            shape((chunks, CHUNK, LANES), f32),
+            shape((ring, rows, LANES), f32),
+            shape((ring, rows, LANES), f32),
             shape((patches, wide), bf16),
         ),
         mib=16,
-    )(exchange, both, upstream, embedded, x_turned, embed_flat, query)
-
-    field_grad = kernel_call(field_kernel, shape((var_local, fields.shape[1]), f32), mib=16)(
-        index_t, weight_t, grad_x
-    )
-
-    core = lax.axis_index("c").astype(jnp.int32)
-    place = lax.axis_index("z").astype(jnp.int32)
-    smem = pl.BlockSpec(memory_space=pltpu.SMEM)
-    rows = chunks // (2 * ring) * CHUNK
-    pair = 2 * depth
-    halves = lax.all_to_all(partial.reshape(2, ring, rows, LANES), "c", 0, 0, tiled=True)
+        scratch=[pltpu.VMEM((chunks, CHUNK, LANES), f32)],
+        in_specs=[smem] + [vmem] * 7,
+    )(core.reshape(1), exchange, both, upstream, x_turned, embed_flat, embed_bias, query)
+    crossed = lax.ppermute(sent, "c", swap)
+    outbox = kernel_call(
+        lambda *refs: tokens_kernel(depth, capacity, *refs),
+        shape((capacity, width), f32),
+        mib=8,
+        in_specs=[smem] + [vmem] * 3,
+    )(place.reshape(1), owner_map, row_map, exchange)
+    crossed, outbox = lax.optimization_barrier((crossed, outbox))
     going, query_half = kernel_call(
-        lambda *refs: merge_kernel(depth, capacity, *refs),
+        merge_kernel,
         (shape((ring, rows + pair, LANES), f32), shape((TILES // 2, LANES), f32)),
         mib=8,
-        in_specs=[smem] + [vmem] * 4,
-    )(place.reshape(1), owner_map, row_map, exchange, halves)
+    )(kept, crossed, outbox)
+
+    field_grad = kernel_call(field_kernel, shape((var_local, fields.shape[1]), f32), mib=16)(
+        matrix, grad_x
+    )
+
     coming = lax.all_to_all(going, "r", 0, 0, tiled=True)
     query_half = lax.psum(query_half, "z")
     own = kernel_call(own_kernel, shape((ring, rows, LANES), f32), mib=8)(coming, query_half)
     half = lax.all_to_all(own, "r", 0, 0, tiled=True)
 
     arrived = coming[:, rows:].astype(bf16).reshape(ring, 2, depth, width)
-    swap = [(0, 1), (1, 0)]
     crossed = lax.ppermute(jnp.where(core == 0, arrived[:, 1], arrived[:, 0]), "c", swap)
     kept = jnp.where(core == 0, arrived[:, 0], arrived[:, 1])
     tokens = jnp.where(

time: 127 us -> 127 us (level)
  local copies, waits for them, and re-layouts: 3.52 us -> 12.1 us
  waiting for transfers between devices: 39 us -> 30.7 us
  blocking collectives: 16.6 us -> 12.1 us
  starting transfers between devices: 43.4 us -> 47.6 us
    unnamed x21 -> x25, local copies, waits for them, and re-layouts: 2.77 us -> 10.6 us
    all_to_all x1, waiting for transfers between devices: 10.2 us -> 2.72 us  [local(): lax.all_to_all(kernel_call(outbox_kernel, shape((row_devices, depth, D),...]
    all_to_all x1 -> x0, blocking collectives: 4.49 us -> none  [local(): lax.all_to_all(partial.reshape(2, ring, rows, LANES), 'c', 0, 0, tiled=True)]
    ppermute x0 -> x1, starting transfers between devices: none -> 2.39 us  [local(): crossed = lax.ppermute(sent, 'c', swap)]
    all_to_all x1, starting transfers between devices: 4.49 us -> 6.74 us  [local(): coming = lax.all_to_all(going, 'r', 0, 0, tiled=True)]
    pallas_call x1, Pallas kernels: 4.51 us -> 2.76 us  [local(): kernel_call(field_kernel, shape((var_local, fields.shape[1]), f32), mib=16)]
    all_to_all x1, waiting for transfers between devices: 22.2 us -> 20.8 us  [local(): exchange = lax.all_to_all(exchange, 'z', 0, 0, tiled=True)]
    pallas_call x2 -> x3, Pallas kernels: 5.79 us -> 7.09 us  [the longest x1 5.5 us: local(): kernel_call(backward_kernel, (shape((ring, rows, LANES), f32), shape((rin...]
  transfers between devices with their start and end apart: 6 -> 7, of which waited for: 5 -> 6; matrix products, arithmetic and copies ran while one was open for 1% -> 2% of each run, Pallas kernels for 9% -> 9%
where the time goes in v5:
time: 127 us; the launch traced here: 126 us
  starting transfers between devices  47.6 us (37%)
  waiting for transfers between devices  30.7 us (24%)
  Pallas kernels  22.6 us (18%)
  local copies, waits for them, and re-layouts  12.1 us (10%)
  blocking collectives  12.1 us (10%)
    all_to_all x1, waiting for transfers between devices, local(): exchange = lax.all_to_all(exchange, 'z', 0, 0, tiled=True)  20.8 us
    psum x1, blocking collectives, local(): query_half = lax.psum(query_half, 'z')  12.1 us
    all_to_all x1, starting transfers between devices, local(): lax.all_to_all(kernel_call(outbox_kernel, shape((row_devices, depth, D),...  11.6 us
    unnamed x25, local copies, waits for them, and re-layouts  10.6 us
    all_to_all x1, starting transfers between devices, local(): exchange = lax.all_to_all(exchange, 'z', 0, 0, tiled=True)  10 us
    pallas_call x1, Pallas kernels, local(): kernel_call(forward_kernel, (shape((patches, wide), bf16), shape((var_loc...  7.46 us
    all_to_all x1, starting transfers between devices, local(): coming = lax.all_to_all(going, 'r', 0, 0, tiled=True)  6.74 us
    ppermute x1, starting transfers between devices, local(): other = lax.ppermute(half, 'c', swap)  6.32 us
  transfers between devices with their start and end apart: 7, of which 6 were waited for; matrix products, arithmetic and copies ran while one was open for 2% of the time, Pallas kernels for 9%

profile of v5, /device:TPU:1, one launch (start us, length us, event | category | flops | bytes accessed | tf_op | source)
XLA Modules:
  0.0 126.0 jit_solution(13974818065652363904)
XLA Ops:
  0.6 0.0 copy-start.3
  0.6 0.0 copy-start.4
  0.7 1.1 copy-done.4
  1.7 0.0 copy-start.6
  1.7 0.0 copy-start.11
  1.7 0.8 shard_map.119
  2.6 11.6 %all-to-all-start = ((bf16[64,4,1024]{2,1,0:T(4,128)(2,1)}), bf16[64,4,1024]{2,1,0:T(4,128)(2,1)S(1)}, u32[]{:S(2)}, u32[]{:S(2)}) async-start(bf16[64,4,1024]{2,1,0:T(4,128)(2,1)} %shard_map.119), calls=%async_computation | async-start | bytes 1048576 | tf_op jit(solution)/shard_map/all_to_all | solution.py:393
  14.2 0.8 reshape.42.query_ref
  15.0 0.8 copy.14.refs_0_.refs_1_
  15.7 0.0 copy-start.2
  15.7 0.9 copy-done.2
  16.7 0.0 copy-start.5
  16.7 0.7 copy-done.5
  17.4 0.0 copy-start.7
  17.4 0.8 copy-done.7
  18.2 0.8 copy-done.8
  19.0 0.8 copy-done.9
  19.8 7.5 %shard_map.120 = (bf16[128,128]{1,0:T(8,128)(2,1)S(1)}, bf16[8,128,1024]{2,1,0:T(8,128)(2,1)S(1)}, f32[128,128]{1,0:T(8,128)S(1)}, f32[8,160,128]{2,1,0:T(8,128)}, bf16[4,1024,512]{2,1,0:T(8,128)(2,1)S(1)}) custom-call(s32[4,2048]{1,0:T(4,128)S(1)} %bitcast.24, f32[4,2048]{1,0:T(4,128)S(1)} %bitcast.25, bf16[8,4096]{1,0:T(8,128)(2,1)S(1)} %copy-done.7, ...), custom_call_target="tpu_custom_call" | custom-call | tf_op jit(solution)/shard_map/pallas_call | solution.py:406
  27.2 1.9 %copy-done = bf16[4,1024,512]{2,1,0:T(8,128)(2,1)} copy-done((bf16[4,1024,512]{2,1,0:T(8,128)(2,1)}, bf16[4,1024,512]{2,1,0:T(8,128)(2,1)S(1)}, u32[]{:S(2)}) %copy-start) | copy-done | bytes 4194328
  29.2 2.7 %all-to-all-done.refs_2_ = bf16[64,4,1024]{2,1,0:T(4,128)(2,1)S(1)} async-done(((bf16[64,4,1024]{2,1,0:T(4,128)(2,1)}), bf16[64,4,1024]{2,1,0:T(4,128)(2,1)S(1)}, u32[]{:S(2)}, u32[]{:S(2)}) %all-to-all-start) | async-done | bytes 524320 | tf_op jit(solution)/shard_map/all_to_all | solution.py:393
  31.9 0.7 copy-done.10
  32.5 2.8 %shard_map.121 = (bf16[128,1024]{1,0:T(8,128)(2,1)S(1)}, f32[2,128,128]{2,1,0:T(8,128)S(1)}, bf16[128,128]{1,0:T(8,128)(2,1)S(1)}, f32[8,160,128]{2,1,0:T(8,128)}) custom-call(s32[128,1]{1,0:T(8,128)S(1)} %copy.14.refs_0_.refs_1_, s32[1,128]{1,0:T(1,128)S(1)} %bitcast.26, ...), custom_call_target="tpu_custom_call", output_to_operand_aliasing={{3}: (6, {})} | custom-call | tf_op jit(solution)/shard_map/pallas_call | solution.py:421
  35.4 10.0 %all-to-all-start.1 = ((f32[8,160,128]{2,1,0:T(8,128)}), f32[8,160,128]{2,1,0:T(8,128)S(1)}, u32[]{:S(2)}, u32[]{:S(2)}) async-start(f32[8,160,128]{2,1,0:T(8,128)} %get-tuple-element.31), calls=%async_computation.1 | async-start | bytes 1310720 | tf_op jit(solution)/shard_map/all_to_all | solution.py:435
  45.4 20.8 %all-to-all-done.1.exch_ref.refs_3_ = f32[8,160,128]{2,1,0:T(8,128)S(1)} async-done(((f32[8,160,128]{2,1,0:T(8,128)}), f32[8,160,128]{2,1,0:T(8,128)S(1)}, u32[]{:S(2)}, u32[]{:S(2)}) %all-to-all-start.1) | async-done | bytes 655392 | tf_op jit(solution)/shard_map/all_to_all | solution.py:435
  66.2 0.0 copy-done.3
  66.2 0.0 copy-done.6
  66.2 5.5 %shard_map.122 = (f32[32,24,128]{2,1,0:T(8,128)S(1)}, f32[32,24,128]{2,1,0:T(8,128)S(1)}, bf16[128,128]{1,0:T(8,128)(2,1)S(1)}) custom-call(s32[1]{0:T(128)} %bitcast.core_ref, f32[8,160,128]{2,1,0:T(8,128)S(1)} %all-to-all-done.1.exch_ref.refs_3_, f32[2,128,128]{2,1,0:T(8,128)S(1)} %get-tuple-element.32.both_ref, ...), custom_call_target="tpu_custom_call" | custom-call | tf_op jit(solution)/shard_map/pallas_call | solution.py:444
  71.7 2.4 %collective-permute-start = (f32[32,24,128]{2,1,0:T(8,128)S(1)}, f32[32,24,128]{2,1,0:T(8,128)S(1)}, u32[]{:S(2)}, u32[]{:S(2)}) collective-permute-start(f32[32,24,128]{2,1,0:T(8,128)S(1)} %get-tuple-element.36), channel_id=1, source_target_pairs={{0,8},{8,0},{1,9},{9,1},{2,10},{10,2},{3,11},{11,3},{4,12},{12,4},... | collective-permute-start | bytes 1179656 | tf_op jit(solution)/shard_map/ppermute | solution.py:455
  74.1 0.0 copy-done.11
  74.1 0.7 shard_map.123.tokens_ref
  74.8 0.6 collective-permute-done.crossed_ref
  75.4 0.9 shard_map.124
  76.3 6.7 %all-to-all-start.2 = ((f32[32,32,128]{2,1,0:T(8,128)}), f32[32,32,128]{2,1,0:T(8,128)S(1)}, u32[]{:S(2)}, u32[]{:S(2)}) async-start(f32[32,32,128]{2,1,0:T(8,128)} %get-tuple-element.39), calls=%async_computation.2 | async-start | bytes 1048576 | tf_op jit(solution)/shard_map/all_to_all | solution.py:473
  83.0 12.1 %psum.7.query_ref = f32[4,128]{1,0:T(4,128)S(1)} all-reduce(f32[4,128]{1,0:T(4,128)S(1)} %get-tuple-element.40), channel_id=1, replica_groups=mesh['r'=32,'c'=2,'z'=8] {'z'}, use_global_device_ids=true, to_apply=%region_0.0 | all-reduce | flops 512 | bytes 4096 | tf_op jit(solution)/shard_map/psum | solution.py:474
  95.1 4.5 %all-to-all-done.2.coming_ref = f32[32,32,128]{2,1,0:T(8,128)S(1)} async-done(((f32[32,32,128]{2,1,0:T(8,128)}), f32[32,32,128]{2,1,0:T(8,128)S(1)}, u32[]{:S(2)}, u32[]{:S(2)}) %all-to-all-start.2) | async-done | bytes 524320 | tf_op jit(solution)/shard_map/all_to_all | solution.py:473
  99.6 0.8 shard_map.125
  100.4 4.9 %all-to-all-start.3 = ((f32[32,24,128]{2,1,0:T(8,128)}), f32[32,24,128]{2,1,0:T(8,128)S(1)}, u32[]{:S(2)}, u32[]{:S(2)}) async-start(f32[32,24,128]{2,1,0:T(8,128)} %shard_map.125), calls=%async_computation.3 | async-start | bytes 786432 | tf_op jit(solution)/shard_map/all_to_all | solution.py:476
  105.4 0.0 copy-start.1
  105.4 2.2 %copy-done.1 = bf16[4,1024,512]{2,1,0:T(8,128)(2,1)S(1)} copy-done((bf16[4,1024,512]{2,1,0:T(8,128)(2,1)S(1)}, bf16[4,1024,512]{2,1,0:T(8,128)(2,1)}, u32[]{:S(2)}) %copy-start.1) | copy-done | bytes 4194328
  107.6 2.8 %shard_map.126 = f32[8,4096]{1,0:T(8,128)} custom-call(bf16[4,1024,512]{2,1,0:T(8,128)(2,1)S(1)} %copy-done.1, bf16[128,128]{1,0:T(8,128)(2,1)S(1)} %get-tuple-element.42.gx_ref), custom_call_target="tpu_custom_call" | custom-call | tf_op jit(solution)/shard_map/pallas_call | solution.py:469
  110.4 5.5 %collective-permute-start.1 = (bf16[32,4,128]{2,1,0:T(4,128)(2,1)S(1)}, bf16[32,4,128]{2,1,0:T(4,128)(2,1)S(1)}, u32[]{:S(2)}, u32[]{:S(2)}) collective-permute-start(bf16[32,4,128]{2,1,0:T(4,128)(2,1)S(1)} %fusion), channel_id=1, source_target_pairs={{0,8},{8,0},{1,9},{9,1},{2,10},{10,2},{3,11},{11,3},{4,12},{12,4},... | collective-permute-start | bytes 98312 | tf_op jit(solution)/shard_map/ppermute | solution.py:479
  115.9 0.8 collective-permute-done.1
  116.8 0.1 maximum_select_fusion
  116.8 0.7 copy.20
  117.5 0.0 all-to-all-done.3.half_ref
  117.5 6.3 %collective-permute-start.2 = (f32[32,24,128]{2,1,0:T(8,128)S(1)}, f32[32,24,128]{2,1,0:T(8,128)S(1)}, u32[]{:S(2)}, u32[]{:S(2)}) collective-permute-start(f32[32,24,128]{2,1,0:T(8,128)S(1)} %all-to-all-done.3.half_ref), channel_id=1, source_target_pairs={{0,8},{8,0},{1,9},{9,1},{2,10},{10,2},{3,11},{11,3},{4,12},{12,4},... | collective-permute-start | bytes 1179656 | tf_op jit(solution)/shard_map/ppermute | solution.py:486
  123.8 1.3 %collective-permute-done.2.other_ref = f32[32,24,128]{2,1,0:T(8,128)S(1)} collective-permute-done((f32[32,24,128]{2,1,0:T(8,128)S(1)}, f32[32,24,128]{2,1,0:T(8,128)S(1)}, u32[]{:S(2)}, u32[]{:S(2)}) %collective-permute-start.2) | collective-permute-done | bytes 393248 | tf_op jit(solution)/shard_map/ppermute | solution.py:486
  125.1 0.9 shard_map.127
  (7 shorter events, 0.1 us)
Async XLA Ops:
  0.6 65.5 %copy-start.3 = (bf16[8,16,1024]{2,1,0:T(8,128)(2,1)S(1)}, bf16[8,16,1024]{2,1,0:T(8,128)(2,1)}, u32[]{:S(2)}) copy-start(bf16[8,16,1024]{2,1,0:T(8,128)(2,1)} %param.12) | copy-start | bytes 786436
  0.6 1.1 copy-start.4
  1.7 64.4 %copy-start.6 = (bf16[8,1024]{1,0:T(8,128)(2,1)S(1)}, bf16[8,1024]{1,0:T(8,128)(2,1)}, u32[]{:S(2)}) copy-start(bf16[8,1024]{1,0:T(8,128)(2,1)} %bias_ref.3) | copy-start | bytes 49156
  1.7 72.4 %copy-start.11 = (s32[128,1]{0,1:T(1,128)S(1)}, s32[128,1]{0,1:T(1,128)}, u32[]{:S(2)}) copy-start(s32[128,1]{0,1:T(1,128)} %param.11) | copy-start | bytes 1540
  2.6 29.3 %all-to-all-start = ((bf16[64,4,1024]{2,1,0:T(4,128)(2,1)}), bf16[64,4,1024]{2,1,0:T(4,128)(2,1)S(1)}, u32[]{:S(2)}, u32[]{:S(2)}) async-start(bf16[64,4,1024]{2,1,0:T(4,128)(2,1)} %shard_map.119), calls=%async_computation | async-start | bytes 1048576 | tf_op jit(solution)/shard_map/all_to_all | solution.py:393
  15.7 0.9 copy-start.2
  16.7 0.7 copy-start.5
  17.4 0.8 copy-start.7
  18.2 0.8 copy-start.8
  19.0 0.8 copy-start.9
  27.2 1.9 %copy-start = (bf16[4,1024,512]{2,1,0:T(8,128)(2,1)}, bf16[4,1024,512]{2,1,0:T(8,128)(2,1)S(1)}, u32[]{:S(2)}) copy-start(bf16[4,1024,512]{2,1,0:T(8,128)(2,1)S(1)} %get-tuple-element.41.matrix_ref) | copy-start | bytes 12582916
  31.9 0.7 copy-start.10
  35.4 30.8 %all-to-all-start.1 = ((f32[8,160,128]{2,1,0:T(8,128)}), f32[8,160,128]{2,1,0:T(8,128)S(1)}, u32[]{:S(2)}, u32[]{:S(2)}) async-start(f32[8,160,128]{2,1,0:T(8,128)} %get-tuple-element.31), calls=%async_computation.1 | async-start | bytes 1310720 | tf_op jit(solution)/shard_map/all_to_all | solution.py:435
  71.7 3.7 %collective-permute-start = (f32[32,24,128]{2,1,0:T(8,128)S(1)}, f32[32,24,128]{2,1,0:T(8,128)S(1)}, u32[]{:S(2)}, u32[]{:S(2)}) collective-permute-start(f32[32,24,128]{2,1,0:T(8,128)S(1)} %get-tuple-element.36), channel_id=1, source_target_pairs={{0,8},{8,0},{1,9},{9,1},{2,10},{10,2},{3,11},{11,3},{4,12},{12,4},... | collective-permute-start | bytes 1179656 | tf_op jit(solution)/shard_map/ppermute | solution.py:455
  76.3 23.4 %all-to-all-start.2 = ((f32[32,32,128]{2,1,0:T(8,128)}), f32[32,32,128]{2,1,0:T(8,128)S(1)}, u32[]{:S(2)}, u32[]{:S(2)}) async-start(f32[32,32,128]{2,1,0:T(8,128)} %get-tuple-element.39), calls=%async_computation.2 | async-start | bytes 1048576 | tf_op jit(solution)/shard_map/all_to_all | solution.py:473
  100.4 17.0 %all-to-all-start.3 = ((f32[32,24,128]{2,1,0:T(8,128)}), f32[32,24,128]{2,1,0:T(8,128)S(1)}, u32[]{:S(2)}, u32[]{:S(2)}) async-start(f32[32,24,128]{2,1,0:T(8,128)} %shard_map.125), calls=%async_computation.3 | async-start | bytes 786432 | tf_op jit(solution)/shard_map/all_to_all | solution.py:476
  105.4 2.2 %copy-start.1 = (bf16[4,1024,512]{2,1,0:T(8,128)(2,1)S(1)}, bf16[4,1024,512]{2,1,0:T(8,128)(2,1)}, u32[]{:S(2)}) copy-start(bf16[4,1024,512]{2,1,0:T(8,128)(2,1)} %copy-done) | copy-start | bytes 12582916
  110.4 6.4 %collective-permute-start.1 = (bf16[32,4,128]{2,1,0:T(4,128)(2,1)S(1)}, bf16[32,4,128]{2,1,0:T(4,128)(2,1)S(1)}, u32[]{:S(2)}, u32[]{:S(2)}) collective-permute-start(bf16[32,4,128]{2,1,0:T(4,128)(2,1)S(1)} %fusion), channel_id=1, source_target_pairs={{0,8},{8,0},{1,9},{9,1},{2,10},{10,2},{3,11},{11,3},{4,12},{12,4},... | collective-permute-start | bytes 98312 | tf_op jit(solution)/shard_map/ppermute | solution.py:479
  117.5 7.7 %collective-permute-start.2 = (f32[32,24,128]{2,1,0:T(8,128)S(1)}, f32[32,24,128]{2,1,0:T(8,128)S(1)}, u32[]{:S(2)}, u32[]{:S(2)}) collective-permute-start(f32[32,24,128]{2,1,0:T(8,128)S(1)} %all-to-all-done.3.half_ref), channel_id=1, source_target_pairs={{0,8},{8,0},{1,9},{9,1},{2,10},{10,2},{3,11},{11,3},{4,12},{12,4},... | collective-permute-start | bytes 1179656 | tf_op jit(solution)/shard_map/ppermute | solution.py:486

commit v6 on v5

--- a/solution.py
+++ b/solution.py
@@ -19,6 +19,11 @@
 LANES = 128
 TILES = D // LANES
 CHUNK = 24
+STATS = 80
+STEPS = 128.0
+FULL = 32600.0
+i16 = jnp.int16
+i32 = jnp.int32
 INTERPRET = False
 
 f32 = jnp.float32
@@ -56,6 +61,22 @@
 
 def group(value, v):
     return value[:, v * H : (v + 1) * H]
+
+
+def scale_code(value):
+    most = jnp.max(jnp.abs(value), axis=1, keepdims=True)
+    return jnp.floor(jnp.log(jnp.maximum(most, 1e-30)) * STEPS) + 1.0
+
+
+def two_words(value):
+    code = scale_code(value)
+    fixed = jnp.round(value * (jnp.exp(code * (-1.0 / STEPS)) * 2.0**30)).astype(i32)
+    low = (fixed & 0xFFFF) - 0x8000
+    return (fixed >> 16).astype(f32), low.astype(f32), code
+
+
+def from_words(high, low, code):
+    return (high * 65536.0 + (low + 32768.0)) * (jnp.exp(code * (1.0 / STEPS)) * 2.0**-30)
 
 
 def kernel_call(body, out_shape, mib, scratch=(), in_specs=None, out_specs=None, aliases=None):
@@ -105,7 +126,7 @@
 
 
 def forward_kernel(
-    index_ref, weight_ref, fields_ref, embed_ref, bias_ref, query_ref, x_ref, e_ref, s_ref, exch_ref, matrix_ref, sum_ref
+    index_ref, weight_ref, fields_ref, embed_ref, bias_ref, query_ref, x_ref, e_ref, s_ref, exch_ref, code_ref, sum_ref
 ):
     var_local = fields_ref.shape[0]
     blocks = fields_ref.shape[1] // PTS_BLK
@@ -114,7 +135,6 @@
     gather = spread(PB, PIX_BLK, lambda r, c: r == c // P_SIZE)
     for block in range(blocks):
         matrix = interp_transposed(index_ref, weight_ref, block)
-        matrix_ref[block] = matrix
         pixels = dot(fields_ref[:, pl.ds(block * PTS_BLK, PTS_BLK)], matrix).astype(bf16)
         widened = jnp.where(own_pixel, dot(copy_rows, pixels), 0.0).astype(bf16)
         x_ref[pl.ds(block * PB, PB), :] = dot_t(gather, widened).astype(bf16)
@@ -148,8 +168,17 @@
             sum_ref[...] += term
     groups = exch_ref.shape[0]
     width = D // groups
+    codes = []
     for g in range(groups):
-        exch_ref[g, :patches, :] = sum_ref[:, g * width : (g + 1) * width]
+        part = sum_ref[:, g * width : (g + 1) * width]
+        code = scale_code(part)
+        coded = jnp.round(part * (jnp.exp(code * (-1.0 / STEPS)) * FULL))
+        exch_ref[g, :patches, :] = coded.astype(i32).astype(i16)
+        codes.append(code)
+    codes = jnp.concatenate(codes + [jnp.zeros((patches, LANES - groups), f32)], axis=1)
+    if patches < LANES:
+        codes = jnp.concatenate([codes, jnp.zeros((LANES - patches, LANES), f32)], axis=0)
+    code_ref[...] = codes.T[:groups, :]
 
 
 def target_of(column_ref, row_ref, depth, as_row):
@@ -177,6 +206,7 @@
     e_ref,
     s_ref,
     x_ref,
+    code_ref,
     old_ref,
     up_ref,
     both_ref,
@@ -206,30 +236,41 @@
     weights = jnp.exp(scores - peak)
     total = over_vars(weights, jnp.add)
     inner = over_vars(weights * grad_attn, jnp.add) / total
-    packed = [group(peak + jnp.log(total), 0), group(inner, 0)]
-    packed = jnp.concatenate(packed + [jnp.zeros((patches, LANES - 2 * H), f32)], axis=1)
+    log_words = two_words(group(peak + jnp.log(total), 0))
+    inner_words = two_words(group(inner, 0))
+    packed = [*log_words[:2], *inner_words[:2], log_words[2], inner_words[2]]
+    packed = jnp.concatenate(packed + [jnp.zeros((patches, LANES - 4 * H - 2), f32)], axis=1)
     if patches < LANES:
         packed = jnp.concatenate([packed, jnp.zeros((LANES - patches, LANES), f32)], axis=0)
-    stats_ref[...] = packed.T[: 2 * H, :]
-    copies = [
-        pltpu.make_async_copy(stats_ref, exch_ref.at[g, pl.ds(patches, 2 * H)], sems.at[g])
-        for g in range(exch_ref.shape[0])
-    ]
-    for copy in copies:
-        copy.start()
+    turned = packed.T[:STATS, :]
+    row = iota((STATS, LANES), 0)
+    copies = []
+    for g in range(exch_ref.shape[0]):
+        one = jnp.where(row == 4 * H + 2, code_ref[g : g + 1, :], turned)
+        stats_ref[g] = one.astype(i32).astype(i16)
+        copies.append(
+            pltpu.make_async_copy(
+                stats_ref.at[g], exch_ref.at[g, pl.ds(patches, STATS)], sems.at[g]
+            )
+        )
+        copies[-1].start()
     for copy in copies:
         copy.wait()
 
 
 def combine_stats(exch_ref, patches):
     groups = exch_ref.shape[0]
-    logs, inners = [], []
+    logs, inners, scales = [], [], []
     for g in range(groups):
-        stats = exch_ref[g, patches : patches + 2 * H, :]
-        rows = jnp.concatenate([stats, jnp.zeros((LANES - 2 * H, LANES), f32)], axis=0).T
+        stats = exch_ref[g, patches : patches + STATS, :].astype(i32).astype(f32)
+        rows = jnp.concatenate([stats, jnp.zeros((LANES - STATS, LANES), f32)], axis=0).T
         rows = rows[:patches]
-        logs.append(rows[:, :H])
-        inners.append(rows[:, H : 2 * H])
+        at = 4 * H
+        logs.append(from_words(rows[:, :H], rows[:, H : 2 * H], rows[:, at : at + 1]))
+        inners.append(
+            from_words(rows[:, 2 * H : 3 * H], rows[:, 3 * H : at], rows[:, at + 1 : at + 2])
+        )
+        scales.append(jnp.exp(rows[:, at + 2 : at + 3] * (1.0 / STEPS)) * (1.0 / FULL))
     peak = logs[0]
     for other in logs[1:]:
         peak = jnp.maximum(peak, other)
@@ -237,7 +278,7 @@
     total = sum(factors)
     shares = [factor / total for factor in factors]
     inner = sum(f * t for f, t in zip(shares, inners))
-    return peak, total, inner, shares
+    return peak, total, inner, [share * scale for share, scale in zip(shares, scales)]
 
 
 def tokens_kernel(depth, slots, place_ref, column_ref, row_ref, exch_ref, out_ref):
@@ -252,7 +293,7 @@
     mixture = jnp.zeros((patches, width), f32)
     for g in range(groups):
         scale = jnp.concatenate(split(shares[g], 3), axis=1)
-        mixture = mixture + dot(scale, pick) * exch_ref[g, :patches, :]
+        mixture = mixture + dot(scale, pick) * exch_ref[g, :patches, :].astype(i32).astype(f32)
     target = target_of(column_ref, row_ref, depth, True)
     place = jnp.where(iota((slots, patches), 0) == target, 1.0, 0.0).astype(bf16)
     out_ref[...] = dot(place, mixture.astype(bf16))
@@ -360,7 +401,7 @@
     send_ref[...] = wide_ref[pl.ds((1 - core) * half, half)].reshape(send_ref.shape)
 
 
-def field_kernel(matrix_ref, gx_ref, out_ref):
+def field_kernel(index_ref, weight_ref, gx_ref, out_ref):
     wide = gx_ref.shape[1]
     var_local = wide // P_SIZE
     blocks = gx_ref.shape[0] // PB
@@ -372,7 +413,9 @@
         wide_grad = dot(gx_t[:, block * PB : (block + 1) * PB], copy)
         wide_grad = jnp.where(own_pixel, wide_grad, 0.0).astype(bf16)
         grad = dot(fold, wide_grad).astype(bf16)
-        out_ref[:, pl.ds(block * PTS_BLK, PTS_BLK)] = dot_t(grad, matrix_ref[block])
+        out_ref[:, pl.ds(block * PTS_BLK, PTS_BLK)] = dot_t(
+            grad, interp_transposed(index_ref, weight_ref, block)
+        )
 
 
 def local(
@@ -403,14 +446,14 @@
     embed_flat = embed_weight.reshape(wide, D)
     query = agg_query.reshape(1, D)
     row_map = owner_map.reshape(1, patches)
-    x_all, embedded, scores, sums, matrix = kernel_call(
+    x_all, embedded, scores, sums, codes = kernel_call(
         forward_kernel,
         (
             shape((patches, wide), bf16),
             shape((var_local, patches, D), bf16),
             shape((patches, var_local * H), f32),
-            shape((groups, patches + 2 * H, width), f32),
-            shape((fields.shape[1] // PTS_BLK, PTS_BLK, PIX_BLK), bf16),
+            shape((groups, patches + STATS, width), i16),
+            shape((groups, LANES), f32),
         ),
         mib=20,
         scratch=[pltpu.VMEM((patches, D), f32)],
@@ -424,14 +467,14 @@
             shape((patches, D), bf16),
             shape((2, patches, var_local * H), f32),
             shape((wide, patches), bf16),
-            shape(sums.shape, f32),
+            shape(sums.shape, i16),
         ),
         mib=12,
-        scratch=[pltpu.VMEM((2 * H, LANES), f32), pltpu.SemaphoreType.DMA((groups,))],
-        in_specs=[vmem] * 6 + [anywhere],
+        scratch=[pltpu.VMEM((groups, STATS, LANES), i16), pltpu.SemaphoreType.DMA((groups,))],
+        in_specs=[vmem] * 7 + [anywhere],
         out_specs=(vmem, vmem, vmem, anywhere),
-        aliases={6: 3},
-    )(owner_map, row_map, inbox, embedded, scores, x_all, sums)
+        aliases={7: 3},
+    )(owner_map, row_map, inbox, embedded, scores, x_all, codes, sums)
     exchange = lax.all_to_all(exchange, "z", 0, 0, tiled=True)
 
     core = lax.axis_index("c").astype(jnp.int32)
@@ -467,7 +510,7 @@
     )(kept, crossed, outbox)
 
     field_grad = kernel_call(field_kernel, shape((var_local, fields.shape[1]), f32), mib=16)(
-        matrix, grad_x
+        index_t, weight_t, grad_x
     )
 
     coming = lax.all_to_all(going, "r", 0, 0, tiled=True)

time: 127 us -> 121 us (0.953)
  local copies, waits for them, and re-layouts: 12.1 us -> 3.33 us
  Pallas kernels: 22.6 us -> 25.3 us
  waiting for transfers between devices: 30.7 us -> 32.6 us
  starting transfers between devices: 47.6 us -> 45.8 us
    unnamed x25 -> x21, local copies, waits for them, and re-layouts: 10.6 us -> 2.58 us
    all_to_all x1, waiting for transfers between devices: 2.72 us -> 9.95 us  [local(): lax.all_to_all(kernel_call(outbox_kernel, shape((row_devices, depth, D),...]
    all_to_all x1, waiting for transfers between devices: 20.8 us -> 15.8 us  [local(): exchange = lax.all_to_all(exchange, 'z', 0, 0, tiled=True)]
    all_to_all x1, starting transfers between devices: 6.74 us -> 4.49 us  [local(): coming = lax.all_to_all(going, 'r', 0, 0, tiled=True)]
    pallas_call x1, Pallas kernels: 2.76 us -> 4.51 us  [local(): kernel_call(field_kernel, shape((var_local, fields.shape[1]), f32), mib=16)]
  transfers between devices with their start and end apart: 7 -> 7, of which waited for: 6 -> 6; matrix products, arithmetic and copies ran while one was open for 2% -> 1% of each run, Pallas kernels for 9% -> 11%
where the time goes in v6:
time: 121 us; the launch traced here: 120 us
  starting transfers between devices  45.8 us (38%)
  waiting for transfers between devices  32.6 us (27%)
  Pallas kernels  25.3 us (21%)
  blocking collectives  12.1 us (10%)
  local copies, waits for them, and re-layouts  3.33 us (3%)
    all_to_all x1, waiting for transfers between devices, local(): exchange = lax.all_to_all(exchange, 'z', 0, 0, tiled=True)  15.8 us
    psum x1, blocking collectives, local(): query_half = lax.psum(query_half, 'z')  12.1 us
    all_to_all x1, starting transfers between devices, local(): lax.all_to_all(kernel_call(outbox_kernel, shape((row_devices, depth, D),...  11.6 us
    all_to_all x1, starting transfers between devices, local(): exchange = lax.all_to_all(exchange, 'z', 0, 0, tiled=True)  10 us
    all_to_all x1, waiting for transfers between devices, local(): lax.all_to_all(kernel_call(outbox_kernel, shape((row_devices, depth, D),...  9.95 us
    pallas_call x1, Pallas kernels, local(): kernel_call(forward_kernel, (shape((patches, wide), bf16), shape((var_loc...  7.49 us
    ppermute x1, starting transfers between devices, local(): other = lax.ppermute(half, 'c', swap)  6.79 us
    pallas_call x1, Pallas kernels, local(): kernel_call(backward_kernel, (shape((ring, rows, LANES), f32), shape((rin...  5.88 us
  transfers between devices with their start and end apart: 7, of which 6 were waited for; matrix products, arithmetic and copies ran while one was open for 1% of the time, Pallas kernels for 11%

profile of v6, /device:TPU:1, one launch (start us, length us, event | category | flops | bytes accessed | tf_op | source)
XLA Modules:
  0.0 120.1 jit_solution(6723505276400943658)
XLA Ops:
  0.6 0.0 copy-start
  0.6 0.0 copy-start.1
  0.7 1.1 copy-done.1
  1.7 0.0 copy-start.9
  1.7 0.0 copy-start.8
  1.7 0.0 copy-start.2
  1.7 0.0 copy-start.3
  1.7 0.0 copy-start.4
  1.8 0.0 copy-start.5
  1.8 0.8 shard_map.119
  2.6 11.6 %all-to-all-start = ((bf16[64,4,1024]{2,1,0:T(4,128)(2,1)}), bf16[64,4,1024]{2,1,0:T(4,128)(2,1)S(1)}, u32[]{:S(2)}, u32[]{:S(2)}) async-start(bf16[64,4,1024]{2,1,0:T(4,128)(2,1)} %shard_map.119), calls=%async_computation | async-start | bytes 1048576 | tf_op jit(solution)/shard_map/all_to_all | solution.py:436
  14.2 0.0 copy-done.9
  14.2 0.1 reshape.42.query_ref
  14.3 0.0 copy-done.8
  14.3 0.1 copy.14.refs_0_.refs_1_
  14.4 0.0 copy-done
  14.4 0.0 copy-done.2
  14.4 0.0 copy-done.3
  14.5 0.0 copy-done.4
  14.5 0.0 copy-done.5
  14.5 7.5 %shard_map.120 = (bf16[128,128]{1,0:T(8,128)(2,1)S(1)}, bf16[8,128,1024]{2,1,0:T(8,128)(2,1)S(1)}, f32[128,128]{1,0:T(8,128)S(1)}, s16[8,208,128]{2,1,0:T(8,128)(2,1)}, f32[8,128]{1,0:T(8,128)S(1)}) custom-call(s32[4,2048]{1,0:T(4,128)S(1)} %bitcast.24, f32[4,2048]{1,0:T(4,128)S(1)} %bitcast.26, bf16[8,4096]{1,0:T(8,128)(2,1)S(1)} %copy-done.5, ...), custom_call_target="tpu_custom_call" | custom-call | tf_op jit(solution)/shard_map/pallas_call | solution.py:449
  22.0 10.0 %all-to-all-done.refs_2_ = bf16[64,4,1024]{2,1,0:T(4,128)(2,1)S(1)} async-done(((bf16[64,4,1024]{2,1,0:T(4,128)(2,1)}), bf16[64,4,1024]{2,1,0:T(4,128)(2,1)S(1)}, u32[]{:S(2)}, u32[]{:S(2)}) %all-to-all-start) | async-done | bytes 524320 | tf_op jit(solution)/shard_map/all_to_all | solution.py:436
  31.9 2.9 %shard_map.121 = (bf16[128,1024]{1,0:T(8,128)(2,1)S(1)}, f32[2,128,128]{2,1,0:T(8,128)S(1)}, bf16[128,128]{1,0:T(8,128)(2,1)S(1)}, s16[8,208,128]{2,1,0:T(8,128)(2,1)}) custom-call(s32[128,1]{1,0:T(8,128)S(1)} %copy.14.refs_0_.refs_1_, s32[1,128]{1,0:T(1,128)S(1)} %bitcast.28, ...), custom_call_target="tpu_custom_call", output_to_operand_aliasing={{3}: (7, {})} | custom-call | tf_op jit(solution)/shard_map/pallas_call | solution.py:464
  34.9 0.0 copy-start.6
  34.9 0.6 copy-done.6
  35.5 10.0 %all-to-all-start.1 = ((s16[8,208,128]{2,1,0:T(8,128)(2,1)}), s16[8,208,128]{2,1,0:T(8,128)(2,1)S(1)}, u32[]{:S(2)}, u32[]{:S(2)}) async-start(s16[8,208,128]{2,1,0:T(8,128)(2,1)} %get-tuple-element.32), calls=%async_computation.1 | async-start | bytes 851968 | tf_op jit(solution)/shard_map/all_to_all | solution.py:478
  45.5 15.8 %all-to-all-done.1.exch_ref.refs_3_ = s16[8,208,128]{2,1,0:T(8,128)(2,1)S(1)} async-done(((s16[8,208,128]{2,1,0:T(8,128)(2,1)}), s16[8,208,128]{2,1,0:T(8,128)(2,1)S(1)}, u32[]{:S(2)}, u32[]{:S(2)}) %all-to-all-start.1) | async-done | bytes 426016 | tf_op jit(solution)/shard_map/all_to_all | solution.py:478
  61.4 0.0 copy-start.7
  61.4 0.8 copy-done.7
  62.1 5.9 %shard_map.122 = (f32[32,24,128]{2,1,0:T(8,128)S(1)}, f32[32,24,128]{2,1,0:T(8,128)S(1)}, bf16[128,128]{1,0:T(8,128)(2,1)S(1)}) custom-call(s32[1]{0:T(128)} %bitcast.core_ref, s16[8,208,128]{2,1,0:T(8,128)(2,1)S(1)} %all-to-all-done.1.exch_ref.refs_3_, f32[2,128,128]{2,1,0:T(8,128)S(1)} %get-tuple-element.33.both_ref, ...), custom_call_target="tpu_custom_call" | custom-call | tf_op jit(solution)/shard_map/pallas_call | solution.py:487
  68.0 2.4 %collective-permute-start = (f32[32,24,128]{2,1,0:T(8,128)S(1)}, f32[32,24,128]{2,1,0:T(8,128)S(1)}, u32[]{:S(2)}, u32[]{:S(2)}) collective-permute-start(f32[32,24,128]{2,1,0:T(8,128)S(1)} %get-tuple-element.37), channel_id=1, source_target_pairs={{0,8},{8,0},{1,9},{9,1},{2,10},{10,2},{3,11},{11,3},{4,12},{12,4},... | collective-permute-start | bytes 1179656 | tf_op jit(solution)/shard_map/ppermute | solution.py:498
  70.4 1.1 shard_map.123.tokens_ref
  71.6 0.2 collective-permute-done.crossed_ref
  71.7 0.9 shard_map.124
  72.6 4.5 %all-to-all-start.2 = ((f32[32,32,128]{2,1,0:T(8,128)}), f32[32,32,128]{2,1,0:T(8,128)S(1)}, u32[]{:S(2)}, u32[]{:S(2)}) async-start(f32[32,32,128]{2,1,0:T(8,128)} %get-tuple-element.40), calls=%async_computation.2 | async-start | bytes 1048576 | tf_op jit(solution)/shard_map/all_to_all | solution.py:516
  77.1 12.1 %psum.7.query_ref = f32[4,128]{1,0:T(4,128)S(1)} all-reduce(f32[4,128]{1,0:T(4,128)S(1)} %get-tuple-element.41), channel_id=1, replica_groups=mesh['r'=32,'c'=2,'z'=8] {'z'}, use_global_device_ids=true, to_apply=%region_0.0 | all-reduce | flops 512 | bytes 4096 | tf_op jit(solution)/shard_map/psum | solution.py:517
  89.2 4.5 %all-to-all-done.2.coming_ref = f32[32,32,128]{2,1,0:T(8,128)S(1)} async-done(((f32[32,32,128]{2,1,0:T(8,128)}), f32[32,32,128]{2,1,0:T(8,128)S(1)}, u32[]{:S(2)}, u32[]{:S(2)}) %all-to-all-start.2) | async-done | bytes 524320 | tf_op jit(solution)/shard_map/all_to_all | solution.py:516
  93.7 0.8 shard_map.125
  94.5 4.9 %all-to-all-start.3 = ((f32[32,24,128]{2,1,0:T(8,128)}), f32[32,24,128]{2,1,0:T(8,128)S(1)}, u32[]{:S(2)}, u32[]{:S(2)}) async-start(f32[32,24,128]{2,1,0:T(8,128)} %shard_map.125), calls=%async_computation.3 | async-start | bytes 786432 | tf_op jit(solution)/shard_map/all_to_all | solution.py:519
  99.5 4.5 %shard_map.126 = f32[8,4096]{1,0:T(8,128)} custom-call(s32[4,2048]{1,0:T(4,128)S(1)} %bitcast.25, f32[4,2048]{1,0:T(4,128)S(1)} %bitcast.27, bf16[128,128]{1,0:T(8,128)(2,1)S(1)} %get-tuple-element.42.gx_ref), custom_call_target="tpu_custom_call" | custom-call | tf_op jit(solution)/shard_map/pallas_call | solution.py:512
  104.0 5.5 %collective-permute-start.1 = (bf16[32,4,128]{2,1,0:T(4,128)(2,1)S(1)}, bf16[32,4,128]{2,1,0:T(4,128)(2,1)S(1)}, u32[]{:S(2)}, u32[]{:S(2)}) collective-permute-start(bf16[32,4,128]{2,1,0:T(4,128)(2,1)S(1)} %fusion), channel_id=1, source_target_pairs={{0,8},{8,0},{1,9},{9,1},{2,10},{10,2},{3,11},{11,3},{4,12},{12,4},... | collective-permute-start | bytes 98312 | tf_op jit(solution)/shard_map/ppermute | solution.py:522
  109.6 0.8 collective-permute-done.1
  110.4 0.1 maximum_select_fusion
  110.4 0.7 copy.20
  111.1 0.0 all-to-all-done.3.half_ref
  111.1 6.8 %collective-permute-start.2 = (f32[32,24,128]{2,1,0:T(8,128)S(1)}, f32[32,24,128]{2,1,0:T(8,128)S(1)}, u32[]{:S(2)}, u32[]{:S(2)}) collective-permute-start(f32[32,24,128]{2,1,0:T(8,128)S(1)} %all-to-all-done.3.half_ref), channel_id=1, source_target_pairs={{0,8},{8,0},{1,9},{9,1},{2,10},{10,2},{3,11},{11,3},{4,12},{12,4},... | collective-permute-start | bytes 1179656 | tf_op jit(solution)/shard_map/ppermute | solution.py:529
  117.9 1.3 %collective-permute-done.2.other_ref = f32[32,24,128]{2,1,0:T(8,128)S(1)} collective-permute-done((f32[32,24,128]{2,1,0:T(8,128)S(1)}, f32[32,24,128]{2,1,0:T(8,128)S(1)}, u32[]{:S(2)}, u32[]{:S(2)}) %collective-permute-start.2) | collective-permute-done | bytes 393248 | tf_op jit(solution)/shard_map/ppermute | solution.py:529
  119.2 0.9 shard_map.127
  (3 shorter events, 0.1 us)
Async XLA Ops:
  0.6 13.8 %copy-start = (bf16[8,16,1024]{2,1,0:T(8,128)(2,1)S(1)}, bf16[8,16,1024]{2,1,0:T(8,128)(2,1)}, u32[]{:S(2)}) copy-start(bf16[8,16,1024]{2,1,0:T(8,128)(2,1)} %param.12) | copy-start | bytes 786436
  0.6 1.1 copy-start.1
  1.7 12.5 %copy-start.9 = (f32[16,64]{1,0:T(8,128)S(1)}, f32[16,64]{1,0:T(8,128)}, u32[]{:S(2)}) copy-start(f32[16,64]{1,0:T(8,128)} %param.14) | copy-start | bytes 12292
  1.7 12.6 %copy-start.8 = (s32[128,1]{0,1:T(1,128)S(1)}, s32[128,1]{0,1:T(1,128)}, u32[]{:S(2)}) copy-start(s32[128,1]{0,1:T(1,128)} %param.11) | copy-start | bytes 1540
  1.7 12.7 %copy-start.2 = (s32[2048,4]{0,1:T(4,128)S(1)}, s32[2048,4]{0,1:T(4,128)}, u32[]{:S(2)}) copy-start(s32[2048,4]{0,1:T(4,128)} %param.9) | copy-start | bytes 98308
  1.7 12.7 %copy-start.3 = (f32[2048,4]{0,1:T(4,128)S(1)}, f32[2048,4]{0,1:T(4,128)}, u32[]{:S(2)}) copy-start(f32[2048,4]{0,1:T(4,128)} %param.10) | copy-start | bytes 98308
  1.7 12.7 %copy-start.4 = (bf16[8,1024]{1,0:T(8,128)(2,1)S(1)}, bf16[8,1024]{1,0:T(8,128)(2,1)}, u32[]{:S(2)}) copy-start(bf16[8,1024]{1,0:T(8,128)(2,1)} %bias_ref.3) | copy-start | bytes 49156
  1.8 12.7 %copy-start.5 = (bf16[8,4096]{1,0:T(8,128)(2,1)S(1)}, bf16[8,4096]{1,0:T(8,128)(2,1)}, u32[]{:S(2)}) copy-start(bf16[8,4096]{1,0:T(8,128)(2,1)} %fields_ref.1) | copy-start | bytes 196612
  2.6 29.3 %all-to-all-start = ((bf16[64,4,1024]{2,1,0:T(4,128)(2,1)}), bf16[64,4,1024]{2,1,0:T(4,128)(2,1)S(1)}, u32[]{:S(2)}, u32[]{:S(2)}) async-start(bf16[64,4,1024]{2,1,0:T(4,128)(2,1)} %shard_map.119), calls=%async_computation | async-start | bytes 1048576 | tf_op jit(solution)/shard_map/all_to_all | solution.py:436
  34.9 0.6 copy-start.6
  35.5 25.9 %all-to-all-start.1 = ((s16[8,208,128]{2,1,0:T(8,128)(2,1)}), s16[8,208,128]{2,1,0:T(8,128)(2,1)S(1)}, u32[]{:S(2)}, u32[]{:S(2)}) async-start(s16[8,208,128]{2,1,0:T(8,128)(2,1)} %get-tuple-element.32), calls=%async_computation.1 | async-start | bytes 851968 | tf_op jit(solution)/shard_map/all_to_all | solution.py:478
  61.4 0.8 copy-start.7
  68.0 3.7 %collective-permute-start = (f32[32,24,128]{2,1,0:T(8,128)S(1)}, f32[32,24,128]{2,1,0:T(8,128)S(1)}, u32[]{:S(2)}, u32[]{:S(2)}) collective-permute-start(f32[32,24,128]{2,1,0:T(8,128)S(1)} %get-tuple-element.37), channel_id=1, source_target_pairs={{0,8},{8,0},{1,9},{9,1},{2,10},{10,2},{3,11},{11,3},{4,12},{12,4},... | collective-permute-start | bytes 1179656 | tf_op jit(solution)/shard_map/ppermute | solution.py:498
  72.6 21.1 %all-to-all-start.2 = ((f32[32,32,128]{2,1,0:T(8,128)}), f32[32,32,128]{2,1,0:T(8,128)S(1)}, u32[]{:S(2)}, u32[]{:S(2)}) async-start(f32[32,32,128]{2,1,0:T(8,128)} %get-tuple-element.40), calls=%async_computation.2 | async-start | bytes 1048576 | tf_op jit(solution)/shard_map/all_to_all | solution.py:516
  94.5 16.6 %all-to-all-start.3 = ((f32[32,24,128]{2,1,0:T(8,128)}), f32[32,24,128]{2,1,0:T(8,128)S(1)}, u32[]{:S(2)}, u32[]{:S(2)}) async-start(f32[32,24,128]{2,1,0:T(8,128)} %shard_map.125), calls=%async_computation.3 | async-start | bytes 786432 | tf_op jit(solution)/shard_map/all_to_all | solution.py:519
  104.0 6.4 %collective-permute-start.1 = (bf16[32,4,128]{2,1,0:T(4,128)(2,1)S(1)}, bf16[32,4,128]{2,1,0:T(4,128)(2,1)S(1)}, u32[]{:S(2)}, u32[]{:S(2)}) collective-permute-start(bf16[32,4,128]{2,1,0:T(4,128)(2,1)S(1)} %fusion), channel_id=1, source_target_pairs={{0,8},{8,0},{1,9},{9,1},{2,10},{10,2},{3,11},{11,3},{4,12},{12,4},... | collective-permute-start | bytes 98312 | tf_op jit(solution)/shard_map/ppermute | solution.py:522
  111.1 8.1 %collective-permute-start.2 = (f32[32,24,128]{2,1,0:T(8,128)S(1)}, f32[32,24,128]{2,1,0:T(8,128)S(1)}, u32[]{:S(2)}, u32[]{:S(2)}) collective-permute-start(f32[32,24,128]{2,1,0:T(8,128)S(1)} %all-to-all-done.3.half_ref), channel_id=1, source_target_pairs={{0,8},{8,0},{1,9},{9,1},{2,10},{10,2},{3,11},{11,3},{4,12},{12,4},... | collective-permute-start | bytes 1179656 | tf_op jit(solution)/shard_map/ppermute | solution.py:529

commit v7 on v6

--- a/solution.py
+++ b/solution.py
@@ -19,6 +19,7 @@
 LANES = 128
 TILES = D // LANES
 CHUNK = 24
+SENT = CHUNK + TILES
 STATS = 80
 STEPS = 128.0
 FULL = 32600.0
@@ -77,6 +78,23 @@
 
 def from_words(high, low, code):
     return (high * 65536.0 + (low + 32768.0)) * (jnp.exp(code * (1.0 / STEPS)) * 2.0**-30)
+
+
+def block_code(value):
+    most = jnp.max(jnp.max(jnp.abs(value), axis=2, keepdims=True), axis=1, keepdims=True)
+    return jnp.floor(jnp.log(jnp.maximum(most, 1e-30)) * STEPS) + 1.0
+
+
+def coded(value, code):
+    return jnp.round(value * (jnp.exp(code * (-1.0 / STEPS)) * FULL))
+
+
+def decoded(value, code):
+    return value * (jnp.exp(code * (1.0 / STEPS)) * (1.0 / FULL))
+
+
+def to_words(value):
+    return value.astype(i32).astype(i16)
 
 
 def kernel_call(body, out_shape, mib, scratch=(), in_specs=None, out_specs=None, aliases=None):
@@ -299,47 +317,83 @@
     out_ref[...] = dot(place, mixture.astype(bf16))
 
 
-def merge_kernel(kept_ref, crossed_ref, tokens_ref, going_ref, query_ref):
+def code_chunks(weights, bias, extra):
+    count = weights.shape[0]
+    weight_code, bias_code = block_code(weights), block_code(bias)
+    rows = [coded(weights, weight_code), coded(bias, bias_code)]
+    rows += [jnp.broadcast_to(code, (count, 1, LANES)) for code in (weight_code, bias_code)]
+    return jnp.concatenate(rows + [extra], axis=1)
+
+
+def merge_kernel(kept_ref, crossed_ref, tokens_ref, going_ref, query_ref, sum_ref):
     ring, rows = kept_ref.shape[0], kept_ref.shape[1]
-    going_ref[:, rows:, :] = tokens_ref[...].reshape(ring, tokens_ref.shape[0] // ring, LANES)
-    going_ref[:, :rows, :] = kept_ref[...] + crossed_ref[...]
     share = rows // CHUNK
+    sum_ref[...] = (kept_ref[...] + crossed_ref[...]).reshape(sum_ref.shape)
     for t in range(TILES // 2):
-        at = (t % share) * CHUNK + P_SIZE + 1
-        query_ref[t : t + 1, :] = going_ref[t // share, at : at + 1, :]
-
-
-def own_kernel(coming_ref, query_ref, out_ref):
-    ring, rows = out_ref.shape[0], out_ref.shape[1]
-    own = coming_ref[0, :rows, :]
-    for r in range(1, ring):
-        own = own + coming_ref[r, :rows, :]
-    spare = jnp.concatenate(
-        [query_ref[...], jnp.zeros((CHUNK - P_SIZE - 1 - TILES // 2, LANES), f32)], axis=0
+        query_ref[t : t + 1, :] = sum_ref[t, P_SIZE + 1 : P_SIZE + 2, :]
+    chunks = sum_ref.shape[0]
+    tokens = tokens_ref[...].reshape(ring, tokens_ref.shape[0] // ring, LANES)
+    token_code = block_code(tokens)
+    if share > 1:
+        token_rows = jnp.concatenate([token_code] * share, axis=1).reshape(chunks, 1, 1)
+    else:
+        token_rows = token_code
+    extra = jnp.broadcast_to(token_rows, (chunks, CHUNK - P_SIZE - 3, LANES))
+    words = code_chunks(sum_ref[:, :P_SIZE, :], sum_ref[:, P_SIZE : P_SIZE + 1, :], extra)
+    going_ref[...] = to_words(
+        jnp.concatenate([words.reshape(ring, rows, LANES), coded(tokens, token_code)], axis=1)
     )
-    rest = [own[CHUNK:]] if rows > CHUNK else []
-    own = jnp.concatenate([own[: P_SIZE + 1], spare] + rest, axis=0)
-    for r in range(ring):
-        out_ref[r] = own
+
+
+def own_kernel(coming_ref, query_ref, out_ref, arrived_ref):
+    ring, whole = coming_ref.shape[0], coming_ref.shape[1]
+    rows = whole - arrived_ref.shape[1]
+    share = rows // CHUNK
+    words = coming_ref[...].astype(i32).astype(f32)
+    arrived_ref[...] = decoded(words[:, rows:, :], words[:, P_SIZE + 3 : P_SIZE + 4, :]).astype(bf16)
+    high, low, code = two_words(query_ref[...])
+    code = jnp.broadcast_to(code, high.shape)
+    for k in range(share):
+        at = k * CHUNK
+        chunk = words[:, at : at + CHUNK, :]
+        weights = decoded(chunk[:, :P_SIZE], chunk[:, P_SIZE + 1 : P_SIZE + 2])
+        bias = decoded(chunk[:, P_SIZE : P_SIZE + 1], chunk[:, P_SIZE + 2 : P_SIZE + 3])
+        weights, bias = (jnp.sum(part, axis=0, keepdims=True) for part in (weights, bias))
+        extra = jnp.concatenate([jnp.zeros((1, LANES), f32), code], axis=0)
+        block = code_chunks(weights, bias, extra[None])
+        block = jnp.concatenate([block, jnp.concatenate([high, low], axis=0)[None]], axis=1)
+        block = to_words(block)
+        for r in range(ring):
+            out_ref[r, k * SENT : (k + 1) * SENT, :] = block[0]
 
 
 def final_kernel(core_ref, half_ref, other_ref, weight_ref, bias_ref, query_ref):
     ring, rows = half_ref.shape[0], half_ref.shape[1]
-    share = rows // CHUNK
+    share = rows // SENT
     low = core_ref[0] == 0
+    quarter = TILES // 2
     for c in range(2):
-        query = jnp.zeros((TILES // 2, LANES), f32)
+        query = jnp.zeros((quarter, LANES), f32)
         for r in range(ring):
-            half, other = half_ref[r], other_ref[r]
-            block = jnp.where(low, half, other) if c == 0 else jnp.where(low, other, half)
+            half, other = (ref[r].astype(i32).astype(f32) for ref in (half_ref, other_ref))
+            words = jnp.where(low, half, other) if c == 0 else jnp.where(low, other, half)
             for k in range(share):
                 v, t = divmod((c * ring + r) * share + k, TILES)
                 cut = slice(t * LANES, (t + 1) * LANES)
-                weight_ref[v * P_SIZE : (v + 1) * P_SIZE, cut] = block[k * CHUNK : k * CHUNK + P_SIZE]
-                bias_ref[v : v + 1, cut] = block[k * CHUNK + P_SIZE : k * CHUNK + P_SIZE + 1]
-            query = query + block[P_SIZE + 1 : P_SIZE + 1 + TILES // 2]
-        for t in range(TILES // 2):
-            at = (c * (TILES // 2) + t) * 2
+                block = words[k * SENT : (k + 1) * SENT]
+                weight_ref[v * P_SIZE : (v + 1) * P_SIZE, cut] = decoded(
+                    block[:P_SIZE], block[P_SIZE + 1 : P_SIZE + 2]
+                )
+                bias_ref[v : v + 1, cut] = decoded(
+                    block[P_SIZE : P_SIZE + 1], block[P_SIZE + 2 : P_SIZE + 3]
+                )
+            query = query + from_words(
+                words[CHUNK : CHUNK + quarter],
+                words[CHUNK + quarter : CHUNK + 2 * quarter],
+                words[CHUNK - quarter : CHUNK],
+            )
+        for t in range(quarter):
+            at = (c * quarter + t) * 2
             query_ref[at : at + 1, :] = query[t : t + 1, :DH]
             query_ref[at + 1 : at + 2, :] = query[t : t + 1, DH:]
 
@@ -505,8 +559,9 @@
     crossed, outbox = lax.optimization_barrier((crossed, outbox))
     going, query_half = kernel_call(
         merge_kernel,
-        (shape((ring, rows + pair, LANES), f32), shape((TILES // 2, LANES), f32)),
+        (shape((ring, rows + pair, LANES), i16), shape((TILES // 2, LANES), f32)),
         mib=8,
+        scratch=[pltpu.VMEM((chunks // 2, CHUNK, LANES), f32)],
     )(kept, crossed, outbox)
 
     field_grad = kernel_call(field_kernel, shape((var_local, fields.shape[1]), f32), mib=16)(
@@ -515,10 +570,17 @@
 
     coming = lax.all_to_all(going, "r", 0, 0, tiled=True)
     query_half = lax.psum(query_half, "z")
-    own = kernel_call(own_kernel, shape((ring, rows, LANES), f32), mib=8)(coming, query_half)
+    own, arrived = kernel_call(
+        own_kernel,
+        (
+            shape((ring, rows // CHUNK * SENT, LANES), i16),
+            shape((ring, pair, width), bf16),
+        ),
+        mib=8,
+    )(coming, query_half)
     half = lax.all_to_all(own, "r", 0, 0, tiled=True)
 
-    arrived = coming[:, rows:].astype(bf16).reshape(ring, 2, depth, width)
+    arrived = arrived.reshape(ring, 2, depth, width)
     crossed = lax.ppermute(jnp.where(core == 0, arrived[:, 1], arrived[:, 0]), "c", swap)
     kept = jnp.where(core == 0, arrived[:, 0], arrived[:, 1])
     tokens = jnp.where(

time: 121 us -> 124 us (1.025)
  starting transfers between devices: 45.8 us -> 52 us
  waiting for transfers between devices: 32.6 us -> 29.9 us
    all_to_all x1, waiting for transfers between devices: 4.47 us -> 0.01 us  [local(): coming = lax.all_to_all(going, 'r', 0, 0, tiled=True)]
    all_to_all x1, starting transfers between devices: 4.92 us -> 8.63 us  [local(): half = lax.all_to_all(own, 'r', 0, 0, tiled=True)]
    all_to_all x1, waiting for transfers between devices: 0.01 us -> 1.99 us  [local(): half = lax.all_to_all(own, 'r', 0, 0, tiled=True)]
    ppermute x1, starting transfers between devices: 5.52 us -> 6.88 us  [local(): lax.ppermute(jnp.where(core == 0, arrived[:, 1], arrived[:, 0]), 'c', swap)]
where the time goes in v7:
time: 124 us
  starting transfers between devices  52 us (42%)
  waiting for transfers between devices  29.9 us (24%)
  Pallas kernels  26 us (21%)
  blocking collectives  11.5 us (9%)
  local copies, waits for them, and re-layouts  3.32 us (3%)
    all_to_all x1, waiting for transfers between devices, local(): exchange = lax.all_to_all(exchange, 'z', 0, 0, tiled=True)  15.8 us
    all_to_all x1, starting transfers between devices, local(): lax.all_to_all(kernel_call(outbox_kernel, shape((row_devices, depth, D),...  11.6 us
    psum x1, blocking collectives, local(): query_half = lax.psum(query_half, 'z')  11.5 us
    all_to_all x1, starting transfers between devices, local(): exchange = lax.all_to_all(exchange, 'z', 0, 0, tiled=True)  10 us
    all_to_all x1, waiting for transfers between devices, local(): lax.all_to_all(kernel_call(outbox_kernel, shape((row_devices, depth, D),...  9.94 us
    all_to_all x1, starting transfers between devices, local(): half = lax.all_to_all(own, 'r', 0, 0, tiled=True)  8.63 us
    ppermute x1, starting transfers between devices, local(): other = lax.ppermute(half, 'c', swap)  7.97 us
    pallas_call x1, Pallas kernels, local(): kernel_call(forward_kernel, (shape((patches, wide), bf16), shape((var_loc...  7.51 us
  transfers between devices with their start and end apart: 7, of which 6 were waited for; matrix products, arithmetic and copies ran while one was open for 1% of the time, Pallas kernels for 11%

profile of v7, /device:TPU:1, one launch (start us, length us, event | category | flops | bytes accessed | tf_op | source)
XLA Modules:
  0.0 123.6 jit_solution(11641771993123767120)
XLA Ops:
  0.6 0.0 copy-start
  0.6 0.0 copy-start.1
  0.7 1.1 copy-done.1
  1.7 0.0 copy-start.9
  1.7 0.0 copy-start.8
  1.7 0.0 copy-start.2
  1.7 0.0 copy-start.3
  1.7 0.0 copy-start.4
  1.8 0.0 copy-start.5
  1.8 0.8 shard_map.119
  2.6 11.6 %all-to-all-start = ((bf16[64,4,1024]{2,1,0:T(4,128)(2,1)}), bf16[64,4,1024]{2,1,0:T(4,128)(2,1)S(1)}, u32[]{:S(2)}, u32[]{:S(2)}) async-start(bf16[64,4,1024]{2,1,0:T(4,128)(2,1)} %shard_map.119), calls=%async_computation | async-start | bytes 1048576 | tf_op jit(solution)/shard_map/all_to_all | solution.py:490
  14.2 0.0 copy-done.9
  14.2 0.1 reshape.42.query_ref
  14.3 0.0 copy-done.8
  14.3 0.1 copy.14.refs_0_.refs_1_
  14.4 0.0 copy-done
  14.4 0.0 copy-done.2
  14.4 0.0 copy-done.3
  14.5 0.0 copy-done.4
  14.5 0.0 copy-done.5
  14.5 7.5 %shard_map.120 = (bf16[128,128]{1,0:T(8,128)(2,1)S(1)}, bf16[8,128,1024]{2,1,0:T(8,128)(2,1)S(1)}, f32[128,128]{1,0:T(8,128)S(1)}, s16[8,208,128]{2,1,0:T(8,128)(2,1)}, f32[8,128]{1,0:T(8,128)S(1)}) custom-call(s32[4,2048]{1,0:T(4,128)S(1)} %bitcast.26, f32[4,2048]{1,0:T(4,128)S(1)} %bitcast.28, bf16[8,4096]{1,0:T(8,128)(2,1)S(1)} %copy-done.5, ...), custom_call_target="tpu_custom_call" | custom-call | tf_op jit(solution)/shard_map/pallas_call | solution.py:503
  22.0 9.9 %all-to-all-done.refs_2_ = bf16[64,4,1024]{2,1,0:T(4,128)(2,1)S(1)} async-done(((bf16[64,4,1024]{2,1,0:T(4,128)(2,1)}), bf16[64,4,1024]{2,1,0:T(4,128)(2,1)S(1)}, u32[]{:S(2)}, u32[]{:S(2)}) %all-to-all-start) | async-done | bytes 524320 | tf_op jit(solution)/shard_map/all_to_all | solution.py:490
  31.9 3.0 %shard_map.121 = (bf16[128,1024]{1,0:T(8,128)(2,1)S(1)}, f32[2,128,128]{2,1,0:T(8,128)S(1)}, bf16[128,128]{1,0:T(8,128)(2,1)S(1)}, s16[8,208,128]{2,1,0:T(8,128)(2,1)}) custom-call(s32[128,1]{1,0:T(8,128)S(1)} %copy.14.refs_0_.refs_1_, s32[1,128]{1,0:T(1,128)S(1)} %bitcast.30, ...), custom_call_target="tpu_custom_call", output_to_operand_aliasing={{3}: (7, {})} | custom-call | tf_op jit(solution)/shard_map/pallas_call | solution.py:518
  34.9 0.0 copy-start.6
  34.9 0.6 copy-done.6
  35.5 10.0 %all-to-all-start.1 = ((s16[8,208,128]{2,1,0:T(8,128)(2,1)}), s16[8,208,128]{2,1,0:T(8,128)(2,1)S(1)}, u32[]{:S(2)}, u32[]{:S(2)}) async-start(s16[8,208,128]{2,1,0:T(8,128)(2,1)} %get-tuple-element.34), calls=%async_computation.1 | async-start | bytes 851968 | tf_op jit(solution)/shard_map/all_to_all | solution.py:532
  45.5 15.8 %all-to-all-done.1.exch_ref.refs_3_ = s16[8,208,128]{2,1,0:T(8,128)(2,1)S(1)} async-done(((s16[8,208,128]{2,1,0:T(8,128)(2,1)}), s16[8,208,128]{2,1,0:T(8,128)(2,1)S(1)}, u32[]{:S(2)}, u32[]{:S(2)}) %all-to-all-start.1) | async-done | bytes 426016 | tf_op jit(solution)/shard_map/all_to_all | solution.py:532
  61.4 0.0 copy-start.7
  61.4 0.8 copy-done.7
  62.1 5.9 %shard_map.122 = (f32[32,24,128]{2,1,0:T(8,128)S(1)}, f32[32,24,128]{2,1,0:T(8,128)S(1)}, bf16[128,128]{1,0:T(8,128)(2,1)S(1)}) custom-call(s32[1]{0:T(128)} %bitcast.core_ref, s16[8,208,128]{2,1,0:T(8,128)(2,1)S(1)} %all-to-all-done.1.exch_ref.refs_3_, f32[2,128,128]{2,1,0:T(8,128)S(1)} %get-tuple-element.35.both_ref, ...), custom_call_target="tpu_custom_call" | custom-call | tf_op jit(solution)/shard_map/pallas_call | solution.py:541
  68.0 2.4 %collective-permute-start = (f32[32,24,128]{2,1,0:T(8,128)S(1)}, f32[32,24,128]{2,1,0:T(8,128)S(1)}, u32[]{:S(2)}, u32[]{:S(2)}) collective-permute-start(f32[32,24,128]{2,1,0:T(8,128)S(1)} %get-tuple-element.39), channel_id=1, source_target_pairs={{0,8},{8,0},{1,9},{9,1},{2,10},{10,2},{3,11},{11,3},{4,12},{12,4},... | collective-permute-start | bytes 1179656 | tf_op jit(solution)/shard_map/ppermute | solution.py:552
  70.4 1.1 shard_map.123.tokens_ref
  71.6 0.2 collective-permute-done.crossed_ref
  71.8 1.1 shard_map.124
  72.8 4.5 %all-to-all-start.2 = ((s16[32,32,128]{2,1,0:T(8,128)(2,1)}), s16[32,32,128]{2,1,0:T(8,128)(2,1)S(1)}, u32[]{:S(2)}, u32[]{:S(2)}) async-start(s16[32,32,128]{2,1,0:T(8,128)(2,1)} %get-tuple-element.42), calls=%async_computation.2 | async-start | bytes 524288 | tf_op jit(solution)/shard_map/all_to_all | solution.py:571
  77.3 4.5 %shard_map.126 = f32[8,4096]{1,0:T(8,128)} custom-call(s32[4,2048]{1,0:T(4,128)S(1)} %bitcast.27, f32[4,2048]{1,0:T(4,128)S(1)} %bitcast.29, bf16[128,128]{1,0:T(8,128)(2,1)S(1)} %get-tuple-element.46.gx_ref), custom_call_target="tpu_custom_call" | custom-call | tf_op jit(solution)/shard_map/pallas_call | solution.py:567
  81.8 11.5 %psum.7.query_ref = f32[4,128]{1,0:T(4,128)S(1)} all-reduce(f32[4,128]{1,0:T(4,128)S(1)} %get-tuple-element.43), channel_id=1, replica_groups=mesh['r'=32,'c'=2,'z'=8] {'z'}, use_global_device_ids=true, to_apply=%region_0.0 | all-reduce | flops 512 | bytes 4096 | tf_op jit(solution)/shard_map/psum | solution.py:572
  93.4 0.0 all-to-all-done.2.coming_ref
  93.4 0.9 shard_map.125
  94.3 8.6 %all-to-all-start.3 = ((s16[32,32,128]{2,1,0:T(8,128)(2,1)}), s16[32,32,128]{2,1,0:T(8,128)(2,1)S(1)}, u32[]{:S(2)}, u32[]{:S(2)}) async-start(s16[32,32,128]{2,1,0:T(8,128)(2,1)} %get-tuple-element.44), calls=%async_computation.3 | async-start | bytes 524288 | tf_op jit(solution)/shard_map/all_to_all | solution.py:581
  103.0 6.9 %collective-permute-start.1 = (bf16[32,4,128]{2,1,0:T(4,128)(2,1)S(1)}, bf16[32,4,128]{2,1,0:T(4,128)(2,1)S(1)}, u32[]{:S(2)}, u32[]{:S(2)}) collective-permute-start(bf16[32,4,128]{2,1,0:T(4,128)(2,1)S(1)} %fusion), channel_id=1, source_target_pairs={{0,8},{8,0},{1,9},{9,1},{2,10},{10,2},{3,11},{11,3},{4,12},{12,4},... | collective-permute-start | bytes 98312 | tf_op jit(solution)/shard_map/ppermute | solution.py:584
  109.9 0.8 collective-permute-done.1
  110.7 0.1 maximum_select_fusion
  110.7 0.7 copy.20
  111.4 2.0 %all-to-all-done.3.half_ref = s16[32,32,128]{2,1,0:T(8,128)(2,1)S(1)} async-done(((s16[32,32,128]{2,1,0:T(8,128)(2,1)}), s16[32,32,128]{2,1,0:T(8,128)(2,1)S(1)}, u32[]{:S(2)}, u32[]{:S(2)}) %all-to-all-start.3) | async-done | bytes 262176 | tf_op jit(solution)/shard_map/all_to_all | solution.py:581
  113.4 8.0 %collective-permute-start.2 = (s16[32,32,128]{2,1,0:T(8,128)(2,1)S(1)}, s16[32,32,128]{2,1,0:T(8,128)(2,1)S(1)}, u32[]{:S(2)}, u32[]{:S(2)}) collective-permute-start(s16[32,32,128]{2,1,0:T(8,128)(2,1)S(1)} %all-to-all-done.3.half_ref), channel_id=1, source_target_pairs={{0,8},{8,0},{1,9},{9,1},{2,10},{10,2},{3,11},{11,3},{4,12},{12,4},... | collective-permute-start | bytes 786440 | tf_op jit(solution)/shard_map/ppermute | solution.py:591
  121.4 1.1 collective-permute-done.2.other_ref
  122.5 1.1 shard_map.127
  (2 shorter events, 0.0 us)
Async XLA Ops:
  0.6 13.8 %copy-start = (bf16[8,16,1024]{2,1,0:T(8,128)(2,1)S(1)}, bf16[8,16,1024]{2,1,0:T(8,128)(2,1)}, u32[]{:S(2)}) copy-start(bf16[8,16,1024]{2,1,0:T(8,128)(2,1)} %param.12) | copy-start | bytes 786436
  0.6 1.1 copy-start.1
  1.7 12.5 %copy-start.9 = (f32[16,64]{1,0:T(8,128)S(1)}, f32[16,64]{1,0:T(8,128)}, u32[]{:S(2)}) copy-start(f32[16,64]{1,0:T(8,128)} %param.14) | copy-start | bytes 12292
  1.7 12.6 %copy-start.8 = (s32[128,1]{0,1:T(1,128)S(1)}, s32[128,1]{0,1:T(1,128)}, u32[]{:S(2)}) copy-start(s32[128,1]{0,1:T(1,128)} %param.11) | copy-start | bytes 1540
  1.7 12.7 %copy-start.2 = (s32[2048,4]{0,1:T(4,128)S(1)}, s32[2048,4]{0,1:T(4,128)}, u32[]{:S(2)}) copy-start(s32[2048,4]{0,1:T(4,128)} %param.9) | copy-start | bytes 98308
  1.7 12.7 %copy-start.3 = (f32[2048,4]{0,1:T(4,128)S(1)}, f32[2048,4]{0,1:T(4,128)}, u32[]{:S(2)}) copy-start(f32[2048,4]{0,1:T(4,128)} %param.10) | copy-start | bytes 98308
  1.7 12.7 %copy-start.4 = (bf16[8,1024]{1,0:T(8,128)(2,1)S(1)}, bf16[8,1024]{1,0:T(8,128)(2,1)}, u32[]{:S(2)}) copy-start(bf16[8,1024]{1,0:T(8,128)(2,1)} %bias_ref.3) | copy-start | bytes 49156
  1.8 12.7 %copy-start.5 = (bf16[8,4096]{1,0:T(8,128)(2,1)S(1)}, bf16[8,4096]{1,0:T(8,128)(2,1)}, u32[]{:S(2)}) copy-start(bf16[8,4096]{1,0:T(8,128)(2,1)} %fields_ref.1) | copy-start | bytes 196612
  2.6 29.3 %all-to-all-start = ((bf16[64,4,1024]{2,1,0:T(4,128)(2,1)}), bf16[64,4,1024]{2,1,0:T(4,128)(2,1)S(1)}, u32[]{:S(2)}, u32[]{:S(2)}) async-start(bf16[64,4,1024]{2,1,0:T(4,128)(2,1)} %shard_map.119), calls=%async_computation | async-start | bytes 1048576 | tf_op jit(solution)/shard_map/all_to_all | solution.py:490
  34.9 0.6 copy-start.6
  35.5 25.9 %all-to-all-start.1 = ((s16[8,208,128]{2,1,0:T(8,128)(2,1)}), s16[8,208,128]{2,1,0:T(8,128)(2,1)S(1)}, u32[]{:S(2)}, u32[]{:S(2)}) async-start(s16[8,208,128]{2,1,0:T(8,128)(2,1)} %get-tuple-element.34), calls=%async_computation.1 | async-start | bytes 851968 | tf_op jit(solution)/shard_map/all_to_all | solution.py:532
  61.4 0.8 copy-start.7
  68.0 3.7 %collective-permute-start = (f32[32,24,128]{2,1,0:T(8,128)S(1)}, f32[32,24,128]{2,1,0:T(8,128)S(1)}, u32[]{:S(2)}, u32[]{:S(2)}) collective-permute-start(f32[32,24,128]{2,1,0:T(8,128)S(1)} %get-tuple-element.39), channel_id=1, source_target_pairs={{0,8},{8,0},{1,9},{9,1},{2,10},{10,2},{3,11},{11,3},{4,12},{12,4},... | collective-permute-start | bytes 1179656 | tf_op jit(solution)/shard_map/ppermute | solution.py:552
  72.8 20.5 %all-to-all-start.2 = ((s16[32,32,128]{2,1,0:T(8,128)(2,1)}), s16[32,32,128]{2,1,0:T(8,128)(2,1)S(1)}, u32[]{:S(2)}, u32[]{:S(2)}) async-start(s16[32,32,128]{2,1,0:T(8,128)(2,1)} %get-tuple-element.42), calls=%async_computation.2 | async-start | bytes 524288 | tf_op jit(solution)/shard_map/all_to_all | solution.py:571
  94.3 19.1 %all-to-all-start.3 = ((s16[32,32,128]{2,1,0:T(8,128)(2,1)}), s16[32,32,128]{2,1,0:T(8,128)(2,1)S(1)}, u32[]{:S(2)}, u32[]{:S(2)}) async-start(s16[32,32,128]{2,1,0:T(8,128)(2,1)} %get-tuple-element.44), calls=%async_computation.3 | async-start | bytes 524288 | tf_op jit(solution)/shard_map/all_to_all | solution.py:581
  103.0 7.7 %collective-permute-start.1 = (bf16[32,4,128]{2,1,0:T(4,128)(2,1)S(1)}, bf16[32,4,128]{2,1,0:T(4,128)(2,1)S(1)}, u32[]{:S(2)}, u32[]{:S(2)}) collective-permute-start(bf16[32,4,128]{2,1,0:T(4,128)(2,1)S(1)} %fusion), channel_id=1, source_target_pairs={{0,8},{8,0},{1,9},{9,1},{2,10},{10,2},{3,11},{11,3},{4,12},{12,4},... | collective-permute-start | bytes 98312 | tf_op jit(solution)/shard_map/ppermute | solution.py:584
  113.4 9.1 %collective-permute-start.2 = (s16[32,32,128]{2,1,0:T(8,128)(2,1)S(1)}, s16[32,32,128]{2,1,0:T(8,128)(2,1)S(1)}, u32[]{:S(2)}, u32[]{:S(2)}) collective-permute-start(s16[32,32,128]{2,1,0:T(8,128)(2,1)S(1)} %all-to-all-done.3.half_ref), channel_id=1, source_target_pairs={{0,8},{8,0},{1,9},{9,1},{2,10},{10,2},{3,11},{11,3},{4,12},{12,4},... | collective-permute-start | bytes 786440 | tf_op jit(solution)/shard_map/ppermute | solution.py:591

commit v8 on v7

--- a/solution.py
+++ b/solution.py
@@ -144,7 +144,7 @@
 
 
 def forward_kernel(
-    index_ref, weight_ref, fields_ref, embed_ref, bias_ref, query_ref, x_ref, e_ref, s_ref, exch_ref, code_ref, sum_ref
+    index_ref, weight_ref, fields_ref, embed_ref, bias_ref, query_ref, e_ref, s_ref, exch_ref, code_ref, sum_ref, x_ref
 ):
     var_local = fields_ref.shape[0]
     blocks = fields_ref.shape[1] // PTS_BLK
@@ -173,7 +173,8 @@
         three = dot_t(embedded, query_rows)
         scores.append(three[:, :H] + three[:, H : 2 * H] + three[:, 2 * H :])
     scores = jnp.concatenate(scores, axis=1) * (1.0 / math.sqrt(DH))
-    s_ref[...] = scores
+    s_ref[0] = scores
+    s_ref[1] = x_all.astype(f32)
     weights = jnp.exp(scores - over_vars(scores, jnp.maximum))
     weights = split(weights / over_vars(weights, jnp.add), 2)
     expand = head_expand(2)
@@ -223,12 +224,10 @@
     inbox_ref,
     e_ref,
     s_ref,
-    x_ref,
     code_ref,
     old_ref,
     up_ref,
     both_ref,
-    xt_ref,
     exch_ref,
     stats_ref,
     sems,
@@ -238,7 +237,8 @@
     target = target_of(column_ref, row_ref, depth, False)
     pick = jnp.where(iota((patches, slots), 1) == target, 1.0, 0.0).astype(bf16)
     upstream = dot(pick, inbox_ref[...].reshape(slots, D))
-    up_ref[...] = upstream.astype(bf16)
+    up_ref[:, :D] = upstream.astype(bf16)
+    up_ref[:, D:] = s_ref[1].astype(bf16)
     reduce_heads = spread(D, H, lambda r, c: r // DH == c)
     var_local = e_ref.shape[0]
     grad_attn = []
@@ -246,10 +246,9 @@
         high, low = split(upstream * e_ref[v].astype(f32), 2)
         grad_attn.append(dot(high, reduce_heads) + dot(low, reduce_heads))
     grad_attn = jnp.concatenate(grad_attn, axis=1)
-    scores = s_ref[...]
+    scores = s_ref[0]
     both_ref[0] = scores
     both_ref[1] = grad_attn
-    xt_ref[...] = x_ref[...].astype(f32).T.astype(bf16)
     peak = over_vars(scores, jnp.maximum)
     weights = jnp.exp(scores - peak)
     total = over_vars(weights, jnp.add)
@@ -399,9 +398,9 @@
 
 
 def backward_kernel(
-    core_ref, exch_ref, both_ref, up_ref, xt_ref, embed_ref, bias_ref, query_ref, kept_ref, send_ref, gx_ref, wide_ref
+    core_ref, exch_ref, both_ref, up_ref, embed_ref, bias_ref, query_ref, kept_ref, send_ref, gx_ref, wide_ref
 ):
-    wide, patches = xt_ref.shape
+    patches, wide = up_ref.shape[0], up_ref.shape[1] - D
     var_local = wide // P_SIZE
     peak, total, inner, _ = combine_stats(exch_ref, patches)
     peak, inner, inverse = (
@@ -419,9 +418,9 @@
     query_rows = jnp.concatenate([jnp.broadcast_to(r.astype(f32), (H, D)) for r in rows], axis=0)
     on_head = iota((6 * H, D), 0) % H == iota((6 * H, D), 1) // DH
     query_rows = jnp.where(on_head, query_rows, 0.0).astype(bf16)
-    upstream = up_ref[...].astype(f32)
-    x_t = xt_ref[...]
-    x_all = x_t.astype(f32).T.astype(bf16)
+    upstream = up_ref[:, :D].astype(f32)
+    x_all = up_ref[:, D:]
+    x_t = x_all.astype(f32).T.astype(bf16)
     embed_t = embed_ref[...].astype(f32).T.astype(bf16)
     lane_var = iota((patches, wide), 1) // P_SIZE
     grad_x = jnp.zeros((patches, wide), f32)
@@ -500,35 +499,33 @@
     embed_flat = embed_weight.reshape(wide, D)
     query = agg_query.reshape(1, D)
     row_map = owner_map.reshape(1, patches)
-    x_all, embedded, scores, sums, codes = kernel_call(
+    embedded, scores, sums, codes = kernel_call(
         forward_kernel,
         (
-            shape((patches, wide), bf16),
             shape((var_local, patches, D), bf16),
-            shape((patches, var_local * H), f32),
+            shape((2, patches, wide), f32),
             shape((groups, patches + STATS, width), i16),
             shape((groups, LANES), f32),
         ),
         mib=20,
-        scratch=[pltpu.VMEM((patches, D), f32)],
+        scratch=[pltpu.VMEM((patches, D), f32), pltpu.VMEM((patches, wide), bf16)],
     )(index_t, weight_t, fields, embed_flat, embed_bias, query)
 
     vmem = pl.BlockSpec(memory_space=pltpu.VMEM)
     anywhere = pl.BlockSpec(memory_space=pl.ANY)
-    upstream, both, x_turned, exchange = kernel_call(
+    upstream, both, exchange = kernel_call(
         lambda *refs: stats_kernel(depth, *refs),
         (
-            shape((patches, D), bf16),
+            shape((patches, D + wide), bf16),
             shape((2, patches, var_local * H), f32),
-            shape((wide, patches), bf16),
             shape(sums.shape, i16),
         ),
         mib=12,
         scratch=[pltpu.VMEM((groups, STATS, LANES), i16), pltpu.SemaphoreType.DMA((groups,))],
-        in_specs=[vmem] * 7 + [anywhere],
-        out_specs=(vmem, vmem, vmem, anywhere),
-        aliases={7: 3},
-    )(owner_map, row_map, inbox, embedded, scores, x_all, codes, sums)
+        in_specs=[vmem] * 6 + [anywhere],
+        out_specs=(vmem, vmem, anywhere),
+        aliases={6: 2},
+    )(owner_map, row_map, inbox, embedded, scores, codes, sums)
     exchange = lax.all_to_all(exchange, "z", 0, 0, tiled=True)
 
     core = lax.axis_index("c").astype(jnp.int32)
@@ -547,8 +544,8 @@
         ),
         mib=16,
         scratch=[pltpu.VMEM((chunks, CHUNK, LANES), f32)],
-        in_specs=[smem] + [vmem] * 7,
-    )(core.reshape(1), exchange, both, upstream, x_turned, embed_flat, embed_bias, query)
+        in_specs=[smem] + [vmem] * 6,
+    )(core.reshape(1), exchange, both, upstream, embed_flat, embed_bias, query)
     crossed = lax.ppermute(sent, "c", swap)
     outbox = kernel_call(
         lambda *refs: tokens_kernel(depth, capacity, *refs),
@@ -564,10 +561,6 @@
         scratch=[pltpu.VMEM((chunks // 2, CHUNK, LANES), f32)],
     )(kept, crossed, outbox)
 
-    field_grad = kernel_call(field_kernel, shape((var_local, fields.shape[1]), f32), mib=16)(
-        index_t, weight_t, grad_x
-    )
-
     coming = lax.all_to_all(going, "r", 0, 0, tiled=True)
     query_half = lax.psum(query_half, "z")
     own, arrived = kernel_call(
@@ -579,6 +572,11 @@
         mib=8,
     )(coming, query_half)
     half = lax.all_to_all(own, "r", 0, 0, tiled=True)
+
+    arrived, grad_x = lax.optimization_barrier((arrived, grad_x))
+    field_grad = kernel_call(field_kernel, shape((var_local, fields.shape[1]), f32), mib=16)(
+        index_t, weight_t, grad_x
+    )
 
     arrived = arrived.reshape(ring, 2, depth, width)
     crossed = lax.ppermute(jnp.where(core == 0, arrived[:, 1], arrived[:, 0]), "c", swap)

time: 124 us -> 119 us (0.960)
  waiting for transfers between devices: 29.9 us -> 26.4 us
  starting transfers between devices: 52 us -> 49.5 us
    all_to_all x1, waiting for transfers between devices: 1.99 us -> 0.01 us  [local(): half = lax.all_to_all(own, 'r', 0, 0, tiled=True)]
    ppermute x1, starting transfers between devices: 7.97 us -> 6.08 us  [local(): other = lax.ppermute(half, 'c', swap)]
  transfers between devices with their start and end apart: 7 -> 7, of which waited for: 6 -> 4; matrix products, arithmetic and copies ran while one was open for 1% -> 1% of each run, Pallas kernels for 11% -> 11%
where the time goes in v8:
time: 119 us
  starting transfers between devices  49.5 us (42%)
  waiting for transfers between devices  26.4 us (22%)
  Pallas kernels  26 us (22%)
  blocking collectives  12.1 us (10%)
  local copies, waits for them, and re-layouts  3.51 us (3%)
    all_to_all x1, waiting for transfers between devices, local(): exchange = lax.all_to_all(exchange, 'z', 0, 0, tiled=True)  15.8 us
    psum x1, blocking collectives, local(): query_half = lax.psum(query_half, 'z')  12.1 us
    all_to_all x1, starting transfers between devices, local(): lax.all_to_all(kernel_call(outbox_kernel, shape((row_devices, depth, D),...  11.6 us
    all_to_all x1, starting transfers between devices, local(): exchange = lax.all_to_all(exchange, 'z', 0, 0, tiled=True)  10 us
    all_to_all x1, waiting for transfers between devices, local(): lax.all_to_all(kernel_call(outbox_kernel, shape((row_devices, depth, D),...  9.27 us
    all_to_all x1, starting transfers between devices, local(): half = lax.all_to_all(own, 'r', 0, 0, tiled=True)  8.63 us
    pallas_call x1, Pallas kernels, local(): kernel_call(forward_kernel, (shape((var_local, patches, D), bf16), shape(...  7.51 us
    ppermute x1, starting transfers between devices, local(): lax.ppermute(jnp.where(core == 0, arrived[:, 1], arrived[:, 0]), 'c', swap)  6.29 us
  transfers between devices with their start and end apart: 7, of which 4 were waited for; matrix products, arithmetic and copies ran while one was open for 1% of the time, Pallas kernels for 11%

profile of v8, /device:TPU:1, one launch (start us, length us, event | category | flops | bytes accessed | tf_op | source)
XLA Modules:
  0.0 118.6 jit_solution(8829786857897625779)
XLA Ops:
  0.6 0.0 copy-start
  0.6 0.0 copy-start.1
  0.7 1.1 copy-done.1
  1.7 0.0 copy-start.9
  1.7 0.0 copy-start.8
  1.7 0.0 copy-start.2
  1.7 0.0 copy-start.3
  1.7 0.0 copy-start.6
  1.8 0.0 copy-start.7
  1.8 0.8 shard_map.119
  2.6 11.6 %all-to-all-start = ((bf16[64,4,1024]{2,1,0:T(4,128)(2,1)}), bf16[64,4,1024]{2,1,0:T(4,128)(2,1)S(1)}, u32[]{:S(2)}, u32[]{:S(2)}) async-start(bf16[64,4,1024]{2,1,0:T(4,128)(2,1)} %shard_map.119), calls=%async_computation | async-start | bytes 1048576 | tf_op jit(solution)/shard_map/all_to_all | solution.py:489
  14.2 0.0 copy-done.9
  14.2 0.1 reshape.42.query_ref
  14.3 0.0 copy-done.8
  14.3 0.1 copy.14.refs_0_.refs_1_
  14.4 0.0 copy-done
  14.4 0.0 copy-done.2
  14.4 0.0 copy-done.3
  14.5 0.0 copy-done.6
  14.5 0.0 copy-done.7
  14.5 7.5 %shard_map.120 = (bf16[8,128,1024]{2,1,0:T(8,128)(2,1)S(1)}, f32[2,128,128]{2,1,0:T(8,128)S(1)}, s16[8,208,128]{2,1,0:T(8,128)(2,1)}, f32[8,128]{1,0:T(8,128)S(1)}) custom-call(s32[4,2048]{1,0:T(4,128)S(1)} %bitcast.26, f32[4,2048]{1,0:T(4,128)S(1)} %bitcast.28, bf16[8,4096]{1,0:T(8,128)(2,1)S(1)} %copy-done.7, bf16[128,1024]{1,0:T(8,128)(2,1)S(1)} %bitcast.22, ...), custom_call_target="tpu_custom_call" | custom-call | tf_op jit(solution)/shard_map/pallas_call | solution.py:502
  22.0 0.0 copy-start.4
  22.0 0.7 copy-done.4
  22.6 9.3 %all-to-all-done.refs_2_ = bf16[64,4,1024]{2,1,0:T(4,128)(2,1)S(1)} async-done(((bf16[64,4,1024]{2,1,0:T(4,128)(2,1)}), bf16[64,4,1024]{2,1,0:T(4,128)(2,1)S(1)}, u32[]{:S(2)}, u32[]{:S(2)}) %all-to-all-start) | async-done | bytes 524320 | tf_op jit(solution)/shard_map/all_to_all | solution.py:489
  31.9 0.0 copy-start.5
  31.9 0.9 copy-done.5
  32.8 3.0 %shard_map.121 = (bf16[128,1152]{1,0:T(8,128)(2,1)S(1)}, f32[2,128,128]{2,1,0:T(8,128)S(1)}, s16[8,208,128]{2,1,0:T(8,128)(2,1)}) custom-call(s32[128,1]{1,0:T(8,128)S(1)} %copy.14.refs_0_.refs_1_, s32[1,128]{1,0:T(1,128)S(1)} %bitcast.30, bf16[64,4,1024]{2,1,0:T(4,128)(2,1)S(1)} %all-to-all-done.refs_2_, ...), custom_call_target="tpu_custom_call", output_to_operand_aliasing={{2}: (6, {})} | custom-call | tf_op jit(solution)/shard_map/pallas_call | solution.py:516
  35.8 10.0 %all-to-all-start.1 = ((s16[8,208,128]{2,1,0:T(8,128)(2,1)}), s16[8,208,128]{2,1,0:T(8,128)(2,1)S(1)}, u32[]{:S(2)}, u32[]{:S(2)}) async-start(s16[8,208,128]{2,1,0:T(8,128)(2,1)} %get-tuple-element.33), calls=%async_computation.1 | async-start | bytes 851968 | tf_op jit(solution)/shard_map/all_to_all | solution.py:529
  45.9 15.8 %all-to-all-done.1.exch_ref.refs_3_ = s16[8,208,128]{2,1,0:T(8,128)(2,1)S(1)} async-done(((s16[8,208,128]{2,1,0:T(8,128)(2,1)}), s16[8,208,128]{2,1,0:T(8,128)(2,1)S(1)}, u32[]{:S(2)}, u32[]{:S(2)}) %all-to-all-start.1) | async-done | bytes 426016 | tf_op jit(solution)/shard_map/all_to_all | solution.py:529
  61.7 5.9 %shard_map.122 = (f32[32,24,128]{2,1,0:T(8,128)S(1)}, f32[32,24,128]{2,1,0:T(8,128)S(1)}, bf16[128,128]{1,0:T(8,128)(2,1)S(1)}) custom-call(s32[1]{0:T(128)} %bitcast.core_ref, s16[8,208,128]{2,1,0:T(8,128)(2,1)S(1)} %all-to-all-done.1.exch_ref.refs_3_, f32[2,128,128]{2,1,0:T(8,128)S(1)} %get-tuple-element.34.both_ref, ...), custom_call_target="tpu_custom_call" | custom-call | tf_op jit(solution)/shard_map/pallas_call | solution.py:538
  67.6 2.4 %collective-permute-start = (f32[32,24,128]{2,1,0:T(8,128)S(1)}, f32[32,24,128]{2,1,0:T(8,128)S(1)}, u32[]{:S(2)}, u32[]{:S(2)}) collective-permute-start(f32[32,24,128]{2,1,0:T(8,128)S(1)} %get-tuple-element.37), channel_id=1, source_target_pairs={{0,8},{8,0},{1,9},{9,1},{2,10},{10,2},{3,11},{11,3},{4,12},{12,4},... | collective-permute-start | bytes 1179656 | tf_op jit(solution)/shard_map/ppermute | solution.py:549
  70.0 1.1 shard_map.123.tokens_ref
  71.2 0.2 collective-permute-done.crossed_ref
  71.3 1.1 shard_map.124
  72.4 4.5 %all-to-all-start.2 = ((s16[32,32,128]{2,1,0:T(8,128)(2,1)}), s16[32,32,128]{2,1,0:T(8,128)(2,1)S(1)}, u32[]{:S(2)}, u32[]{:S(2)}) async-start(s16[32,32,128]{2,1,0:T(8,128)(2,1)} %get-tuple-element.40), calls=%async_computation.2 | async-start | bytes 524288 | tf_op jit(solution)/shard_map/all_to_all | solution.py:564
  76.9 12.1 %psum.7.query_ref = f32[4,128]{1,0:T(4,128)S(1)} all-reduce(f32[4,128]{1,0:T(4,128)S(1)} %get-tuple-element.41), channel_id=1, replica_groups=mesh['r'=32,'c'=2,'z'=8] {'z'}, use_global_device_ids=true, to_apply=%region_0.0 | all-reduce | flops 512 | bytes 4096 | tf_op jit(solution)/shard_map/psum | solution.py:565
  89.1 0.0 all-to-all-done.2.coming_ref
  89.1 0.9 shard_map.125
  90.0 8.6 %all-to-all-start.3 = ((s16[32,32,128]{2,1,0:T(8,128)(2,1)}), s16[32,32,128]{2,1,0:T(8,128)(2,1)S(1)}, u32[]{:S(2)}, u32[]{:S(2)}) async-start(s16[32,32,128]{2,1,0:T(8,128)(2,1)} %get-tuple-element.42), calls=%async_computation.3 | async-start | bytes 524288 | tf_op jit(solution)/shard_map/all_to_all | solution.py:574
  98.6 6.3 %collective-permute-start.1 = (bf16[32,4,128]{2,1,0:T(4,128)(2,1)S(1)}, bf16[32,4,128]{2,1,0:T(4,128)(2,1)S(1)}, u32[]{:S(2)}, u32[]{:S(2)}) collective-permute-start(bf16[32,4,128]{2,1,0:T(4,128)(2,1)S(1)} %fusion), channel_id=1, source_target_pairs={{0,8},{8,0},{1,9},{9,1},{2,10},{10,2},{3,11},{11,3},{4,12},{12,4},... | collective-permute-start | bytes 98312 | tf_op jit(solution)/shard_map/ppermute | solution.py:582
  105.0 4.5 %shard_map.126 = f32[8,4096]{1,0:T(8,128)} custom-call(s32[4,2048]{1,0:T(4,128)S(1)} %bitcast.27, f32[4,2048]{1,0:T(4,128)S(1)} %bitcast.29, bf16[128,128]{1,0:T(8,128)(2,1)S(1)} %get-tuple-element.46.gx_ref), custom_call_target="tpu_custom_call" | custom-call | tf_op jit(solution)/shard_map/pallas_call | solution.py:577
  109.5 0.0 collective-permute-done.1
  109.5 0.1 maximum_select_fusion
  109.5 0.7 copy.20
  110.2 0.0 all-to-all-done.3.half_ref
  110.2 6.1 %collective-permute-start.2 = (s16[32,32,128]{2,1,0:T(8,128)(2,1)S(1)}, s16[32,32,128]{2,1,0:T(8,128)(2,1)S(1)}, u32[]{:S(2)}, u32[]{:S(2)}) collective-permute-start(s16[32,32,128]{2,1,0:T(8,128)(2,1)S(1)} %all-to-all-done.3.half_ref), channel_id=1, source_target_pairs={{0,8},{8,0},{1,9},{9,1},{2,10},{10,2},{3,11},{11,3},{4,12},{12,4},... | collective-permute-start | bytes 786440 | tf_op jit(solution)/shard_map/ppermute | solution.py:589
  116.3 1.1 collective-permute-done.2.other_ref
  117.4 1.1 shard_map.127
  (2 shorter events, 0.0 us)
Async XLA Ops:
  0.6 13.8 %copy-start = (bf16[8,16,1024]{2,1,0:T(8,128)(2,1)S(1)}, bf16[8,16,1024]{2,1,0:T(8,128)(2,1)}, u32[]{:S(2)}) copy-start(bf16[8,16,1024]{2,1,0:T(8,128)(2,1)} %param.12) | copy-start | bytes 786436
  0.6 1.1 copy-start.1
  1.7 12.5 %copy-start.9 = (f32[16,64]{1,0:T(8,128)S(1)}, f32[16,64]{1,0:T(8,128)}, u32[]{:S(2)}) copy-start(f32[16,64]{1,0:T(8,128)} %param.14) | copy-start | bytes 12292
  1.7 12.6 %copy-start.8 = (s32[128,1]{0,1:T(1,128)S(1)}, s32[128,1]{0,1:T(1,128)}, u32[]{:S(2)}) copy-start(s32[128,1]{0,1:T(1,128)} %param.11) | copy-start | bytes 1540
  1.7 12.7 %copy-start.2 = (s32[2048,4]{0,1:T(4,128)S(1)}, s32[2048,4]{0,1:T(4,128)}, u32[]{:S(2)}) copy-start(s32[2048,4]{0,1:T(4,128)} %param.9) | copy-start | bytes 98308
  1.7 12.7 %copy-start.3 = (f32[2048,4]{0,1:T(4,128)S(1)}, f32[2048,4]{0,1:T(4,128)}, u32[]{:S(2)}) copy-start(f32[2048,4]{0,1:T(4,128)} %param.10) | copy-start | bytes 98308
  1.7 12.7 %copy-start.6 = (bf16[8,1024]{1,0:T(8,128)(2,1)S(1)}, bf16[8,1024]{1,0:T(8,128)(2,1)}, u32[]{:S(2)}) copy-start(bf16[8,1024]{1,0:T(8,128)(2,1)} %bias_ref.3) | copy-start | bytes 49156
  1.8 12.7 %copy-start.7 = (bf16[8,4096]{1,0:T(8,128)(2,1)S(1)}, bf16[8,4096]{1,0:T(8,128)(2,1)}, u32[]{:S(2)}) copy-start(bf16[8,4096]{1,0:T(8,128)(2,1)} %fields_ref.1) | copy-start | bytes 196612
  2.6 29.3 %all-to-all-start = ((bf16[64,4,1024]{2,1,0:T(4,128)(2,1)}), bf16[64,4,1024]{2,1,0:T(4,128)(2,1)S(1)}, u32[]{:S(2)}, u32[]{:S(2)}) async-start(bf16[64,4,1024]{2,1,0:T(4,128)(2,1)} %shard_map.119), calls=%async_computation | async-start | bytes 1048576 | tf_op jit(solution)/shard_map/all_to_all | solution.py:489
  22.0 0.7 copy-start.4
  31.9 0.9 copy-start.5
  35.8 25.9 %all-to-all-start.1 = ((s16[8,208,128]{2,1,0:T(8,128)(2,1)}), s16[8,208,128]{2,1,0:T(8,128)(2,1)S(1)}, u32[]{:S(2)}, u32[]{:S(2)}) async-start(s16[8,208,128]{2,1,0:T(8,128)(2,1)} %get-tuple-element.33), calls=%async_computation.1 | async-start | bytes 851968 | tf_op jit(solution)/shard_map/all_to_all | solution.py:529
  67.6 3.7 %collective-permute-start = (f32[32,24,128]{2,1,0:T(8,128)S(1)}, f32[32,24,128]{2,1,0:T(8,128)S(1)}, u32[]{:S(2)}, u32[]{:S(2)}) collective-permute-start(f32[32,24,128]{2,1,0:T(8,128)S(1)} %get-tuple-element.37), channel_id=1, source_target_pairs={{0,8},{8,0},{1,9},{9,1},{2,10},{10,2},{3,11},{11,3},{4,12},{12,4},... | collective-permute-start | bytes 1179656 | tf_op jit(solution)/shard_map/ppermute | solution.py:549
  72.4 16.7 %all-to-all-start.2 = ((s16[32,32,128]{2,1,0:T(8,128)(2,1)}), s16[32,32,128]{2,1,0:T(8,128)(2,1)S(1)}, u32[]{:S(2)}, u32[]{:S(2)}) async-start(s16[32,32,128]{2,1,0:T(8,128)(2,1)} %get-tuple-element.40), calls=%async_computation.2 | async-start | bytes 524288 | tf_op jit(solution)/shard_map/all_to_all | solution.py:564
  90.0 20.2 %all-to-all-start.3 = ((s16[32,32,128]{2,1,0:T(8,128)(2,1)}), s16[32,32,128]{2,1,0:T(8,128)(2,1)S(1)}, u32[]{:S(2)}, u32[]{:S(2)}) async-start(s16[32,32,128]{2,1,0:T(8,128)(2,1)} %get-tuple-element.42), calls=%async_computation.3 | async-start | bytes 524288 | tf_op jit(solution)/shard_map/all_to_all | solution.py:574
  98.6 10.8 %collective-permute-start.1 = (bf16[32,4,128]{2,1,0:T(4,128)(2,1)S(1)}, bf16[32,4,128]{2,1,0:T(4,128)(2,1)S(1)}, u32[]{:S(2)}, u32[]{:S(2)}) collective-permute-start(bf16[32,4,128]{2,1,0:T(4,128)(2,1)S(1)} %fusion), channel_id=1, source_target_pairs={{0,8},{8,0},{1,9},{9,1},{2,10},{10,2},{3,11},{11,3},{4,12},{12,4},... | collective-permute-start | bytes 98312 | tf_op jit(solution)/shard_map/ppermute | solution.py:582
  110.2 7.2 %collective-permute-start.2 = (s16[32,32,128]{2,1,0:T(8,128)(2,1)S(1)}, s16[32,32,128]{2,1,0:T(8,128)(2,1)S(1)}, u32[]{:S(2)}, u32[]{:S(2)}) collective-permute-start(s16[32,32,128]{2,1,0:T(8,128)(2,1)S(1)} %all-to-all-done.3.half_ref), channel_id=1, source_target_pairs={{0,8},{8,0},{1,9},{9,1},{2,10},{10,2},{3,11},{11,3},{4,12},{12,4},... | collective-permute-start | bytes 786440 | tf_op jit(solution)/shard_map/ppermute | solution.py:589

commit v9 on v8

--- a/solution.py
+++ b/solution.py
@@ -7,6 +7,7 @@
 from jax.experimental.pallas import tpu as pltpu
 from jax.sharding import Mesh
 from jax.sharding import PartitionSpec as P
+
 
 D = 1024
 H = 16
@@ -476,7 +477,8 @@
 ):
     by_rows = ("r", "c")
     ring = lax.axis_size("r")
-    groups = lax.axis_size("z")
+    by_vars = ("z1", "z2")
+    groups = lax.axis_size(by_vars)
     row_devices = ring * 2
     var_local = fields.shape[0]
     patches = owner_map.shape[0]
@@ -526,10 +528,10 @@
         out_specs=(vmem, vmem, anywhere),
         aliases={6: 2},
     )(owner_map, row_map, inbox, embedded, scores, codes, sums)
-    exchange = lax.all_to_all(exchange, "z", 0, 0, tiled=True)
+    exchange = lax.all_to_all(exchange, by_vars, 0, 0, tiled=True)
 
     core = lax.axis_index("c").astype(jnp.int32)
-    place = lax.axis_index("z").astype(jnp.int32)
+    place = lax.axis_index(by_vars).astype(jnp.int32)
     smem = pl.BlockSpec(memory_space=pltpu.SMEM)
     swap = [(0, 1), (1, 0)]
     chunks = var_local * TILES
@@ -561,8 +563,9 @@
         scratch=[pltpu.VMEM((chunks // 2, CHUNK, LANES), f32)],
     )(kept, crossed, outbox)
 
+    query_far = lax.ppermute(query_half, "z1", swap)
     coming = lax.all_to_all(going, "r", 0, 0, tiled=True)
-    query_half = lax.psum(query_half, "z")
+    query_half = lax.psum(query_half + query_far, "z2")
     own, arrived = kernel_call(
         own_kernel,
         (
@@ -599,26 +602,27 @@
 
 def solution(mesh):
     rows, groups = mesh.shape["rows"], mesh.shape["vars"]
-    inner = Mesh(mesh.devices.reshape(rows // 2, 2, groups), ("r", "c", "z"))
+    inner = Mesh(mesh.devices.reshape(rows // 2, 2, 2, groups // 2), ("r", "c", "z1", "z2"))
+    by_vars = ("z1", "z2")
     by_rows = ("r", "c")
     return jax.shard_map(
         local,
         mesh=inner,
         in_specs=(
-            P("z", by_rows),
+            P(by_vars, by_rows),
             P(by_rows, None),
             P(by_rows, None),
             P(by_rows, None),
-            P("z", None, None),
-            P("z", None),
+            P(by_vars, None, None),
+            P(by_vars, None),
             P(),
             P(by_rows, None),
         ),
         out_specs=(
-            P(by_rows, "z"),
-            P("z", by_rows),
-            P("z", None, None),
-            P("z", None),
+            P(by_rows, by_vars),
+            P(by_vars, by_rows),
+            P(by_vars, None, None),
+            P(by_vars, None),
             P(),
         ),
         check_vma=False,

time: 119 us -> 123 us (1.034)
  waiting for transfers between devices: 26.4 us -> 32.7 us
  blocking collectives: 12.1 us -> 6.88 us
  starting transfers between devices: 49.5 us -> 52.2 us
    ppermute x0 -> x1, waiting for transfers between devices: none -> 6.21 us  [local(): query_far = lax.ppermute(query_half, 'z1', swap)]
    psum x1, blocking collectives: 12.1 us -> 6.88 us  [local(): query_half = lax.psum(query_half + query_far, 'z2')]
    ppermute x0 -> x1, starting transfers between devices: none -> 2.19 us  [local(): query_far = lax.ppermute(query_half, 'z1', swap)]
  transfers between devices with their start and end apart: 7 -> 8, of which waited for: 4 -> 5; matrix products, arithmetic and copies ran while one was open for 1% -> 1% of each run, Pallas kernels for 11% -> 11%
where the time goes in v9:
time: 123 us; the launch traced here: 122 us
  starting transfers between devices  52.2 us (42%)
  waiting for transfers between devices  32.7 us (27%)
  Pallas kernels  26 us (21%)
  blocking collectives  6.88 us (6%)
  local copies, waits for them, and re-layouts  3.51 us (3%)
    all_to_all x1, waiting for transfers between devices, local(): exchange = lax.all_to_all(exchange, by_vars, 0, 0, tiled=True)  15.8 us
    all_to_all x1, starting transfers between devices, local(): lax.all_to_all(kernel_call(outbox_kernel, shape((row_devices, depth, D),...  11.6 us
    all_to_all x1, starting transfers between devices, local(): exchange = lax.all_to_all(exchange, by_vars, 0, 0, tiled=True)  10 us
    all_to_all x1, waiting for transfers between devices, local(): lax.all_to_all(kernel_call(outbox_kernel, shape((row_devices, depth, D),...  9.28 us
    all_to_all x1, starting transfers between devices, local(): half = lax.all_to_all(own, 'r', 0, 0, tiled=True)  9.04 us
    pallas_call x1, Pallas kernels, local(): kernel_call(forward_kernel, (shape((var_local, patches, D), bf16), shape(...  7.5 us
    psum x1, blocking collectives, local(): query_half = lax.psum(query_half + query_far, 'z2')  6.88 us
    ppermute x1, starting transfers between devices, local(): lax.ppermute(jnp.where(core == 0, arrived[:, 1], arrived[:, 0]), 'c', swap)  6.29 us
  transfers between devices with their start and end apart: 8, of which 5 were waited for; matrix products, arithmetic and copies ran while one was open for 1% of the time, Pallas kernels for 11%

profile of v9, /device:TPU:1, one launch (start us, length us, event | category | flops | bytes accessed | tf_op | source)
XLA Modules:
  0.0 122.2 jit_solution(2090049052773189094)
XLA Ops:
  0.6 0.0 copy-start
  0.6 0.0 copy-start.1
  0.7 1.1 copy-done.1
  1.7 0.0 copy-start.9
  1.7 0.0 copy-start.8
  1.7 0.0 copy-start.2
  1.7 0.0 copy-start.3
  1.7 0.0 copy-start.6
  1.8 0.0 copy-start.7
  1.8 0.8 shard_map.119
  2.6 11.6 %all-to-all-start = ((bf16[64,4,1024]{2,1,0:T(4,128)(2,1)}), bf16[64,4,1024]{2,1,0:T(4,128)(2,1)S(1)}, u32[]{:S(2)}, u32[]{:S(2)}) async-start(bf16[64,4,1024]{2,1,0:T(4,128)(2,1)} %shard_map.119), calls=%async_computation | async-start | bytes 1048576 | tf_op jit(solution)/shard_map/all_to_all | solution.py:491
  14.2 0.0 copy-done.9
  14.2 0.1 reshape.42.query_ref
  14.3 0.0 copy-done.8
  14.3 0.1 copy.14.refs_0_.refs_1_
  14.4 0.0 copy-done
  14.4 0.0 copy-done.2
  14.4 0.0 copy-done.3
  14.5 0.0 copy-done.6
  14.5 0.0 copy-done.7
  14.5 7.5 %shard_map.120 = (bf16[8,128,1024]{2,1,0:T(8,128)(2,1)S(1)}, f32[2,128,128]{2,1,0:T(8,128)S(1)}, s16[8,208,128]{2,1,0:T(8,128)(2,1)}, f32[8,128]{1,0:T(8,128)S(1)}) custom-call(s32[4,2048]{1,0:T(4,128)S(1)} %bitcast.26, f32[4,2048]{1,0:T(4,128)S(1)} %bitcast.28, bf16[8,4096]{1,0:T(8,128)(2,1)S(1)} %copy-done.7, bf16[128,1024]{1,0:T(8,128)(2,1)S(1)} %bitcast.22, ...), custom_call_target="tpu_custom_call" | custom-call | tf_op jit(solution)/shard_map/pallas_call | solution.py:504
  22.0 0.7 copy-done.4
  22.6 9.3 %all-to-all-done.refs_2_ = bf16[64,4,1024]{2,1,0:T(4,128)(2,1)S(1)} async-done(((bf16[64,4,1024]{2,1,0:T(4,128)(2,1)}), bf16[64,4,1024]{2,1,0:T(4,128)(2,1)S(1)}, u32[]{:S(2)}, u32[]{:S(2)}) %all-to-all-start) | async-done | bytes 524320 | tf_op jit(solution)/shard_map/all_to_all | solution.py:491
  31.9 0.9 copy-done.5
  32.8 3.0 %shard_map.121 = (bf16[128,1152]{1,0:T(8,128)(2,1)S(1)}, f32[2,128,128]{2,1,0:T(8,128)S(1)}, s16[8,208,128]{2,1,0:T(8,128)(2,1)}) custom-call(s32[128,1]{1,0:T(8,128)S(1)} %copy.14.refs_0_.refs_1_, s32[1,128]{1,0:T(1,128)S(1)} %bitcast.30, bf16[64,4,1024]{2,1,0:T(4,128)(2,1)S(1)} %all-to-all-done.refs_2_, ...), custom_call_target="tpu_custom_call", output_to_operand_aliasing={{2}: (6, {})} | custom-call | tf_op jit(solution)/shard_map/pallas_call | solution.py:518
  35.9 10.0 %all-to-all-start.1 = ((s16[8,208,128]{2,1,0:T(8,128)(2,1)}), s16[8,208,128]{2,1,0:T(8,128)(2,1)S(1)}, u32[]{:S(2)}, u32[]{:S(2)}) async-start(s16[8,208,128]{2,1,0:T(8,128)(2,1)} %get-tuple-element.33), calls=%async_computation.1 | async-start | bytes 851968 | tf_op jit(solution)/shard_map/all_to_all | solution.py:531
  45.9 15.8 %all-to-all-done.1.exch_ref.refs_3_ = s16[8,208,128]{2,1,0:T(8,128)(2,1)S(1)} async-done(((s16[8,208,128]{2,1,0:T(8,128)(2,1)}), s16[8,208,128]{2,1,0:T(8,128)(2,1)S(1)}, u32[]{:S(2)}, u32[]{:S(2)}) %all-to-all-start.1) | async-done | bytes 426016 | tf_op jit(solution)/shard_map/all_to_all | solution.py:531
  61.8 5.9 %shard_map.122 = (f32[32,24,128]{2,1,0:T(8,128)S(1)}, f32[32,24,128]{2,1,0:T(8,128)S(1)}, bf16[128,128]{1,0:T(8,128)(2,1)S(1)}) custom-call(s32[1]{0:T(128)} %bitcast.core_ref, s16[8,208,128]{2,1,0:T(8,128)(2,1)S(1)} %all-to-all-done.1.exch_ref.refs_3_, f32[2,128,128]{2,1,0:T(8,128)S(1)} %get-tuple-element.34.both_ref, ...), custom_call_target="tpu_custom_call" | custom-call | tf_op jit(solution)/shard_map/pallas_call | solution.py:540
  67.6 2.4 %collective-permute-start = (f32[32,24,128]{2,1,0:T(8,128)S(1)}, f32[32,24,128]{2,1,0:T(8,128)S(1)}, u32[]{:S(2)}, u32[]{:S(2)}) collective-permute-start(f32[32,24,128]{2,1,0:T(8,128)S(1)} %get-tuple-element.37), channel_id=1, source_target_pairs={{0,8},{8,0},{1,9},{9,1},{2,10},{10,2},{3,11},{11,3},{4,12},{12,4},... | collective-permute-start | bytes 1179656 | tf_op jit(solution)/shard_map/ppermute | solution.py:551
  70.1 1.1 shard_map.123.tokens_ref
  71.2 0.2 collective-permute-done.crossed_ref
  71.4 1.1 shard_map.124
  72.4 4.5 %all-to-all-start.2 = ((s16[32,32,128]{2,1,0:T(8,128)(2,1)}), s16[32,32,128]{2,1,0:T(8,128)(2,1)S(1)}, u32[]{:S(2)}, u32[]{:S(2)}) async-start(s16[32,32,128]{2,1,0:T(8,128)(2,1)} %get-tuple-element.40), calls=%async_computation.2 | async-start | bytes 524288 | tf_op jit(solution)/shard_map/all_to_all | solution.py:567
  76.9 2.2 %collective-permute-start.1 = (f32[4,128]{1,0:T(4,128)S(1)}, f32[4,128]{1,0:T(4,128)S(1)}, u32[]{:S(2)}, u32[]{:S(2)}) collective-permute-start(f32[4,128]{1,0:T(4,128)S(1)} %get-tuple-element.41), channel_id=1, source_target_pairs={{0,4},{4,0},{1,5},{5,1},{2,6},{6,2},{3,7},{7,3},{8,12},{12,8},{9,1... | collective-permute-start | bytes 6152 | tf_op jit(solution)/shard_map/ppermute | solution.py:566
  79.2 6.2 %collective-permute-done.1 = f32[4,128]{1,0:T(4,128)S(1)} collective-permute-done((f32[4,128]{1,0:T(4,128)S(1)}, f32[4,128]{1,0:T(4,128)S(1)}, u32[]{:S(2)}, u32[]{:S(2)}) %collective-permute-start.1) | collective-permute-done | bytes 2080 | tf_op jit(solution)/shard_map/ppermute | solution.py:566
  85.4 6.9 %psum.7.query_ref = f32[4,128]{1,0:T(4,128)S(1)} all-reduce(f32[4,128]{1,0:T(4,128)S(1)} %add.9), channel_id=1, replica_groups=mesh['r'=32,'c'=2,'z1'=2,'z2'=4] {'z2'}, use_global_device_ids=true, to_apply=%region_0.0 | all-reduce | flops 512 | bytes 4096 | tf_op jit(solution)/shard_map/psum | solution.py:568
  92.2 0.0 all-to-all-done.2.coming_ref
  92.3 0.9 shard_map.125
  93.2 9.0 %all-to-all-start.3 = ((s16[32,32,128]{2,1,0:T(8,128)(2,1)}), s16[32,32,128]{2,1,0:T(8,128)(2,1)S(1)}, u32[]{:S(2)}, u32[]{:S(2)}) async-start(s16[32,32,128]{2,1,0:T(8,128)(2,1)} %get-tuple-element.42), calls=%async_computation.3 | async-start | bytes 524288 | tf_op jit(solution)/shard_map/all_to_all | solution.py:577
  102.3 6.3 %collective-permute-start.2 = (bf16[32,4,128]{2,1,0:T(4,128)(2,1)S(1)}, bf16[32,4,128]{2,1,0:T(4,128)(2,1)S(1)}, u32[]{:S(2)}, u32[]{:S(2)}) collective-permute-start(bf16[32,4,128]{2,1,0:T(4,128)(2,1)S(1)} %fusion), channel_id=1, source_target_pairs={{0,8},{8,0},{1,9},{9,1},{2,10},{10,2},{3,11},{11,3},{4,12},{12,4},... | collective-permute-start | bytes 98312 | tf_op jit(solution)/shard_map/ppermute | solution.py:585
  108.6 4.5 %shard_map.126 = f32[8,4096]{1,0:T(8,128)} custom-call(s32[4,2048]{1,0:T(4,128)S(1)} %bitcast.27, f32[4,2048]{1,0:T(4,128)S(1)} %bitcast.29, bf16[128,128]{1,0:T(8,128)(2,1)S(1)} %get-tuple-element.46.gx_ref), custom_call_target="tpu_custom_call" | custom-call | tf_op jit(solution)/shard_map/pallas_call | solution.py:580
  113.1 0.0 collective-permute-done.2
  113.1 0.1 maximum_select_fusion
  113.1 0.7 copy.20
  113.8 0.0 all-to-all-done.3.half_ref
  113.8 6.1 %collective-permute-start.3 = (s16[32,32,128]{2,1,0:T(8,128)(2,1)S(1)}, s16[32,32,128]{2,1,0:T(8,128)(2,1)S(1)}, u32[]{:S(2)}, u32[]{:S(2)}) collective-permute-start(s16[32,32,128]{2,1,0:T(8,128)(2,1)S(1)} %all-to-all-done.3.half_ref), channel_id=1, source_target_pairs={{0,8},{8,0},{1,9},{9,1},{2,10},{10,2},{3,11},{11,3},{4,12},{12,4},... | collective-permute-start | bytes 786440 | tf_op jit(solution)/shard_map/ppermute | solution.py:592
  119.9 1.1 collective-permute-done.3.other_ref
  121.0 1.1 shard_map.127
  (5 shorter events, 0.0 us)
Async XLA Ops:
  0.6 13.8 %copy-start = (bf16[8,16,1024]{2,1,0:T(8,128)(2,1)S(1)}, bf16[8,16,1024]{2,1,0:T(8,128)(2,1)}, u32[]{:S(2)}) copy-start(bf16[8,16,1024]{2,1,0:T(8,128)(2,1)} %param.12) | copy-start | bytes 786436
  0.6 1.1 copy-start.1
  1.7 12.5 %copy-start.9 = (f32[16,64]{1,0:T(8,128)S(1)}, f32[16,64]{1,0:T(8,128)}, u32[]{:S(2)}) copy-start(f32[16,64]{1,0:T(8,128)} %param.14) | copy-start | bytes 12292
  1.7 12.6 %copy-start.8 = (s32[128,1]{0,1:T(1,128)S(1)}, s32[128,1]{0,1:T(1,128)}, u32[]{:S(2)}) copy-start(s32[128,1]{0,1:T(1,128)} %param.11) | copy-start | bytes 1540
  1.7 12.7 %copy-start.2 = (s32[2048,4]{0,1:T(4,128)S(1)}, s32[2048,4]{0,1:T(4,128)}, u32[]{:S(2)}) copy-start(s32[2048,4]{0,1:T(4,128)} %param.9) | copy-start | bytes 98308
  1.7 12.7 %copy-start.3 = (f32[2048,4]{0,1:T(4,128)S(1)}, f32[2048,4]{0,1:T(4,128)}, u32[]{:S(2)}) copy-start(f32[2048,4]{0,1:T(4,128)} %param.10) | copy-start | bytes 98308
  1.7 12.7 %copy-start.6 = (bf16[8,1024]{1,0:T(8,128)(2,1)S(1)}, bf16[8,1024]{1,0:T(8,128)(2,1)}, u32[]{:S(2)}) copy-start(bf16[8,1024]{1,0:T(8,128)(2,1)} %bias_ref.3) | copy-start | bytes 49156
  1.8 12.7 %copy-start.7 = (bf16[8,4096]{1,0:T(8,128)(2,1)S(1)}, bf16[8,4096]{1,0:T(8,128)(2,1)}, u32[]{:S(2)}) copy-start(bf16[8,4096]{1,0:T(8,128)(2,1)} %fields_ref.1) | copy-start | bytes 196612
  2.6 29.3 %all-to-all-start = ((bf16[64,4,1024]{2,1,0:T(4,128)(2,1)}), bf16[64,4,1024]{2,1,0:T(4,128)(2,1)S(1)}, u32[]{:S(2)}, u32[]{:S(2)}) async-start(bf16[64,4,1024]{2,1,0:T(4,128)(2,1)} %shard_map.119), calls=%async_computation | async-start | bytes 1048576 | tf_op jit(solution)/shard_map/all_to_all | solution.py:491
  22.0 0.7 copy-start.4
  31.9 0.9 copy-start.5
  35.9 25.9 %all-to-all-start.1 = ((s16[8,208,128]{2,1,0:T(8,128)(2,1)}), s16[8,208,128]{2,1,0:T(8,128)(2,1)S(1)}, u32[]{:S(2)}, u32[]{:S(2)}) async-start(s16[8,208,128]{2,1,0:T(8,128)(2,1)} %get-tuple-element.33), calls=%async_computation.1 | async-start | bytes 851968 | tf_op jit(solution)/shard_map/all_to_all | solution.py:531
  67.6 3.7 %collective-permute-start = (f32[32,24,128]{2,1,0:T(8,128)S(1)}, f32[32,24,128]{2,1,0:T(8,128)S(1)}, u32[]{:S(2)}, u32[]{:S(2)}) collective-permute-start(f32[32,24,128]{2,1,0:T(8,128)S(1)} %get-tuple-element.37), channel_id=1, source_target_pairs={{0,8},{8,0},{1,9},{9,1},{2,10},{10,2},{3,11},{11,3},{4,12},{12,4},... | collective-permute-start | bytes 1179656 | tf_op jit(solution)/shard_map/ppermute | solution.py:551
  72.4 19.8 %all-to-all-start.2 = ((s16[32,32,128]{2,1,0:T(8,128)(2,1)}), s16[32,32,128]{2,1,0:T(8,128)(2,1)S(1)}, u32[]{:S(2)}, u32[]{:S(2)}) async-start(s16[32,32,128]{2,1,0:T(8,128)(2,1)} %get-tuple-element.40), calls=%async_computation.2 | async-start | bytes 524288 | tf_op jit(solution)/shard_map/all_to_all | solution.py:567
  76.9 8.4 %collective-permute-start.1 = (f32[4,128]{1,0:T(4,128)S(1)}, f32[4,128]{1,0:T(4,128)S(1)}, u32[]{:S(2)}, u32[]{:S(2)}) collective-permute-start(f32[4,128]{1,0:T(4,128)S(1)} %get-tuple-element.41), channel_id=1, source_target_pairs={{0,4},{4,0},{1,5},{5,1},{2,6},{6,2},{3,7},{7,3},{8,12},{12,8},{9,1... | collective-permute-start | bytes 6152 | tf_op jit(solution)/shard_map/ppermute | solution.py:566
  93.2 20.6 %all-to-all-start.3 = ((s16[32,32,128]{2,1,0:T(8,128)(2,1)}), s16[32,32,128]{2,1,0:T(8,128)(2,1)S(1)}, u32[]{:S(2)}, u32[]{:S(2)}) async-start(s16[32,32,128]{2,1,0:T(8,128)(2,1)} %get-tuple-element.42), calls=%async_computation.3 | async-start | bytes 524288 | tf_op jit(solution)/shard_map/all_to_all | solution.py:577
  102.3 10.8 %collective-permute-start.2 = (bf16[32,4,128]{2,1,0:T(4,128)(2,1)S(1)}, bf16[32,4,128]{2,1,0:T(4,128)(2,1)S(1)}, u32[]{:S(2)}, u32[]{:S(2)}) collective-permute-start(bf16[32,4,128]{2,1,0:T(4,128)(2,1)S(1)} %fusion), channel_id=1, source_target_pairs={{0,8},{8,0},{1,9},{9,1},{2,10},{10,2},{3,11},{11,3},{4,12},{12,4},... | collective-permute-start | bytes 98312 | tf_op jit(solution)/shard_map/ppermute | solution.py:585
  113.8 7.2 %collective-permute-start.3 = (s16[32,32,128]{2,1,0:T(8,128)(2,1)S(1)}, s16[32,32,128]{2,1,0:T(8,128)(2,1)S(1)}, u32[]{:S(2)}, u32[]{:S(2)}) collective-permute-start(s16[32,32,128]{2,1,0:T(8,128)(2,1)S(1)} %all-to-all-done.3.half_ref), channel_id=1, source_target_pairs={{0,8},{8,0},{1,9},{9,1},{2,10},{10,2},{3,11},{11,3},{4,12},{12,4},... | collective-permute-start | bytes 786440 | tf_op jit(solution)/shard_map/ppermute | solution.py:592

commit v10 on v9

--- a/solution.py
+++ b/solution.py
@@ -216,6 +216,20 @@
 
 def outbox_kernel(grad_ref, out_ref):
     out_ref[...] = grad_ref[...].reshape(out_ref.shape)
+
+
+def outbox_call(row_devices, depth):
+    steps = 4
+    places = row_devices // steps
+    return pl.pallas_call(
+        outbox_kernel,
+        out_shape=jax.ShapeDtypeStruct((row_devices, depth, D), bf16),
+        grid=(steps,),
+        in_specs=[pl.BlockSpec((places * depth, D), lambda i: (i, 0))],
+        out_specs=pl.BlockSpec((places, depth, D), lambda i: (i, 0, 0)),
+        interpret=INTERPRET,
+        compiler_params=pltpu.CompilerParams(vmem_limit_bytes=4 << 20),
+    )
 
 
 def stats_kernel(
@@ -489,7 +503,7 @@
     shape = jax.ShapeDtypeStruct
 
     inbox = lax.all_to_all(
-        kernel_call(outbox_kernel, shape((row_devices, depth, D), bf16), mib=8)(out_grad),
+        outbox_call(row_devices, depth)(out_grad),
         by_rows,
         split_axis=0,
         concat_axis=0,

time: 123 us -> 123 us (level)
  no operation moved by 1% of the time
where the time goes in v10:
time: 123 us
  starting transfers between devices  52.1 us (42%)
  waiting for transfers between devices  32.7 us (27%)
  Pallas kernels  26.6 us (22%)
  blocking collectives  6.88 us (6%)
  local copies, waits for them, and re-layouts  3.51 us (3%)
    all_to_all x1, waiting for transfers between devices, local(): exchange = lax.all_to_all(exchange, by_vars, 0, 0, tiled=True)  15.8 us
    all_to_all x1, starting transfers between devices, local(): lax.all_to_all(outbox_call(row_devices, depth)(out_grad), by_rows, split_...  11.6 us
    all_to_all x1, starting transfers between devices, local(): exchange = lax.all_to_all(exchange, by_vars, 0, 0, tiled=True)  10 us
    all_to_all x1, waiting for transfers between devices, local(): lax.all_to_all(outbox_call(row_devices, depth)(out_grad), by_rows, split_...  9.29 us
    all_to_all x1, starting transfers between devices, local(): half = lax.all_to_all(own, 'r', 0, 0, tiled=True)  9.04 us
    pallas_call x1, Pallas kernels, local(): kernel_call(forward_kernel, (shape((var_local, patches, D), bf16), shape(...  7.49 us
    psum x1, blocking collectives, local(): query_half = lax.psum(query_half + query_far, 'z2')  6.88 us
    ppermute x1, starting transfers between devices, local(): lax.ppermute(jnp.where(core == 0, arrived[:, 1], arrived[:, 0]), 'c', swap)  6.29 us
  transfers between devices with their start and end apart: 8, of which 5 were waited for; matrix products, arithmetic and copies ran while one was open for 1% of the time, Pallas kernels for 11%

profile of v10, /device:TPU:1, one launch (start us, length us, event | category | flops | bytes accessed | tf_op | source)
XLA Modules:
  0.0 122.7 jit_solution(234815737043346710)
XLA Ops:
  0.6 0.0 copy-start
  0.6 0.0 copy-start.1
  0.7 1.1 copy-done.1
  1.7 0.0 copy-start.9
  1.7 0.0 copy-start.8
  1.7 0.0 copy-start.2
  1.7 0.0 copy-start.3
  1.7 0.0 copy-start.6
  1.8 0.0 copy-start.7
  1.8 1.4 %shard_map.119 = bf16[64,4,1024]{2,1,0:T(4,128)(2,1)} custom-call(bf16[256,1024]{1,0:T(8,128)(2,1)S(1)} %copy-done.1), custom_call_target="tpu_custom_call" | custom-call | tf_op jit(solution)/shard_map/pallas_call | solution.py:506
  3.2 11.6 %all-to-all-start = ((bf16[64,4,1024]{2,1,0:T(4,128)(2,1)}), bf16[64,4,1024]{2,1,0:T(4,128)(2,1)S(1)}, u32[]{:S(2)}, u32[]{:S(2)}) async-start(bf16[64,4,1024]{2,1,0:T(4,128)(2,1)} %shard_map.119), calls=%async_computation | async-start | bytes 1048576 | tf_op jit(solution)/shard_map/all_to_all | solution.py:505
  14.8 0.0 copy-done.9
  14.8 0.1 reshape.42.query_ref
  14.9 0.0 copy-done.8
  14.9 0.1 copy.14.refs_0_.refs_1_
  15.0 0.0 copy-done
  15.0 0.0 copy-done.2
  15.0 0.0 copy-done.3
  15.0 0.0 copy-done.6
  15.0 0.0 copy-done.7
  15.0 7.5 %shard_map.120 = (bf16[8,128,1024]{2,1,0:T(8,128)(2,1)S(1)}, f32[2,128,128]{2,1,0:T(8,128)S(1)}, s16[8,208,128]{2,1,0:T(8,128)(2,1)}, f32[8,128]{1,0:T(8,128)S(1)}) custom-call(s32[4,2048]{1,0:T(4,128)S(1)} %bitcast.26, f32[4,2048]{1,0:T(4,128)S(1)} %bitcast.28, bf16[8,4096]{1,0:T(8,128)(2,1)S(1)} %copy-done.7, bf16[128,1024]{1,0:T(8,128)(2,1)S(1)} %bitcast.22, ...), custom_call_target="tpu_custom_call" | custom-call | tf_op jit(solution)/shard_map/pallas_call | solution.py:518
  22.5 0.7 copy-done.4
  23.2 9.3 %all-to-all-done.refs_2_ = bf16[64,4,1024]{2,1,0:T(4,128)(2,1)S(1)} async-done(((bf16[64,4,1024]{2,1,0:T(4,128)(2,1)}), bf16[64,4,1024]{2,1,0:T(4,128)(2,1)S(1)}, u32[]{:S(2)}, u32[]{:S(2)}) %all-to-all-start) | async-done | bytes 524320 | tf_op jit(solution)/shard_map/all_to_all | solution.py:505
  32.5 0.9 copy-done.5
  33.4 3.0 %shard_map.121 = (bf16[128,1152]{1,0:T(8,128)(2,1)S(1)}, f32[2,128,128]{2,1,0:T(8,128)S(1)}, s16[8,208,128]{2,1,0:T(8,128)(2,1)}) custom-call(s32[128,1]{1,0:T(8,128)S(1)} %copy.14.refs_0_.refs_1_, s32[1,128]{1,0:T(1,128)S(1)} %bitcast.30, bf16[64,4,1024]{2,1,0:T(4,128)(2,1)S(1)} %all-to-all-done.refs_2_, ...), custom_call_target="tpu_custom_call", output_to_operand_aliasing={{2}: (6, {})} | custom-call | tf_op jit(solution)/shard_map/pallas_call | solution.py:532
  36.4 10.0 %all-to-all-start.1 = ((s16[8,208,128]{2,1,0:T(8,128)(2,1)}), s16[8,208,128]{2,1,0:T(8,128)(2,1)S(1)}, u32[]{:S(2)}, u32[]{:S(2)}) async-start(s16[8,208,128]{2,1,0:T(8,128)(2,1)} %get-tuple-element.33), calls=%async_computation.1 | async-start | bytes 851968 | tf_op jit(solution)/shard_map/all_to_all | solution.py:545
  46.5 15.8 %all-to-all-done.1.exch_ref.refs_3_ = s16[8,208,128]{2,1,0:T(8,128)(2,1)S(1)} async-done(((s16[8,208,128]{2,1,0:T(8,128)(2,1)}), s16[8,208,128]{2,1,0:T(8,128)(2,1)S(1)}, u32[]{:S(2)}, u32[]{:S(2)}) %all-to-all-start.1) | async-done | bytes 426016 | tf_op jit(solution)/shard_map/all_to_all | solution.py:545
  62.3 5.9 %shard_map.122 = (f32[32,24,128]{2,1,0:T(8,128)S(1)}, f32[32,24,128]{2,1,0:T(8,128)S(1)}, bf16[128,128]{1,0:T(8,128)(2,1)S(1)}) custom-call(s32[1]{0:T(128)} %bitcast.core_ref, s16[8,208,128]{2,1,0:T(8,128)(2,1)S(1)} %all-to-all-done.1.exch_ref.refs_3_, f32[2,128,128]{2,1,0:T(8,128)S(1)} %get-tuple-element.34.both_ref, ...), custom_call_target="tpu_custom_call" | custom-call | tf_op jit(solution)/shard_map/pallas_call | solution.py:554
  68.2 2.4 %collective-permute-start = (f32[32,24,128]{2,1,0:T(8,128)S(1)}, f32[32,24,128]{2,1,0:T(8,128)S(1)}, u32[]{:S(2)}, u32[]{:S(2)}) collective-permute-start(f32[32,24,128]{2,1,0:T(8,128)S(1)} %get-tuple-element.37), channel_id=1, source_target_pairs={{0,8},{8,0},{1,9},{9,1},{2,10},{10,2},{3,11},{11,3},{4,12},{12,4},... | collective-permute-start | bytes 1179656 | tf_op jit(solution)/shard_map/ppermute | solution.py:565
  70.6 1.1 shard_map.123.tokens_ref
  71.8 0.2 collective-permute-done.crossed_ref
  71.9 1.1 shard_map.124
  73.0 4.5 %all-to-all-start.2 = ((s16[32,32,128]{2,1,0:T(8,128)(2,1)}), s16[32,32,128]{2,1,0:T(8,128)(2,1)S(1)}, u32[]{:S(2)}, u32[]{:S(2)}) async-start(s16[32,32,128]{2,1,0:T(8,128)(2,1)} %get-tuple-element.40), calls=%async_computation.2 | async-start | bytes 524288 | tf_op jit(solution)/shard_map/all_to_all | solution.py:581
  77.5 2.2 %collective-permute-start.1 = (f32[4,128]{1,0:T(4,128)S(1)}, f32[4,128]{1,0:T(4,128)S(1)}, u32[]{:S(2)}, u32[]{:S(2)}) collective-permute-start(f32[4,128]{1,0:T(4,128)S(1)} %get-tuple-element.41), channel_id=1, source_target_pairs={{0,4},{4,0},{1,5},{5,1},{2,6},{6,2},{3,7},{7,3},{8,12},{12,8},{9,1... | collective-permute-start | bytes 6152 | tf_op jit(solution)/shard_map/ppermute | solution.py:580
  79.7 6.2 %collective-permute-done.1 = f32[4,128]{1,0:T(4,128)S(1)} collective-permute-done((f32[4,128]{1,0:T(4,128)S(1)}, f32[4,128]{1,0:T(4,128)S(1)}, u32[]{:S(2)}, u32[]{:S(2)}) %collective-permute-start.1) | collective-permute-done | bytes 2080 | tf_op jit(solution)/shard_map/ppermute | solution.py:580
  85.9 6.9 %psum.7.query_ref = f32[4,128]{1,0:T(4,128)S(1)} all-reduce(f32[4,128]{1,0:T(4,128)S(1)} %add.9), channel_id=1, replica_groups=mesh['r'=32,'c'=2,'z1'=2,'z2'=4] {'z2'}, use_global_device_ids=true, to_apply=%region_0.0 | all-reduce | flops 512 | bytes 4096 | tf_op jit(solution)/shard_map/psum | solution.py:582
  92.8 0.0 all-to-all-done.2.coming_ref
  92.8 0.9 shard_map.125
  93.7 9.0 %all-to-all-start.3 = ((s16[32,32,128]{2,1,0:T(8,128)(2,1)}), s16[32,32,128]{2,1,0:T(8,128)(2,1)S(1)}, u32[]{:S(2)}, u32[]{:S(2)}) async-start(s16[32,32,128]{2,1,0:T(8,128)(2,1)} %get-tuple-element.42), calls=%async_computation.3 | async-start | bytes 524288 | tf_op jit(solution)/shard_map/all_to_all | solution.py:591
  102.8 6.3 %collective-permute-start.2 = (bf16[32,4,128]{2,1,0:T(4,128)(2,1)S(1)}, bf16[32,4,128]{2,1,0:T(4,128)(2,1)S(1)}, u32[]{:S(2)}, u32[]{:S(2)}) collective-permute-start(bf16[32,4,128]{2,1,0:T(4,128)(2,1)S(1)} %fusion), channel_id=1, source_target_pairs={{0,8},{8,0},{1,9},{9,1},{2,10},{10,2},{3,11},{11,3},{4,12},{12,4},... | collective-permute-start | bytes 98312 | tf_op jit(solution)/shard_map/ppermute | solution.py:599
  109.1 4.5 %shard_map.126 = f32[8,4096]{1,0:T(8,128)} custom-call(s32[4,2048]{1,0:T(4,128)S(1)} %bitcast.27, f32[4,2048]{1,0:T(4,128)S(1)} %bitcast.29, bf16[128,128]{1,0:T(8,128)(2,1)S(1)} %get-tuple-element.46.gx_ref), custom_call_target="tpu_custom_call" | custom-call | tf_op jit(solution)/shard_map/pallas_call | solution.py:594
  113.6 0.0 collective-permute-done.2
  113.6 0.1 maximum_select_fusion
  113.7 0.7 copy.20
  114.4 0.0 all-to-all-done.3.half_ref
  114.4 6.1 %collective-permute-start.3 = (s16[32,32,128]{2,1,0:T(8,128)(2,1)S(1)}, s16[32,32,128]{2,1,0:T(8,128)(2,1)S(1)}, u32[]{:S(2)}, u32[]{:S(2)}) collective-permute-start(s16[32,32,128]{2,1,0:T(8,128)(2,1)S(1)} %all-to-all-done.3.half_ref), channel_id=1, source_target_pairs={{0,8},{8,0},{1,9},{9,1},{2,10},{10,2},{3,11},{11,3},{4,12},{12,4},... | collective-permute-start | bytes 786440 | tf_op jit(solution)/shard_map/ppermute | solution.py:606
  120.4 1.1 collective-permute-done.3.other_ref
  121.6 1.1 shard_map.127
  (5 shorter events, 0.0 us)
Async XLA Ops:
  0.6 14.4 %copy-start = (bf16[8,16,1024]{2,1,0:T(8,128)(2,1)S(1)}, bf16[8,16,1024]{2,1,0:T(8,128)(2,1)}, u32[]{:S(2)}) copy-start(bf16[8,16,1024]{2,1,0:T(8,128)(2,1)} %param.12) | copy-start | bytes 786436
  0.6 1.1 copy-start.1
  1.7 13.1 %copy-start.9 = (f32[16,64]{1,0:T(8,128)S(1)}, f32[16,64]{1,0:T(8,128)}, u32[]{:S(2)}) copy-start(f32[16,64]{1,0:T(8,128)} %param.14) | copy-start | bytes 12292
  1.7 13.1 %copy-start.8 = (s32[128,1]{0,1:T(1,128)S(1)}, s32[128,1]{0,1:T(1,128)}, u32[]{:S(2)}) copy-start(s32[128,1]{0,1:T(1,128)} %param.11) | copy-start | bytes 1540
  1.7 13.3 %copy-start.2 = (s32[2048,4]{0,1:T(4,128)S(1)}, s32[2048,4]{0,1:T(4,128)}, u32[]{:S(2)}) copy-start(s32[2048,4]{0,1:T(4,128)} %param.9) | copy-start | bytes 98308
  1.7 13.3 %copy-start.3 = (f32[2048,4]{0,1:T(4,128)S(1)}, f32[2048,4]{0,1:T(4,128)}, u32[]{:S(2)}) copy-start(f32[2048,4]{0,1:T(4,128)} %param.10) | copy-start | bytes 98308
  1.7 13.3 %copy-start.6 = (bf16[8,1024]{1,0:T(8,128)(2,1)S(1)}, bf16[8,1024]{1,0:T(8,128)(2,1)}, u32[]{:S(2)}) copy-start(bf16[8,1024]{1,0:T(8,128)(2,1)} %bias_ref.3) | copy-start | bytes 49156
  1.8 13.3 %copy-start.7 = (bf16[8,4096]{1,0:T(8,128)(2,1)S(1)}, bf16[8,4096]{1,0:T(8,128)(2,1)}, u32[]{:S(2)}) copy-start(bf16[8,4096]{1,0:T(8,128)(2,1)} %fields_ref.1) | copy-start | bytes 196612
  3.2 29.3 %all-to-all-start = ((bf16[64,4,1024]{2,1,0:T(4,128)(2,1)}), bf16[64,4,1024]{2,1,0:T(4,128)(2,1)S(1)}, u32[]{:S(2)}, u32[]{:S(2)}) async-start(bf16[64,4,1024]{2,1,0:T(4,128)(2,1)} %shard_map.119), calls=%async_computation | async-start | bytes 1048576 | tf_op jit(solution)/shard_map/all_to_all | solution.py:505
  22.5 0.7 copy-start.4
  32.5 0.9 copy-start.5
  36.4 25.9 %all-to-all-start.1 = ((s16[8,208,128]{2,1,0:T(8,128)(2,1)}), s16[8,208,128]{2,1,0:T(8,128)(2,1)S(1)}, u32[]{:S(2)}, u32[]{:S(2)}) async-start(s16[8,208,128]{2,1,0:T(8,128)(2,1)} %get-tuple-element.33), calls=%async_computation.1 | async-start | bytes 851968 | tf_op jit(solution)/shard_map/all_to_all | solution.py:545
  68.2 3.7 %collective-permute-start = (f32[32,24,128]{2,1,0:T(8,128)S(1)}, f32[32,24,128]{2,1,0:T(8,128)S(1)}, u32[]{:S(2)}, u32[]{:S(2)}) collective-permute-start(f32[32,24,128]{2,1,0:T(8,128)S(1)} %get-tuple-element.37), channel_id=1, source_target_pairs={{0,8},{8,0},{1,9},{9,1},{2,10},{10,2},{3,11},{11,3},{4,12},{12,4},... | collective-permute-start | bytes 1179656 | tf_op jit(solution)/shard_map/ppermute | solution.py:565
  73.0 19.8 %all-to-all-start.2 = ((s16[32,32,128]{2,1,0:T(8,128)(2,1)}), s16[32,32,128]{2,1,0:T(8,128)(2,1)S(1)}, u32[]{:S(2)}, u32[]{:S(2)}) async-start(s16[32,32,128]{2,1,0:T(8,128)(2,1)} %get-tuple-element.40), calls=%async_computation.2 | async-start | bytes 524288 | tf_op jit(solution)/shard_map/all_to_all | solution.py:581
  77.5 8.4 %collective-permute-start.1 = (f32[4,128]{1,0:T(4,128)S(1)}, f32[4,128]{1,0:T(4,128)S(1)}, u32[]{:S(2)}, u32[]{:S(2)}) collective-permute-start(f32[4,128]{1,0:T(4,128)S(1)} %get-tuple-element.41), channel_id=1, source_target_pairs={{0,4},{4,0},{1,5},{5,1},{2,6},{6,2},{3,7},{7,3},{8,12},{12,8},{9,1... | collective-permute-start | bytes 6152 | tf_op jit(solution)/shard_map/ppermute | solution.py:580
  93.7 20.6 %all-to-all-start.3 = ((s16[32,32,128]{2,1,0:T(8,128)(2,1)}), s16[32,32,128]{2,1,0:T(8,128)(2,1)S(1)}, u32[]{:S(2)}, u32[]{:S(2)}) async-start(s16[32,32,128]{2,1,0:T(8,128)(2,1)} %get-tuple-element.42), calls=%async_computation.3 | async-start | bytes 524288 | tf_op jit(solution)/shard_map/all_to_all | solution.py:591
  102.8 10.8 %collective-permute-start.2 = (bf16[32,4,128]{2,1,0:T(4,128)(2,1)S(1)}, bf16[32,4,128]{2,1,0:T(4,128)(2,1)S(1)}, u32[]{:S(2)}, u32[]{:S(2)}) collective-permute-start(bf16[32,4,128]{2,1,0:T(4,128)(2,1)S(1)} %fusion), channel_id=1, source_target_pairs={{0,8},{8,0},{1,9},{9,1},{2,10},{10,2},{3,11},{11,3},{4,12},{12,4},... | collective-permute-start | bytes 98312 | tf_op jit(solution)/shard_map/ppermute | solution.py:599
  114.4 7.2 %collective-permute-start.3 = (s16[32,32,128]{2,1,0:T(8,128)(2,1)S(1)}, s16[32,32,128]{2,1,0:T(8,128)(2,1)S(1)}, u32[]{:S(2)}, u32[]{:S(2)}) collective-permute-start(s16[32,32,128]{2,1,0:T(8,128)(2,1)S(1)} %all-to-all-done.3.half_ref), channel_id=1, source_target_pairs={{0,8},{8,0},{1,9},{9,1},{2,10},{10,2},{3,11},{11,3},{4,12},{12,4},... | collective-permute-start | bytes 786440 | tf_op jit(solution)/shard_map/ppermute | solution.py:606
